TPU v7x, 32 devices: a whole 2x2x4 slice. The times are simulated.
32 devices in a mesh: dp: 2 (over core), fsdp: 16 (over z, y, x).
Axes of the slice: x: 2, y: 2, z: 4, core: 2. Of those that a mesh axis runs over, the one named last changes fastest.
Arguments:
- tokens: bfloat16 [32, 128, 768], P(('dp', 'fsdp')), may hold values from -6 to 6
- cotangent: bfloat16 [32, 128, 768], P(('dp', 'fsdp')), may hold values from -6 to 6
- lengths: int32 [32, 2], P(('dp', 'fsdp')), may hold values from 1 to 128, as said below
- joint_weight: bfloat16 [1, 768, 2304], P(None, 'fsdp'), may hold values from -0.21875 to 0.21875
- output_weight: bfloat16 [1, 768, 768], P(None, 'fsdp'), may hold values from -0.875 to 0.875
- expand_weight: bfloat16 [1, 768, 3072], P(None, 'fsdp'), may hold values from -0.21875 to 0.21875
- shrink_weight: bfloat16 [1, 3072, 768], P(None, 'fsdp'), may hold values from -0.109375 to 0.109375
- norm_gains: bfloat16 [1, 2, 768], P(None, None, 'fsdp'), may hold values from 0.5 to 1.5
- bias_rows: bfloat16 [1, 10, 768], P(None, None, 'fsdp'), may hold values from -2 to 2
- master_joint: float32 [1, 768, 2304], P(None, 'fsdp', 'dp'), may hold values from -0.21875 to 0.21875
- master_output: float32 [1, 768, 768], P(None, 'fsdp', 'dp'), may hold values from -0.875 to 0.875
- master_expand: float32 [1, 768, 3072], P(None, 'fsdp', 'dp'), may hold values from -0.21875 to 0.21875
- master_shrink: float32 [1, 3072, 768], P(None, 'fsdp', 'dp'), may hold values from -0.109375 to 0.109375
- master_gains: float32 [1, 2, 768], P(None, None, 'fsdp'), may hold values from 0.5 to 1.5
- master_biases: float32 [1, 10, 768], P(None, None, 'fsdp'), may hold values from -2 to 2
- first_joint: float32 [1, 768, 2304], P(None, 'fsdp', 'dp'), may hold values from -192 to 192
- first_output: float32 [1, 768, 768], P(None, 'fsdp', 'dp'), may hold values from -192 to 192
- first_expand: float32 [1, 768, 3072], P(None, 'fsdp', 'dp'), may hold values from -192 to 192
- first_shrink: float32 [1, 3072, 768], P(None, 'fsdp', 'dp'), may hold values from -192 to 192
- first_gains: float32 [1, 2, 768], P(None, None, 'fsdp'), may hold values from -192 to 192
- first_biases: float32 [1, 10, 768], P(None, None, 'fsdp'), may hold values from -192 to 192
- second_joint: float32 [1, 768, 2304], P(None, 'fsdp', 'dp'), may hold values from 204.8 to 8192
- second_output: float32 [1, 768, 768], P(None, 'fsdp', 'dp'), may hold values from 204.8 to 8192
- second_expand: float32 [1, 768, 3072], P(None, 'fsdp', 'dp'), may hold values from 204.8 to 8192
- second_shrink: float32 [1, 3072, 768], P(None, 'fsdp', 'dp'), may hold values from 204.8 to 8192
- second_gains: float32 [1, 2, 768], P(None, None, 'fsdp'), may hold values from 204.8 to 8192
- second_biases: float32 [1, 10, 768], P(None, None, 'fsdp'), may hold values from 204.8 to 8192
Outputs:
- output_rows: float32 [32, 128, 768], P(('dp', 'fsdp'))
- input_grad: float32 [32, 128, 768], P(('dp', 'fsdp'))
- grad_joint: float32 [1, 768, 2304], P(None, 'fsdp', 'dp')
- new_master_joint: float32 [1, 768, 2304], P(None, 'fsdp', 'dp')
- new_first_joint: float32 [1, 768, 2304], P(None, 'fsdp', 'dp')
- new_second_joint: float32 [1, 768, 2304], P(None, 'fsdp', 'dp')
- new_copy_joint: bfloat16 [1, 768, 2304], P(None, 'fsdp', 'dp')
- grad_output: float32 [1, 768, 768], P(None, 'fsdp', 'dp')
- new_master_output: float32 [1, 768, 768], P(None, 'fsdp', 'dp')
- new_first_output: float32 [1, 768, 768], P(None, 'fsdp', 'dp')
- new_second_output: float32 [1, 768, 768], P(None, 'fsdp', 'dp')
- new_copy_output: bfloat16 [1, 768, 768], P(None, 'fsdp', 'dp')
- grad_expand: float32 [1, 768, 3072], P(None, 'fsdp', 'dp')
- new_master_expand: float32 [1, 768, 3072], P(None, 'fsdp', 'dp')
- new_first_expand: float32 [1, 768, 3072], P(None, 'fsdp', 'dp')
- new_second_expand: float32 [1, 768, 3072], P(None, 'fsdp', 'dp')
- new_copy_expand: bfloat16 [1, 768, 3072], P(None, 'fsdp', 'dp')
- grad_shrink: float32 [1, 3072, 768], P(None, 'fsdp', 'dp')
- new_master_shrink: float32 [1, 3072, 768], P(None, 'fsdp', 'dp')
- new_first_shrink: float32 [1, 3072, 768], P(None, 'fsdp', 'dp')
- new_second_shrink: float32 [1, 3072, 768], P(None, 'fsdp', 'dp')
- new_copy_shrink: bfloat16 [1, 3072, 768], P(None, 'fsdp', 'dp')
- grad_gains: float32 [1, 2, 768], P(None, None, 'fsdp')
- new_master_gains: float32 [1, 2, 768], P(None, None, 'fsdp')
- new_first_gains: float32 [1, 2, 768], P(None, None, 'fsdp')
- new_second_gains: float32 [1, 2, 768], P(None, None, 'fsdp')
- new_copy_gains: bfloat16 [1, 2, 768], P(None, None, 'fsdp')
- grad_biases: float32 [1, 10, 768], P(None, None, 'fsdp')
- new_master_biases: float32 [1, 10, 768], P(None, None, 'fsdp')
- new_first_biases: float32 [1, 10, 768], P(None, None, 'fsdp')
- new_second_biases: float32 [1, 10, 768], P(None, None, 'fsdp')
- new_copy_biases: bfloat16 [1, 10, 768], P(None, None, 'fsdp')
Inputs may be any that keep to these rules, and one draw needn't show every extreme that they name: `lengths`: column 0 of an item's row is its prefix length, 1 to its total; column 1 is its total filled length, 32 to 128; some item fills all 128 slots.
All inputs are finite; a program needn't handle non-finite values.
Results may differ from a plain program's by a relative error of at most 0.012.
Values may be sent and summed in bfloat16 or wider, within the bound.
No kernel may reach another device: no remote copies, remote signals or barrier semaphores. Data moves between devices by JAX's collectives and lax.ppermute only.
A program may use at most 128 MiB of HBM per device.

v0:
```python
import jax
import jax.numpy as jnp
from jax import lax
from jax.sharding import PartitionSpec as P

HEAD_DIM = 64
STEP_COUNT = 3


beta_one = 0.5
beta_two = 0.5
learning_rate = 0.02
small_rate = 0.25
weight_decay = 0.1
epsilon = 1e-08
norm_epsilon = 1e-05


def layer_norm(stream, gain, shift):
    centred = stream - jnp.mean(stream, axis=-1, keepdims=True)
    spread = jnp.mean(centred * centred, axis=-1, keepdims=True)
    return centred * lax.rsqrt(spread + norm_epsilon) * gain + shift


def visible_mask(prefix, total, token_count):
    position = jnp.arange(token_count, dtype=jnp.int32)
    query_pos = position[:, None]
    key_pos = position[None, :]
    return (key_pos < total) & ((key_pos <= query_pos) | (key_pos < prefix))


def softmax_rows(scores, visible):
    return jax.nn.softmax(jnp.where(visible[None], scores, -1e30), axis=-1)


def outer_sum(left, right):
    return lax.dot_general(
        left, right, (((0,), (0,)), ((), ())), preferred_element_type=jnp.float32
    )


def times_back(left, right):
    return lax.dot_general(
        left, right, (((1,), (1,)), ((), ())), preferred_element_type=jnp.float32
    )


def layer_parts(stream, gathered, visible):
    joint_mat, output, expand, shrink, gain_rows, biases = gathered
    token_count, model_width = stream.shape
    head_count = model_width // HEAD_DIM
    gain_full = gain_rows.astype(jnp.float32)
    bias_full = biases.astype(jnp.float32)
    normed = layer_norm(stream, gain_full[0], bias_full[0]).astype(jnp.bfloat16)
    joint_bias = jnp.concatenate([bias_full[2], jnp.zeros_like(bias_full[2]), bias_full[3]])
    projected = (
        jnp.dot(normed, joint_mat, preferred_element_type=jnp.float32) + joint_bias
    ).astype(jnp.bfloat16)
    queries = projected[:, :model_width].reshape(token_count, head_count, HEAD_DIM)
    key_rows = projected[:, model_width : 2 * model_width].reshape(
        token_count, head_count, HEAD_DIM
    )
    values = projected[:, 2 * model_width :].reshape(token_count, head_count, HEAD_DIM)
    dot_scores = jnp.einsum("qhd,khd->hqk", queries, key_rows, preferred_element_type=jnp.float32)
    scaled = dot_scores * HEAD_DIM ** (-0.5)
    attend_low = softmax_rows(scaled, visible).astype(jnp.bfloat16)
    attended = jnp.einsum("hqk,khd->qhd", attend_low, values, preferred_element_type=jnp.float32)
    attended = attended.reshape(token_count, model_width).astype(jnp.bfloat16)
    branch = jnp.dot(attended, output, preferred_element_type=jnp.float32) + bias_full[4]
    middle = stream + branch
    normed_two = layer_norm(middle, gain_full[1], bias_full[1]).astype(jnp.bfloat16)
    hidden = jnp.dot(normed_two, expand, preferred_element_type=jnp.float32) + bias_full[
        6:
    ].reshape(-1)
    active = jax.nn.gelu(hidden, approximate=True).astype(jnp.bfloat16)
    second = jnp.dot(active, shrink, preferred_element_type=jnp.float32) + bias_full[5]
    kept = (normed, projected, scaled, attend_low, attended, middle, normed_two, hidden, active)
    return (middle + second, kept)


def layer_back(stream, gathered, visible, upstream):
    joint_mat, output, expand, shrink, gain_rows, biases = gathered
    token_count, model_width = stream.shape
    head_count = model_width // HEAD_DIM
    score_scale = HEAD_DIM ** (-0.5)
    gain_full = gain_rows.astype(jnp.float32)
    bias_full = biases.astype(jnp.float32)
    unused_out, kept = layer_parts(stream, gathered, visible)
    normed, projected, scaled, attend_low, attended, middle, normed_two, hidden, active = kept
    queries = projected[:, :model_width].reshape(token_count, head_count, HEAD_DIM)
    key_rows = projected[:, model_width : 2 * model_width].reshape(
        token_count, head_count, HEAD_DIM
    )
    values = projected[:, 2 * model_width :].reshape(token_count, head_count, HEAD_DIM)
    back_second = upstream.astype(jnp.bfloat16)
    grad_shrink = outer_sum(active, back_second)
    bias_shrink = jnp.sum(back_second.astype(jnp.float32), axis=0)
    back_active = times_back(back_second, shrink)
    gelu_value, gelu_pull = jax.vjp(lambda inner: jax.nn.gelu(inner, approximate=True), hidden)
    back_hidden = gelu_pull(back_active)[0].astype(jnp.bfloat16)
    grad_expand = outer_sum(normed_two, back_hidden)
    bias_expand = jnp.sum(back_hidden.astype(jnp.float32), axis=0)
    back_normed_two = times_back(back_hidden, expand)
    norm_value, norm_pull = jax.vjp(layer_norm, middle, gain_full[1], bias_full[1])
    back_inner, gain_two, shift_two = norm_pull(back_normed_two)
    back_middle = upstream + back_inner
    back_branch = back_middle.astype(jnp.bfloat16)
    grad_output = outer_sum(attended, back_branch)
    bias_output = jnp.sum(back_branch.astype(jnp.float32), axis=0)
    back_attended = (
        times_back(back_branch, output)
        .astype(jnp.bfloat16)
        .reshape(token_count, head_count, HEAD_DIM)
    )
    grad_values = jnp.einsum(
        "hqk,qhd->khd", attend_low, back_attended, preferred_element_type=jnp.float32
    )
    back_attention = jnp.einsum(
        "qhd,khd->hqk", back_attended, values, preferred_element_type=jnp.float32
    )
    soft_value, soft_pull = jax.vjp(lambda inner: softmax_rows(inner, visible), scaled)
    back_scores = (soft_pull(back_attention)[0] * score_scale).astype(jnp.bfloat16)
    grad_queries = jnp.einsum(
        "hqk,khd->qhd", back_scores, key_rows, preferred_element_type=jnp.float32
    )
    grad_keys = jnp.einsum("hqk,qhd->khd", back_scores, queries, preferred_element_type=jnp.float32)
    back_projected = jnp.concatenate(
        [
            grad_queries.reshape(token_count, model_width),
            grad_keys.reshape(token_count, model_width),
            grad_values.reshape(token_count, model_width),
        ],
        axis=1,
    ).astype(jnp.bfloat16)
    grad_joint = outer_sum(normed, back_projected)
    project_wide = back_projected.astype(jnp.float32)
    bias_query = jnp.sum(project_wide[:, :model_width], axis=0)
    bias_value = jnp.sum(project_wide[:, 2 * model_width :], axis=0)
    back_normed = times_back(back_projected, joint_mat)
    first_value, first_pull = jax.vjp(layer_norm, stream, gain_full[0], bias_full[0])
    back_stream, gain_one, shift_one = first_pull(back_normed)
    gain_grad = jnp.stack([gain_one, gain_two])
    bias_grad = jnp.concatenate(
        [
            jnp.stack([shift_one, shift_two, bias_query, bias_value, bias_output, bias_shrink]),
            bias_expand.reshape(-1, model_width),
        ]
    )
    return (
        back_middle + back_stream,
        (grad_joint, grad_output, grad_expand, grad_shrink, gain_grad, bias_grad),
    )


def adamw(master, first, second, gradient, rate):
    first_new = beta_one * first + (1.0 - beta_one) * gradient
    second_new = beta_two * second + (1.0 - beta_two) * gradient * gradient
    first_hat = first_new / (1.0 - beta_one**STEP_COUNT)
    second_hat = second_new / (1.0 - beta_two**STEP_COUNT)
    master_new = master - rate * (
        first_hat / (jnp.sqrt(second_hat) + epsilon) + weight_decay * master
    )
    return (master_new, first_new, second_new, master_new.astype(jnp.bfloat16))


def local(
    tokens,
    cotangent,
    lengths,
    joint_weight,
    output_weight,
    expand_weight,
    shrink_weight,
    norm_gains,
    bias_rows,
    master_joint,
    master_output,
    master_expand,
    master_shrink,
    master_gains,
    master_biases,
    first_joint,
    first_output,
    first_expand,
    first_shrink,
    first_gains,
    first_biases,
    second_joint,
    second_output,
    second_expand,
    second_shrink,
    second_gains,
    second_biases,
):
    stream = tokens[0].astype(jnp.float32)
    visible = visible_mask(lengths[0, 0], lengths[0, 1], stream.shape[0])
    layers = joint_weight.shape[0]
    gathered_kept = []
    layer_index = 0
    gathered = (
        lax.all_gather(joint_weight[layer_index], "fsdp", axis=0, tiled=True),
        lax.all_gather(output_weight[layer_index], "fsdp", axis=0, tiled=True),
        lax.all_gather(expand_weight[layer_index], "fsdp", axis=0, tiled=True),
        lax.all_gather(shrink_weight[layer_index], "fsdp", axis=0, tiled=True),
        lax.all_gather(norm_gains[layer_index], "fsdp", axis=1, tiled=True),
        lax.all_gather(bias_rows[layer_index], "fsdp", axis=1, tiled=True),
    )
    gathered_kept.append(gathered)
    inputs_kept = [stream]
    stream, unused_kept = layer_parts(stream, gathered, visible)
    upstream = cotangent[0].astype(jnp.float32)
    pieces = [None] * layers
    for layer_index in reversed(range(layers)):
        gathered = (
            lax.all_gather(joint_weight[layer_index], "fsdp", axis=0, tiled=True),
            lax.all_gather(output_weight[layer_index], "fsdp", axis=0, tiled=True),
            lax.all_gather(expand_weight[layer_index], "fsdp", axis=0, tiled=True),
            lax.all_gather(shrink_weight[layer_index], "fsdp", axis=0, tiled=True),
            lax.all_gather(norm_gains[layer_index], "fsdp", axis=1, tiled=True),
            lax.all_gather(bias_rows[layer_index], "fsdp", axis=1, tiled=True),
        )
        upstream, layer_grads = layer_back(inputs_kept[layer_index], gathered, visible, upstream)
        matrices = (layer_grads[0], layer_grads[1], layer_grads[2], layer_grads[3])
        pieces[layer_index] = (
            lax.psum_scatter(matrices[0], "fsdp", scatter_dimension=0, tiled=True),
            lax.psum_scatter(matrices[1], "fsdp", scatter_dimension=0, tiled=True),
            lax.psum_scatter(matrices[2], "fsdp", scatter_dimension=0, tiled=True),
            lax.psum_scatter(matrices[3], "fsdp", scatter_dimension=0, tiled=True),
            lax.psum_scatter(layer_grads[4], "fsdp", scatter_dimension=1, tiled=True),
            lax.psum_scatter(layer_grads[5], "fsdp", scatter_dimension=1, tiled=True),
        )
    stacked = tuple(
        (jnp.stack([piece[group_index] for piece in pieces]) for group_index in range(6))
    )
    masters = (
        master_joint,
        master_output,
        master_expand,
        master_shrink,
        master_gains,
        master_biases,
    )
    firsts = (first_joint, first_output, first_expand, first_shrink, first_gains, first_biases)
    seconds = (
        second_joint,
        second_output,
        second_expand,
        second_shrink,
        second_gains,
        second_biases,
    )
    matrix_sums = (
        lax.psum_scatter(stacked[0], "dp", scatter_dimension=2, tiled=True),
        lax.psum_scatter(stacked[1], "dp", scatter_dimension=2, tiled=True),
        lax.psum_scatter(stacked[2], "dp", scatter_dimension=2, tiled=True),
        lax.psum_scatter(stacked[3], "dp", scatter_dimension=2, tiled=True),
    )
    small_sums = lax.psum((stacked[4], stacked[5]), "dp")
    totals_all = (
        matrix_sums[0],
        matrix_sums[1],
        matrix_sums[2],
        matrix_sums[3],
        small_sums[0],
        small_sums[1],
    )
    results = [stream[None], upstream[None]]
    for group_index in range(6):
        group_rate = learning_rate if group_index < 4 else small_rate
        new_master, new_first, new_second, new_copy = adamw(
            masters[group_index],
            firsts[group_index],
            seconds[group_index],
            totals_all[group_index],
            group_rate,
        )
        results.extend([totals_all[group_index], new_master, new_first, new_second, new_copy])
    return tuple(results)


def solution(mesh):
    placed = (
        P(("dp", "fsdp"), None, None),
        P(("dp", "fsdp"), None, None),
        P(("dp", "fsdp"), None),
        P(None, "fsdp", None),
        P(None, "fsdp", None),
        P(None, "fsdp", None),
        P(None, "fsdp", None),
        P(None, None, "fsdp"),
        P(None, None, "fsdp"),
        P(None, "fsdp", "dp"),
        P(None, "fsdp", "dp"),
        P(None, "fsdp", "dp"),
        P(None, "fsdp", "dp"),
        P(None, None, "fsdp"),
        P(None, None, "fsdp"),
        P(None, "fsdp", "dp"),
        P(None, "fsdp", "dp"),
        P(None, "fsdp", "dp"),
        P(None, "fsdp", "dp"),
        P(None, None, "fsdp"),
        P(None, None, "fsdp"),
        P(None, "fsdp", "dp"),
        P(None, "fsdp", "dp"),
        P(None, "fsdp", "dp"),
        P(None, "fsdp", "dp"),
        P(None, None, "fsdp"),
        P(None, None, "fsdp"),
    )
    return jax.shard_map(
        local,
        mesh=mesh,
        in_specs=placed,
        out_specs=(
            P(("dp", "fsdp"), None, None),
            P(("dp", "fsdp"), None, None),
            P(None, "fsdp", "dp"),
            P(None, "fsdp", "dp"),
            P(None, "fsdp", "dp"),
            P(None, "fsdp", "dp"),
            P(None, "fsdp", "dp"),
            P(None, "fsdp", "dp"),
            P(None, "fsdp", "dp"),
            P(None, "fsdp", "dp"),
            P(None, "fsdp", "dp"),
            P(None, "fsdp", "dp"),
            P(None, "fsdp", "dp"),
            P(None, "fsdp", "dp"),
            P(None, "fsdp", "dp"),
            P(None, "fsdp", "dp"),
            P(None, "fsdp", "dp"),
            P(None, "fsdp", "dp"),
            P(None, "fsdp", "dp"),
            P(None, "fsdp", "dp"),
            P(None, "fsdp", "dp"),
            P(None, "fsdp", "dp"),
            P(None, None, "fsdp"),
            P(None, None, "fsdp"),
            P(None, None, "fsdp"),
            P(None, None, "fsdp"),
            P(None, None, "fsdp"),
            P(None, None, "fsdp"),
            P(None, None, "fsdp"),
            P(None, None, "fsdp"),
            P(None, None, "fsdp"),
            P(None, None, "fsdp"),
        ),
        check_vma=False,
    )
```

profile of v0, /device:TPU:0, one launch (start us, length us, event | category | flops | bytes accessed | tf_op | source)
XLA Modules:
  0.0 1265.2 jit_solution(5211753290707726675)
XLA Ops:
  10.8 45.5 %all-gather.1 = bf16[1,10,768]{1,0,2:T(2,128)(2,1)S(1)} all-gather(bf16[1,10,48]{1,0,2:T(2,128)(2,1)S(1)} %copy.100), channel_id=3, replica_groups=mesh['dp'=2,'fsdp'=16] {'fsdp'}, dimensions={2}, use_global_device_ids=true | all-gather | bytes 16320 | tf_op jit(solution)/shard_map/all_gather | solution.py:206
  56.8 0.9 slice.99
  57.8 39.5 %all-gather = bf16[1,2,768]{1,0,2:T(2,128)(2,1)S(1)} all-gather(bf16[1,2,48]{1,0,2:T(2,128)(2,1)S(1)} %copy.99), channel_id=2, replica_groups=mesh['dp'=2,'fsdp'=16] {'fsdp'}, dimensions={2}, use_global_device_ids=true | all-gather | bytes 3264 | tf_op jit(solution)/shard_map/all_gather | solution.py:205
  98.6 1.3 iota_compare_fusion.1
  99.9 13.5 %slice_reduce_fusion.3 = (f32[768]{0:T(1024)S(1)}, f32[768]{0:T(1024)S(1)}, f32[768]{0:T(1024)S(1)}, f32[768]{0:T(1024)S(1)}, f32[768]{0:T(1024)S(1)}, /*index=5*/f32[768]{0:T(1024)}) fusion(f32[1,10,768]{1,0,2:T(1,128)S(1)} %convert_element_type.117), kind=kLoop, calls=%fused_computation.72 | loop fusion | bytes 36864 | tf_op jit(solution)/shard_map/slice | solution.py:71
  113.7 4.5 slice_reduce_fusion.4
  118.5 2.7 fusion.12
  121.8 1.3 fusion.98
  123.7 24.8 %all-gather.13.cloned.1.call-done = bf16[1,768,768]{2,1,0:T(8,128)(2,1)} async-done(((bf16[1,48,768]{2,1,0:T(8,128)(2,1)}), bf16[1,768,768]{2,1,0:T(8,128)(2,1)}) %all-gather.13.cloned.1.call-update) | async-done | bytes 1179664 | tf_op jit(solution)/shard_map/all_gather | solution.py:202
  148.5 1.7 fusion.99
  150.4 80.2 %all-gather.15.cloned.1.call-done = bf16[1,768,3072]{2,1,0:T(8,128)(2,1)} async-done(((bf16[1,48,3072]{2,1,0:T(8,128)(2,1)}), bf16[1,768,3072]{2,1,0:T(8,128)(2,1)}) %all-gather.15.cloned.1.call-update) | async-done | bytes 4718608 | tf_op jit(solution)/shard_map/all_gather | solution.py:203
  230.7 3.2 fusion.9
  233.9 78.5 %all-gather.17.cloned.1.call-done = bf16[1,3072,768]{2,1,0:T(8,128)(2,1)} async-done(((bf16[1,192,768]{2,1,0:T(8,128)(2,1)}), bf16[1,3072,768]{2,1,0:T(8,128)(2,1)}) %all-gather.17.cloned.1.call-update) | async-done | bytes 4718608 | tf_op jit(solution)/shard_map/all_gather | solution.py:204
  312.5 5.0 convert_reduce_fusion
  317.5 2.3 multiply_reduce_fusion.1
  320.1 1.4 convert_reduce_fusion.3
  321.5 2.8 fusion.100
  324.6 1.4 multiply_divide_fusion
  326.0 2.1 fusion.41
  328.1 1.1 copy.106
  329.3 2.4 multiply_reduce_fusion
  332.3 2.4 convolution_convert_fusion
  334.7 1.4 multiply_convert_fusion.1
  336.7 4.1 fusion.75
  340.9 1.1 copy-done.6
  342.0 5.8 fusion.80
  348.5 4.2 fusion.81
  353.0 1.0 copy.122
  353.9 1.7 convert_reduce_fusion.1
  355.6 1.0 fusion.78
  358.0 0.9 copy.124
  359.0 5.2 fusion.60
  364.3 87.3 %reduce-scatter.19.cloned.1.call-done = f32[48,768]{1,0:T(8,128)} async-done(((f32[768,768]{1,0:T(8,128)}), f32[48,768]{1,0:T(8,128)}) %reduce-scatter.19.cloned.1.call-update) | async-done | bytes 147472 | tf_op jit(solution)/shard_map/reduce_scatter | solution.py:226
  451.6 156.4 %reduce-scatter.15.cloned.1.call-done = f32[48,2304]{1,0:T(8,128)} async-done(((f32[768,2304]{1,0:T(8,128)}), f32[48,2304]{1,0:T(8,128)}) %reduce-scatter.15.cloned.1.call-update) | async-done | bytes 442384 | tf_op jit(solution)/shard_map/reduce_scatter | solution.py:225
  608.2 176.3 %reduce-scatter.23.cloned.1.call-done = f32[48,3072]{1,0:T(8,128)} async-done(((f32[768,3072]{1,0:T(8,128)}), f32[48,3072]{1,0:T(8,128)}) %reduce-scatter.23.cloned.1.call-update) | async-done | bytes 589840 | tf_op jit(solution)/shard_map/reduce_scatter | solution.py:227
  784.7 4.3 fusion.35
  788.9 120.7 %reduce-scatter.31.cloned.1.call-done = f32[48,2]{1,0:T(8,128)} async-done(((f32[768,2]{1,0:T(8,128)}), f32[48,2]{1,0:T(8,128)}) %reduce-scatter.31.cloned.1.call-update) | async-done | bytes 400
  910.5 125.3 %reduce-scatter.33.cloned.1.call-done = f32[48,10]{1,0:T(8,128)} async-done(((f32[768,10]{1,0:T(8,128)}), f32[48,10]{1,0:T(8,128)}) %reduce-scatter.33.cloned.1.call-update) | async-done | bytes 1936
  1036.6 2.5 all-reduce
  1042.7 168.7 %reduce-scatter.27.cloned.1.call-done = f32[192,768]{1,0:T(8,128)} async-done(((f32[3072,768]{1,0:T(8,128)}), f32[192,768]{1,0:T(8,128)}) %reduce-scatter.27.cloned.1.call-update) | async-done | bytes 589840 | tf_op jit(solution)/shard_map/reduce_scatter | solution.py:228
  1211.4 9.3 reduce-scatter.21.cloned.1.call-done
  1220.7 1.6 fusion.91
  1222.3 10.2 reduce-scatter.17.cloned.1.call-done
  1232.5 1.9 fusion.93
  1234.4 10.1 reduce-scatter.25.cloned.1.call-done
  1244.6 2.1 fusion.89
  1246.7 9.9 reduce-scatter.29.cloned.1.call-done
  1256.6 2.1 fusion.87
  (197 shorter events, 16.9 us)
Async XLA Ops:
  7.2 50.5 %copy-start.58 = (bf16[1,2,48]{2,1,0:T(2,128)(2,1)S(1)}, bf16[1,2,48]{2,1,0:T(2,128)(2,1)}, u32[]{:S(2)}) copy-start(bf16[1,2,48]{2,1,0:T(2,128)(2,1)} %param.34) | copy-start | bytes 580
  7.2 111.2 %all-gather.11.cloned.1.call-start = ((), (), s32[]{:S(2)}) async-start(), calls=%async_computation.18 | async-start | bytes 3760128 | tf_op jit(solution)/shard_map/all_gather | solution.py:201
  7.9 140.5 %all-gather.13.cloned.1.call-start = ((), (), s32[]{:S(2)}) async-start(), calls=%async_computation.19 | async-start | bytes 1253376 | tf_op jit(solution)/shard_map/all_gather | solution.py:202
  8.7 222.0 %all-gather.15.cloned.1.call-start = ((), (), s32[]{:S(2)}) async-start(), calls=%async_computation.20 | async-start | bytes 5013504 | tf_op jit(solution)/shard_map/all_gather | solution.py:203
  9.4 303.0 %all-gather.17.cloned.1.call-start = ((), (), s32[]{:S(2)}) async-start(), calls=%async_computation.21 | async-start | bytes 5013504 | tf_op jit(solution)/shard_map/all_gather | solution.py:204
  10.0 441.6 %reduce-scatter.19.cloned.1.call-start = ((), (), s32[]{:S(2)}) async-start(), calls=%async_computation.12 | async-start | bytes 2506752 | tf_op jit(solution)/shard_map/reduce_scatter | solution.py:226
  56.4 41.6 %copy-start.50 = (s32[1,2]{1,0:T(1,128)S(1)}, s32[1,2]{1,0:T(1,128)}, u32[]{:S(2)}) copy-start(s32[1,2]{1,0:T(1,128)} %param.29) | copy-start | bytes 28
  97.7 15.7 %copy-start.1 = (bf16[1,128,768]{2,1,0:T(8,128)(2,1)S(1)}, bf16[1,128,768]{2,1,0:T(8,128)(2,1)}, u32[]{:S(2)}) copy-start(bf16[1,128,768]{2,1,0:T(8,128)(2,1)} %param.27) | copy-start | bytes 589828
  113.5 7.7 copy-start.33
  113.7 4.6 copy-start.56
  118.4 4.7 copy-start.31
  150.2 169.6 %copy-start.36 = (f32[128]{0:T(128)}, f32[128]{0:T(128)S(1)}, u32[]{:S(2)}) copy-start(f32[128]{0:T(128)S(1)} %broadcast_multiply_fusion) | copy-start | bytes 1540
  150.4 169.4 %copy-start.44 = (f32[128]{0:T(128)}, f32[128]{0:T(128)S(1)}, u32[]{:S(2)}) copy-start(f32[128]{0:T(128)S(1)} %fusion.71) | copy-start | bytes 1540
  230.7 81.8 %copy-start.8 = (bf16[1,128,768]{2,1,0:T(8,128)(2,1)S(1)}, bf16[1,128,768]{2,1,0:T(8,128)(2,1)}, u32[]{:S(2)}) copy-start(bf16[1,128,768]{2,1,0:T(8,128)(2,1)} %param.28) | copy-start | bytes 589828
  312.5 5.0 copy-start
  324.3 283.8 %reduce-scatter.15.cloned.1.call-start = ((), (), s32[]{:S(2)}) async-start(), calls=%async_computation.10 | async-start | bytes 7520256 | tf_op jit(solution)/shard_map/reduce_scatter | solution.py:225
  336.7 11.8 copy-start.9
  340.9 443.6 %reduce-scatter.23.cloned.1.call-start = ((), (), s32[]{:S(2)}) async-start(), calls=%async_computation.14 | async-start | bytes 10027008 | tf_op jit(solution)/shard_map/reduce_scatter | solution.py:227
  347.8 561.9 %reduce-scatter.31.cloned.1.call-start = ((), (), s32[]{:S(2)}) async-start(), calls=%async_computation.22 | async-start | bytes 417792
  348.5 4.2 copy-start.57
  348.5 4.2 copy-start.43
  348.5 5.5 copy-start.4
  356.7 679.1 %reduce-scatter.33.cloned.1.call-start = ((), (), s32[]{:S(2)}) async-start(), calls=%async_computation.23 | async-start | bytes 417792
  359.0 852.4 %reduce-scatter.27.cloned.1.call-start = ((), (), s32[]{:S(2)}) async-start(), calls=%async_computation.16 | async-start | bytes 10027008 | tf_op jit(solution)/shard_map/reduce_scatter | solution.py:228
  364.2 420.3 %copy-start.48 = (f32[768]{0:T(1024)S(1)}, f32[768]{0:T(1024)}, u32[]{:S(2)}) copy-start(f32[768]{0:T(1024)} %get-tuple-element.112) | copy-start | bytes 9220
  364.3 856.5 %reduce-scatter.21.cloned.1.call-start = ((), (), s32[]{:S(2)}) async-start(), calls=%async_computation.13 | async-start | bytes 221184 | tf_op jit(solution)/shard_map/reduce_scatter | solution.py:254
  451.6 780.9 %reduce-scatter.17.cloned.1.call-start = ((), (), s32[]{:S(2)}) async-start(), calls=%async_computation.11 | async-start | bytes 663552 | tf_op jit(solution)/shard_map/reduce_scatter | solution.py:253
  608.1 636.5 %reduce-scatter.25.cloned.1.call-start = ((), (), s32[]{:S(2)}) async-start(), calls=%async_computation.15 | async-start | bytes 884736 | tf_op jit(solution)/shard_map/reduce_scatter | solution.py:255
  784.5 472.1 %reduce-scatter.29.cloned.1.call-start = ((), (), s32[]{:S(2)}) async-start(), calls=%async_computation.17 | async-start | bytes 884736 | tf_op jit(solution)/shard_map/reduce_scatter | solution.py:256
  784.5 255.2 %copy-start.45 = (f32[1,10,48]{2,0,1:T(1,128)S(1)}, f32[1,10,48]{2,0,1:T(1,128)}, u32[]{:S(2)}) copy-start(f32[1,10,48]{2,0,1:T(1,128)} %param.41) | copy-start | bytes 5764
  784.5 255.2 %copy-start.46 = (f32[1,10,48]{2,0,1:T(1,128)S(1)}, f32[1,10,48]{2,0,1:T(1,128)}, u32[]{:S(2)}) copy-start(f32[1,10,48]{2,0,1:T(1,128)} %param.47) | copy-start | bytes 5764
  784.5 255.1 %copy-start.47 = (f32[1,10,48]{2,0,1:T(1,128)S(1)}, f32[1,10,48]{2,0,1:T(1,128)}, u32[]{:S(2)}) copy-start(f32[1,10,48]{2,0,1:T(1,128)} %param.53) | copy-start | bytes 5764
  784.6 257.6 %copy-start.52 = (f32[1,2,48]{2,1,0:T(2,128)S(1)}, f32[1,2,48]{2,1,0:T(2,128)}, u32[]{:S(2)}) copy-start(f32[1,2,48]{2,1,0:T(2,128)} %param.40) | copy-start | bytes 1156
  784.6 257.5 %copy-start.53 = (f32[1,2,48]{2,1,0:T(2,128)S(1)}, f32[1,2,48]{2,1,0:T(2,128)}, u32[]{:S(2)}) copy-start(f32[1,2,48]{2,1,0:T(2,128)} %param.46) | copy-start | bytes 1156
  784.6 257.5 %copy-start.54 = (f32[1,2,48]{2,1,0:T(2,128)S(1)}, f32[1,2,48]{2,1,0:T(2,128)}, u32[]{:S(2)}) copy-start(f32[1,2,48]{2,1,0:T(2,128)} %param.52) | copy-start | bytes 1156
  784.6 436.1 %copy-start.28 = (f32[1,48,384]{2,1,0:T(8,128)S(1)}, f32[1,48,384]{2,1,0:T(8,128)}, u32[]{:S(2)}) copy-start(f32[1,48,384]{2,1,0:T(8,128)} %param.37) | copy-start | bytes 221188
  784.6 436.1 %copy-start.29 = (f32[1,48,384]{2,1,0:T(8,128)S(1)}, f32[1,48,384]{2,1,0:T(8,128)}, u32[]{:S(2)}) copy-start(f32[1,48,384]{2,1,0:T(8,128)} %param.43) | copy-start | bytes 221188
  784.6 436.1 %copy-start.30 = (f32[1,48,384]{2,1,0:T(8,128)S(1)}, f32[1,48,384]{2,1,0:T(8,128)}, u32[]{:S(2)}) copy-start(f32[1,48,384]{2,1,0:T(8,128)} %param.49) | copy-start | bytes 221188
  784.6 447.9 %copy-start.25 = (f32[1,48,1152]{2,1,0:T(8,128)S(1)}, f32[1,48,1152]{2,1,0:T(8,128)}, u32[]{:S(2)}) copy-start(f32[1,48,1152]{2,1,0:T(8,128)} %param.36) | copy-start | bytes 663556
  784.6 447.9 %copy-start.26 = (f32[1,48,1152]{2,1,0:T(8,128)S(1)}, f32[1,48,1152]{2,1,0:T(8,128)}, u32[]{:S(2)}) copy-start(f32[1,48,1152]{2,1,0:T(8,128)} %param.42) | copy-start | bytes 663556
  784.6 447.9 %copy-start.27 = (f32[1,48,1152]{2,1,0:T(8,128)S(1)}, f32[1,48,1152]{2,1,0:T(8,128)}, u32[]{:S(2)}) copy-start(f32[1,48,1152]{2,1,0:T(8,128)} %param.48) | copy-start | bytes 663556
  788.9 455.7 %copy-start.19 = (f32[1,48,1536]{2,1,0:T(8,128)S(1)}, f32[1,48,1536]{2,1,0:T(8,128)}, u32[]{:S(2)}) copy-start(f32[1,48,1536]{2,1,0:T(8,128)} %param.38) | copy-start | bytes 884740
  788.9 455.7 %copy-start.20 = (f32[1,48,1536]{2,1,0:T(8,128)S(1)}, f32[1,48,1536]{2,1,0:T(8,128)}, u32[]{:S(2)}) copy-start(f32[1,48,1536]{2,1,0:T(8,128)} %param.44) | copy-start | bytes 884740
  788.9 455.7 %copy-start.21 = (f32[1,48,1536]{2,1,0:T(8,128)S(1)}, f32[1,48,1536]{2,1,0:T(8,128)}, u32[]{:S(2)}) copy-start(f32[1,48,1536]{2,1,0:T(8,128)} %param.50) | copy-start | bytes 884740
  1039.1 207.6 %copy-start.55 = (f32[1,2,48]{2,1,0:T(2,128)}, f32[1,2,48]{2,1,0:T(2,128)S(1)}, u32[]{:S(2)}) copy-start(f32[1,2,48]{2,1,0:T(2,128)S(1)} %get-tuple-element.113) | copy-start | bytes 1156
  1222.3 34.3 %copy-start.22 = (f32[1,192,384]{2,1,0:T(8,128)S(1)}, f32[1,192,384]{2,1,0:T(8,128)}, u32[]{:S(2)}) copy-start(f32[1,192,384]{2,1,0:T(8,128)} %param.39) | copy-start | bytes 884740
  1222.3 34.3 %copy-start.23 = (f32[1,192,384]{2,1,0:T(8,128)S(1)}, f32[1,192,384]{2,1,0:T(8,128)}, u32[]{:S(2)}) copy-start(f32[1,192,384]{2,1,0:T(8,128)} %param.45) | copy-start | bytes 884740
  1222.3 34.3 %copy-start.24 = (f32[1,192,384]{2,1,0:T(8,128)S(1)}, f32[1,192,384]{2,1,0:T(8,128)}, u32[]{:S(2)}) copy-start(f32[1,192,384]{2,1,0:T(8,128)} %param.51) | copy-start | bytes 884740
  (25 other events, 47.5 us)
Sparse Core Ops, SparseCore 0:
  10.8 79.2 all-gather.10
  93.0 55.4 all-gather.12
  151.3 79.3 all-gather.14
  233.3 79.0 all-gather.16
  324.4 127.0 reduce-scatter.18
  457.6 150.4 reduce-scatter.14
  614.7 169.6 reduce-scatter.22
  789.1 120.5 reduce-scatter.30
  915.0 120.7 reduce-scatter.32
  1041.3 170.0 reduce-scatter.26
  1214.2 6.4 reduce-scatter.20
  1223.5 8.9 reduce-scatter.16
  1235.4 9.1 reduce-scatter.24
  1247.4 9.1 reduce-scatter.28
where the time goes:
time: 1270 us
  waiting for transfers between devices  1060 us (83%)
  blocking collectives  87.5 us (7%)
  matrix products  50.7 us (4%)
  local copies, waits for them, and re-layouts  31.1 us (2%)
  other arithmetic  19.9 us (2%)
  between operations  14.7 us (1%)
    unnamed x16, waiting for transfers between devices  249 us
    reduce_scatter x1, waiting for transfers between devices, local(): lax.psum_scatter(matrices[2], 'fsdp', scatter_dimension=0, tiled=True)  176 us
    reduce_scatter x1, waiting for transfers between devices, local(): lax.psum_scatter(matrices[3], 'fsdp', scatter_dimension=0, tiled=True)  169 us
    reduce_scatter x1, waiting for transfers between devices, local(): lax.psum_scatter(matrices[0], 'fsdp', scatter_dimension=0, tiled=True)  156 us
    reduce_scatter x1, waiting for transfers between devices, local(): lax.psum_scatter(matrices[1], 'fsdp', scatter_dimension=0, tiled=True)  87.3 us
    all_gather x1, waiting for transfers between devices, local(): lax.all_gather(expand_weight[layer_index], 'fsdp', axis=0, tiled=True)  80.2 us
    all_gather x1, waiting for transfers between devices, local(): lax.all_gather(shrink_weight[layer_index], 'fsdp', axis=0, tiled=True)  78.5 us
    all_gather x1, blocking collectives, local(): lax.all_gather(bias_rows[layer_index], 'fsdp', axis=1, tiled=True)  45.5 us
  transfers between devices with their start and end apart: 14, of which 13 were waited for; matrix products, arithmetic and copies ran while one was open for 7% of the time, Pallas kernels for 0%

commit v1 on v0

--- a/solution.py
+++ b/solution.py
@@ -78,14 +78,14 @@
     return (middle + second, kept)
 
 
-def layer_back(stream, gathered, visible, upstream):
+def layer_both(stream, gathered, visible, upstream):
     joint_mat, output, expand, shrink, gain_rows, biases = gathered
     token_count, model_width = stream.shape
     head_count = model_width // HEAD_DIM
     score_scale = HEAD_DIM ** (-0.5)
     gain_full = gain_rows.astype(jnp.float32)
     bias_full = biases.astype(jnp.float32)
-    unused_out, kept = layer_parts(stream, gathered, visible)
+    result, kept = layer_parts(stream, gathered, visible)
     normed, projected, scaled, attend_low, attended, middle, normed_two, hidden, active = kept
     queries = projected[:, :model_width].reshape(token_count, head_count, HEAD_DIM)
     key_rows = projected[:, model_width : 2 * model_width].reshape(
@@ -147,6 +147,7 @@
         ]
     )
     return (
+        result,
         back_middle + back_stream,
         (grad_joint, grad_output, grad_expand, grad_shrink, gain_grad, bias_grad),
     )
@@ -161,6 +162,109 @@
         first_hat / (jnp.sqrt(second_hat) + epsilon) + weight_decay * master
     )
     return (master_new, first_new, second_new, master_new.astype(jnp.bfloat16))
+
+
+def bit_plan(size):
+    bits = size.bit_length() - 1
+    side = bits // 3
+    x_bits = tuple(range(side))
+    y_bits = tuple(range(side, 2 * side))
+    z_bits = tuple(range(2 * side, bits))
+    return x_bits, y_bits, z_bits
+
+
+def swap(value, bit, size):
+    return lax.ppermute(value, "fsdp", [(i, i ^ (1 << bit)) for i in range(size)])
+
+
+def swap_core(value):
+    return lax.ppermute(value, "dp", [(0, 1), (1, 0)])
+
+
+def gather_bits(value, bits, held, index, size):
+    held = list(held)
+    for bit in bits:
+        other = swap(value, bit, size)
+        mine = ((index >> bit) & 1) == 0
+        spot = sum(1 for kept in held if kept > bit)
+        low = jnp.where(mine, value, other)
+        high = jnp.where(mine, other, value)
+        value = jnp.stack([low, high], axis=spot)
+        held.append(bit)
+    return value, held
+
+
+def gather_weight(shard, index, core, size):
+    x_bits, y_bits, z_bits = bit_plan(size)
+    rows, width = shard.shape
+    half = width // 2
+    mine = lax.dynamic_slice_in_dim(shard, core * half, half, axis=1)
+    depth, held = gather_bits(mine, z_bits, (), index, size)
+    lead = len(held)
+    one = lax.slice_in_dim(depth, 0, rows // 2, axis=lead)
+    two = lax.slice_in_dim(depth, rows // 2, rows, axis=lead)
+    one, held_one = gather_bits(one, x_bits + y_bits, held, index, size)
+    two, held_two = gather_bits(two, y_bits + x_bits, held, index, size)
+    whole = jnp.concatenate([one, two], axis=len(held_one)).reshape(size * rows, half)
+    other = swap_core(whole)
+    return jnp.concatenate(
+        [jnp.where(core == 0, whole, other), jnp.where(core == 0, other, whole)], axis=1
+    )
+
+
+def scatter_bits(value, bits, held, index, size, last=False):
+    held = list(held)
+    for place, bit in enumerate(bits):
+        spot = sum(1 for kept in held if kept > bit)
+        mine = (index >> bit) & 1
+        keep = lax.dynamic_index_in_dim(value, mine, axis=spot, keepdims=False)
+        send = lax.dynamic_index_in_dim(value, 1 - mine, axis=spot, keepdims=False)
+        got = swap(send, bit, size)
+        value = keep.astype(jnp.float32) + got.astype(jnp.float32)
+        held.remove(bit)
+        if not (last and place == len(bits) - 1):
+            value = value.astype(jnp.bfloat16)
+    return value, held
+
+
+def scatter_grad(grad, index, core, size):
+    x_bits, y_bits, z_bits = bit_plan(size)
+    total_rows, width = grad.shape
+    rows = total_rows // size
+    half = width // 2
+    keep = lax.dynamic_slice_in_dim(grad, core * half, half, axis=1)
+    send = lax.dynamic_slice_in_dim(grad, (1 - core) * half, half, axis=1)
+    got = swap_core(send)
+    value = (keep.astype(jnp.float32) + got.astype(jnp.float32)).astype(jnp.bfloat16)
+    bits = len(x_bits) + len(y_bits) + len(z_bits)
+    value = value.reshape((2,) * bits + (rows, half))
+    held = list(range(bits))
+    one = lax.slice_in_dim(value, 0, rows // 2, axis=bits)
+    two = lax.slice_in_dim(value, rows // 2, rows, axis=bits)
+    one, held_one = scatter_bits(one, y_bits + x_bits, held, index, size)
+    two, held_two = scatter_bits(two, x_bits + y_bits, held, index, size)
+    both = jnp.concatenate([one, two], axis=len(held_one))
+    result, _ = scatter_bits(both, tuple(reversed(z_bits)), held_one, index, size, last=True)
+    return result
+
+
+def sum_all(value, size):
+    value = value + swap_core(value)
+    bits = size.bit_length() - 1
+    for bit in range(bits):
+        value = value + swap(value, bit, size)
+    return value
+
+
+def join_small(gains, biases, index, size):
+    piece = jnp.concatenate([gains, biases], axis=0)
+    rows, width = piece.shape
+    room = jnp.zeros((rows, width * size), piece.dtype)
+    value = lax.dynamic_update_slice(room, piece, (0, index * width))
+    bits = size.bit_length() - 1
+    for bit in range(bits):
+        value = value + swap(value, bit, size)
+    return value
 
 
 def local(
@@ -192,46 +296,29 @@
     second_gains,
     second_biases,
 ):
+    size = lax.axis_size("fsdp")
+    index = lax.axis_index("fsdp")
+    core = lax.axis_index("dp")
     stream = tokens[0].astype(jnp.float32)
     visible = visible_mask(lengths[0, 0], lengths[0, 1], stream.shape[0])
-    layers = joint_weight.shape[0]
-    gathered_kept = []
-    layer_index = 0
+    small = join_small(norm_gains[0], bias_rows[0], index, size)
     gathered = (
-        lax.all_gather(joint_weight[layer_index], "fsdp", axis=0, tiled=True),
-        lax.all_gather(output_weight[layer_index], "fsdp", axis=0, tiled=True),
-        lax.all_gather(expand_weight[layer_index], "fsdp", axis=0, tiled=True),
-        lax.all_gather(shrink_weight[layer_index], "fsdp", axis=0, tiled=True),
-        lax.all_gather(norm_gains[layer_index], "fsdp", axis=1, tiled=True),
-        lax.all_gather(bias_rows[layer_index], "fsdp", axis=1, tiled=True),
-    )
-    gathered_kept.append(gathered)
-    inputs_kept = [stream]
-    stream, unused_kept = layer_parts(stream, gathered, visible)
+        gather_weight(joint_weight[0], index, core, size),
+        gather_weight(output_weight[0], index, core, size),
+        gather_weight(expand_weight[0], index, core, size),
+        gather_weight(shrink_weight[0], index, core, size),
+        small[:2],
+        small[2:],
+    )
     upstream = cotangent[0].astype(jnp.float32)
-    pieces = [None] * layers
-    for layer_index in reversed(range(layers)):
-        gathered = (
-            lax.all_gather(joint_weight[layer_index], "fsdp", axis=0, tiled=True),
-            lax.all_gather(output_weight[layer_index], "fsdp", axis=0, tiled=True),
-            lax.all_gather(expand_weight[layer_index], "fsdp", axis=0, tiled=True),
-            lax.all_gather(shrink_weight[layer_index], "fsdp", axis=0, tiled=True),
-            lax.all_gather(norm_gains[layer_index], "fsdp", axis=1, tiled=True),
-            lax.all_gather(bias_rows[layer_index], "fsdp", axis=1, tiled=True),
-        )
-        upstream, layer_grads = layer_back(inputs_kept[layer_index], gathered, visible, upstream)
-        matrices = (layer_grads[0], layer_grads[1], layer_grads[2], layer_grads[3])
-        pieces[layer_index] = (
-            lax.psum_scatter(matrices[0], "fsdp", scatter_dimension=0, tiled=True),
-            lax.psum_scatter(matrices[1], "fsdp", scatter_dimension=0, tiled=True),
-            lax.psum_scatter(matrices[2], "fsdp", scatter_dimension=0, tiled=True),
-            lax.psum_scatter(matrices[3], "fsdp", scatter_dimension=0, tiled=True),
-            lax.psum_scatter(layer_grads[4], "fsdp", scatter_dimension=1, tiled=True),
-            lax.psum_scatter(layer_grads[5], "fsdp", scatter_dimension=1, tiled=True),
-        )
-    stacked = tuple(
-        (jnp.stack([piece[group_index] for piece in pieces]) for group_index in range(6))
-    )
+    result, input_grad, layer_grads = layer_both(stream, gathered, visible, upstream)
+    matrix_sums = tuple(
+        scatter_grad(layer_grads[place].astype(jnp.bfloat16), index, core, size)
+        for place in range(4)
+    )
+    small_grads = sum_all(jnp.concatenate([layer_grads[4], layer_grads[5]], axis=0), size)
+    width = norm_gains.shape[2]
+    small_own = lax.dynamic_slice_in_dim(small_grads, index * width, width, axis=1)
     masters = (
         master_joint,
         master_output,
@@ -249,22 +336,11 @@
         second_gains,
         second_biases,
     )
-    matrix_sums = (
-        lax.psum_scatter(stacked[0], "dp", scatter_dimension=2, tiled=True),
-        lax.psum_scatter(stacked[1], "dp", scatter_dimension=2, tiled=True),
-        lax.psum_scatter(stacked[2], "dp", scatter_dimension=2, tiled=True),
-        lax.psum_scatter(stacked[3], "dp", scatter_dimension=2, tiled=True),
-    )
-    small_sums = lax.psum((stacked[4], stacked[5]), "dp")
-    totals_all = (
-        matrix_sums[0],
-        matrix_sums[1],
-        matrix_sums[2],
-        matrix_sums[3],
-        small_sums[0],
-        small_sums[1],
-    )
-    results = [stream[None], upstream[None]]
+    totals_all = tuple(value[None] for value in matrix_sums) + (
+        small_own[None, :2],
+        small_own[None, 2:],
+    )
+    results = [result[None], input_grad[None]]
     for group_index in range(6):
         group_rate = learning_rate if group_index < 4 else small_rate
         new_master, new_first, new_second, new_copy = adamw(

time: 1270 us -> 282 us (0.22)
  waiting for transfers between devices: 1060 us -> 132 us
  blocking collectives: 87.5 us -> 0 us
  starting transfers between devices: 0.77 us -> 65.7 us
  matrix products: 50.7 us -> 27.8 us
  other arithmetic: 19.9 us -> 34.4 us
    reduce_scatter x8 -> x0, waiting for transfers between devices: 628 us -> none  [the longest x1 176 us: local(): lax.psum_scatter(matrices[2], 'fsdp', scatter_dimension=0, tiled=True)]
    unnamed x16 -> x0, waiting for transfers between devices: 249 us -> none
    all_gather x4 -> x0, waiting for transfers between devices: 184 us -> none  [the longest x1 80.2 us: local(): lax.all_gather(expand_weight[layer_index], 'fsdp', axis=0, tiled=True)]
    ppermute x0 -> x65, waiting for transfers between devices: none -> 132 us  [the longest x56 132 us: swap(): return lax.ppermute(value, 'fsdp', [(i, i ^ 1 << bit) for i in range(size)])]
    all_gather x2 -> x0, blocking collectives: 85.1 us -> none  [the longest x1 45.5 us: local(): lax.all_gather(bias_rows[layer_index], 'fsdp', axis=1, tiled=True)]
    ppermute x0 -> x65, starting transfers between devices: none -> 65.7 us  [the longest x56 64.5 us: swap(): return lax.ppermute(value, 'fsdp', [(i, i ^ 1 << bit) for i in range(size)])]
    slice x1, local copies, waits for them, and re-layouts: 13.5 us -> 0.63 us  [layer_parts(): bias_full[1]]
  transfers between devices with their start and end apart: 14 -> 65, of which waited for: 13 -> 39; matrix products, arithmetic and copies ran while one was open for 7% -> 17% of each run, Pallas kernels for 0% -> 0%
where the time goes in v1:
time: 282 us
  waiting for transfers between devices  132 us (47%)
  starting transfers between devices  65.7 us (23%)
  other arithmetic  34.4 us (12%)
  matrix products  27.8 us (10%)
  local copies, waits for them, and re-layouts  19.4 us (7%)
    ppermute x56, waiting for transfers between devices, swap(): return lax.ppermute(value, 'fsdp', [(i, i ^ 1 << bit) for i in range(size)])  132 us
    ppermute x56, starting transfers between devices, swap(): return lax.ppermute(value, 'fsdp', [(i, i ^ 1 << bit) for i in range(size)])  64.5 us
    dot_general x4, matrix products, outer_sum(): lax.dot_general(left, right, (((0,), (0,)), ((), ())), preferred_element_...  11.1 us
    select_n x4, other arithmetic, gather_weight(): jnp.where(core == 0, whole, other)  7.05 us
    dot_general x4, matrix products, times_back(): lax.dot_general(left, right, (((1,), (1,)), ((), ())), preferred_element_...  6.67 us
  transfers between devices with their start and end apart: 65, of which 39 were waited for; matrix products, arithmetic and copies ran while one was open for 17% of the time, Pallas kernels for 0%

profile of v1, /device:TPU:0, one launch (start us, length us, event | category | flops | bytes accessed | tf_op | source)
XLA Modules:
  0.0 281.5 jit_solution(2249262072628932390)
XLA Ops:
  1.6 3.1 %collective-permute-start = (bf16[12,768]{1,0:T(8,128)(2,1)S(1)}, bf16[12,768]{1,0:T(8,128)(2,1)S(1)}, u32[]{:S(2)}, u32[]{:S(2)}) collective-permute-start(bf16[12,768]{1,0:T(8,128)(2,1)S(1)} %dynamic_update_slice.5), channel_id=1, source_target_pairs={{0,1},{1,0},{2,3},{3,2},{4,5},{5,4},{6,7},{7,6},{8,9},{9,8},{10,11... | collective-permute-start | bytes 55304 | tf_op jit(solution)/shard_map/ppermute | solution.py:177
  21.9 2.2 collective-permute-done.1
  28.3 2.4 collective-permute-start.3
  34.5 2.4 collective-permute-start.5
  36.9 11.6 %collective-permute-done.12 = bf16[2,48,384]{2,1,0:T(8,128)(2,1)S(1)} collective-permute-done((bf16[2,48,384]{2,1,0:T(8,128)(2,1)S(1)}, bf16[2,48,384]{2,1,0:T(8,128)(2,1)S(1)}, u32[]{:S(2)}, u32[]{:S(2)}) %collective-permute-start.12) | collective-permute-done | bytes 73760 | tf_op jit(solution)/shard_map/ppermute | solution.py:177
  49.0 3.0 %collective-permute-start.19 = (bf16[2,48,1536]{2,1,0:T(8,128)(2,1)S(1)}, bf16[2,48,1536]{2,1,0:T(8,128)(2,1)S(1)}, u32[]{:S(2)}, u32[]{:S(2)}) collective-permute-start(bf16[2,48,1536]{2,1,0:T(8,128)(2,1)S(1)} %pad_maximum_fusion.33), channel_id=1, source_target_pairs={{0,8},{1,9},{2,10},{3,11},{4,12},{5,13},{6,14},{7,15},{8,0},{9,1},... | collective-permute-start | bytes 884744 | tf_op jit(solution)/shard_map/ppermute | solution.py:177
  54.2 2.0 collective-permute-start.14
  56.4 2.5 collective-permute-done.16
  59.6 6.5 %collective-permute-done.26 = bf16[2,192,384]{2,1,0:T(8,128)(2,1)S(1)} collective-permute-done((bf16[2,192,384]{2,1,0:T(8,128)(2,1)S(1)}, bf16[2,192,384]{2,1,0:T(8,128)(2,1)S(1)}, u32[]{:S(2)}, u32[]{:S(2)}) %collective-permute-start.26) | collective-permute-done | bytes 294944 | tf_op jit(solution)/shard_map/ppermute | solution.py:177
  66.2 2.1 collective-permute-start.29
  73.8 5.6 %collective-permute-done.22 = bf16[2,2,24,1536]{3,2,1,0:T(8,128)(2,1)S(1)} collective-permute-done((bf16[2,2,24,1536]{3,2,1,0:T(8,128)(2,1)S(1)}, bf16[2,2,24,1536]{3,2,1,0:T(8,128)(2,1)S(1)}, u32[]{:S(2)}, u32[]{:S(2)}) %collective-permute-start.22) | collective-permute-done | bytes 294944 | tf_op jit(solution)/shard_map/ppermute | solution.py:177
  82.9 2.9 %collective-permute-done.20 = bf16[2,2,24,1536]{3,2,1,0:T(8,128)(2,1)S(1)} collective-permute-done((bf16[2,2,24,1536]{3,2,1,0:T(8,128)(2,1)S(1)}, bf16[2,2,24,1536]{3,2,1,0:T(8,128)(2,1)S(1)}, u32[]{:S(2)}, u32[]{:S(2)}) %collective-permute-start.20) | collective-permute-done | bytes 294944 | tf_op jit(solution)/shard_map/ppermute | solution.py:177
  88.2 7.0 %collective-permute-done.9 = bf16[2,2,2,24,1152]{4,3,2,1,0:T(8,128)(2,1)S(1)} collective-permute-done((bf16[2,2,2,24,1152]{4,3,2,1,0:T(8,128)(2,1)S(1)}, bf16[2,2,2,24,1152]{4,3,2,1,0:T(8,128)(2,1)S(1)}, u32[]{:S(2)}, u32[]{:S(2)}) %collective-permute-start.9) | collective-permute-done | bytes 442400 | tf_op jit(solution)/shard_map/ppermute | solution.py:177
  96.7 11.2 %collective-permute-done.30 = bf16[2,2,2,96,384]{4,3,2,1,0:T(8,128)(2,1)S(1)} collective-permute-done((bf16[2,2,2,96,384]{4,3,2,1,0:T(8,128)(2,1)S(1)}, bf16[2,2,2,96,384]{4,3,2,1,0:T(8,128)(2,1)S(1)}, u32[]{:S(2)}, u32[]{:S(2)}) %collective-permute-start.30) | collective-permute-done | bytes 589856 | tf_op jit(solution)/shard_map/ppermute | solution.py:177
  108.6 8.5 %collective-permute-done.23 = bf16[2,2,2,24,1536]{4,3,2,1,0:T(8,128)(2,1)S(1)} collective-permute-done((bf16[2,2,2,24,1536]{4,3,2,1,0:T(8,128)(2,1)S(1)}, bf16[2,2,2,24,1536]{4,3,2,1,0:T(8,128)(2,1)S(1)}, u32[]{:S(2)}, u32[]{:S(2)}) %collective-permute-start.23) | collective-permute-done | bytes 589856 | tf_op jit(solution)/shard_map/ppermute | solution.py:177
  121.8 2.1 fusion.139
  127.9 2.7 broadcast_select_fusion.3
  131.5 2.7 broadcast_select_fusion.1
  134.3 2.5 convert_reduce_fusion
  136.8 2.3 multiply_reduce_fusion.1
  146.0 3.1 %convolution_convert_fusion.2 = bf16[768,2304]{1,0:T(8,128)(2,1)} fusion(bf16[1,128,768]{2,1,0:T(8,128)(2,1)S(1)} %copy-done.1, f32[768]{0:T(1024)S(1)} %get-tuple-element.110, f32[768]{0:T(1024)S(1)} %get-tuple-element.247, f32[128]{0:T(128)S(1)} %copy-done.50, f32[128]{0:T(128)S(1)} %copy-done.47, bf16[128,768]{0,1:T(8,128)(2,1)S(1)} %bitcast.489, ...), kind=kOutput, calls=%fused_computation.3 | convolution fusion | flops 457113600 | bytes 4332544 | tf_op jit(solution)/shard_map/dot_general | solution.py:37
  149.1 3.7 %convolution_convert_fusion.1 = bf16[768,3072]{1,0:T(8,128)(2,1)} fusion(bf16[128,3072]{1,0:T(8,128)(2,1)S(1)} %copy-done.15, f32[128,768]{1,0:T(8,128)S(1)} %get-tuple-element.240, f32[768]{0:T(1024)S(1)} %get-tuple-element.105, f32[768]{0:T(1024)S(1)} %get-tuple-element.248, f32[128]{0:T(128)S(1)} %copy-done.56, f32[128]{0:T(128)S(1)} %copy-done.52), kind=kOutput, calls=%fused_computation.2 | convolution fusion | flops 606830592 | bytes 5905408 | tf_op jit(solution)/shard_map/dot_general | solution.py:37
  152.8 3.9 %convolution_convert_fusion = bf16[3072,768]{1,0:T(8,128)(2,1)} fusion(bf16[1,128,768]{2,1,0:T(8,128)(2,1)S(1)} %copy-done.13, f32[128,3072]{1,0:T(8,128)S(1)} %copy-done.3), kind=kOutput, calls=%fused_computation.1 | convolution fusion | flops 609878016 | bytes 6488064 | tf_op jit(solution)/shard_map/dot_general | solution.py:37
  164.0 3.3 %collective-permute-done.61 = f32[12,768]{1,0:T(8,128)S(1)} collective-permute-done((f32[12,768]{1,0:T(8,128)S(1)}, f32[12,768]{1,0:T(8,128)S(1)}, u32[]{:S(2)}, u32[]{:S(2)}) %collective-permute-start.61) | collective-permute-done | bytes 36896 | tf_op jit(solution)/shard_map/ppermute | solution.py:177
  168.5 3.0 %collective-permute-done.62 = f32[12,768]{1,0:T(8,128)S(1)} collective-permute-done((f32[12,768]{1,0:T(8,128)S(1)}, f32[12,768]{1,0:T(8,128)S(1)}, u32[]{:S(2)}, u32[]{:S(2)}) %collective-permute-start.62) | collective-permute-done | bytes 36896 | tf_op jit(solution)/shard_map/ppermute | solution.py:177
  171.5 2.5 collective-permute-start.63
  176.0 3.4 %collective-permute-start.64 = (f32[12,768]{1,0:T(8,128)S(1)}, f32[12,768]{1,0:T(8,128)S(1)}, u32[]{:S(2)}, u32[]{:S(2)}) collective-permute-start(f32[12,768]{1,0:T(8,128)S(1)} %add.514), channel_id=1, source_target_pairs={{0,8},{1,9},{2,10},{3,11},{4,12},{5,13},{6,14},{7,15},{8,0},{9,1},... | collective-permute-start | bytes 110600 | tf_op jit(solution)/shard_map/ppermute | solution.py:177
  179.9 1.9 collective-permute-done.64
  184.0 4.1 %collective-permute-done.40 = bf16[2,2,2,24,384]{4,3,1,0,2:T(8,128)(2,1)S(1)} collective-permute-done((bf16[2,2,2,24,384]{4,3,1,0,2:T(8,128)(2,1)S(1)}, bf16[2,2,2,24,384]{4,3,1,0,2:T(8,128)(2,1)S(1)}, u32[]{:S(2)}, u32[]{:S(2)}) %collective-permute-start.40) | collective-permute-done | bytes 147488 | tf_op jit(solution)/shard_map/ppermute | solution.py:177
  189.0 1.9 collective-permute-start.43
  193.5 3.1 %collective-permute-start.44 = (bf16[2,48,384]{2,1,0:T(8,128)(2,1)S(1)}, bf16[2,48,384]{2,1,0:T(8,128)(2,1)S(1)}, u32[]{:S(2)}, u32[]{:S(2)}) collective-permute-start(bf16[2,48,384]{2,1,0:T(8,128)(2,1)S(1)} %fusion.86), channel_id=1, source_target_pairs={{0,8},{1,9},{2,10},{3,11},{4,12},{5,13},{6,14},{7,15},{8,0},{9,1},... | collective-permute-start | bytes 221192 | tf_op jit(solution)/shard_map/ppermute | solution.py:177
  199.0 2.1 collective-permute-start.45
  204.6 2.1 collective-permute-start.33
  207.8 5.7 %collective-permute-done.33 = bf16[2,2,2,24,1152]{4,3,1,0,2:T(8,128)(2,1)S(1)} collective-permute-done((bf16[2,2,2,24,1152]{4,3,1,0,2:T(8,128)(2,1)S(1)}, bf16[2,2,2,24,1152]{4,3,1,0,2:T(8,128)(2,1)S(1)}, u32[]{:S(2)}, u32[]{:S(2)}) %collective-permute-start.33) | collective-permute-done | bytes 442400 | tf_op jit(solution)/shard_map/ppermute | solution.py:177
  214.7 5.1 %collective-permute-done.35 = bf16[2,2,2,24,1152]{4,3,1,0,2:T(8,128)(2,1)S(1)} collective-permute-done((bf16[2,2,2,24,1152]{4,3,1,0,2:T(8,128)(2,1)S(1)}, bf16[2,2,2,24,1152]{4,3,1,0,2:T(8,128)(2,1)S(1)}, u32[]{:S(2)}, u32[]{:S(2)}) %collective-permute-start.35) | collective-permute-done | bytes 442400 | tf_op jit(solution)/shard_map/ppermute | solution.py:177
  221.2 2.1 collective-permute-start.47
  224.5 3.8 %collective-permute-done.36 = bf16[2,2,24,1152]{3,2,1,0:T(8,128)(2,1)S(1)} collective-permute-done((bf16[2,2,24,1152]{3,2,1,0:T(8,128)(2,1)S(1)}, bf16[2,2,24,1152]{3,2,1,0:T(8,128)(2,1)S(1)}, u32[]{:S(2)}, u32[]{:S(2)}) %collective-permute-start.36) | collective-permute-done | bytes 221216 | tf_op jit(solution)/shard_map/ppermute | solution.py:177
  230.8 2.1 collective-permute-start.54
  232.9 4.8 %collective-permute-done.37 = bf16[2,48,1152]{2,1,0:T(8,128)(2,1)S(1)} collective-permute-done((bf16[2,48,1152]{2,1,0:T(8,128)(2,1)S(1)}, bf16[2,48,1152]{2,1,0:T(8,128)(2,1)S(1)}, u32[]{:S(2)}, u32[]{:S(2)}) %collective-permute-start.37) | collective-permute-done | bytes 221216 | tf_op jit(solution)/shard_map/ppermute | solution.py:177
  238.4 4.2 %collective-permute-done.38 = bf16[48,1152]{1,0:T(8,128)(2,1)S(1)} collective-permute-done((bf16[48,1152]{1,0:T(8,128)(2,1)S(1)}, bf16[48,1152]{1,0:T(8,128)(2,1)S(1)}, u32[]{:S(2)}, u32[]{:S(2)}) %collective-permute-start.38) | collective-permute-done | bytes 110624 | tf_op jit(solution)/shard_map/ppermute | solution.py:177
  245.7 4.3 %collective-permute-done.54 = bf16[2,2,2,96,384]{4,3,1,0,2:T(8,128)(2,1)S(1)} collective-permute-done((bf16[2,2,2,96,384]{4,3,1,0,2:T(8,128)(2,1)S(1)}, bf16[2,2,2,96,384]{4,3,1,0,2:T(8,128)(2,1)S(1)}, u32[]{:S(2)}, u32[]{:S(2)}) %collective-permute-start.54) | collective-permute-done | bytes 589856 | tf_op jit(solution)/shard_map/ppermute | solution.py:177
  252.6 2.9 %collective-permute-done.48 = bf16[2,2,24,1536]{3,2,1,0:T(8,128)(2,1)S(1)} collective-permute-done((bf16[2,2,24,1536]{3,2,1,0:T(8,128)(2,1)S(1)}, bf16[2,2,24,1536]{3,2,1,0:T(8,128)(2,1)S(1)}, u32[]{:S(2)}, u32[]{:S(2)}) %collective-permute-start.48) | collective-permute-done | bytes 294944 | tf_op jit(solution)/shard_map/ppermute | solution.py:177
  255.7 1.8 collective-permute-start.51
  259.5 1.8 collective-permute-start.58
  261.3 8.7 %collective-permute-done.51 = bf16[2,48,1536]{2,1,0:T(8,128)(2,1)S(1)} collective-permute-done((bf16[2,48,1536]{2,1,0:T(8,128)(2,1)S(1)}, bf16[2,48,1536]{2,1,0:T(8,128)(2,1)S(1)}, u32[]{:S(2)}, u32[]{:S(2)}) %collective-permute-start.51) | collective-permute-done | bytes 294944 | tf_op jit(solution)/shard_map/ppermute | solution.py:177
  270.2 2.9 %collective-permute-done.58 = bf16[2,192,384]{2,1,0:T(8,128)(2,1)S(1)} collective-permute-done((bf16[2,192,384]{2,1,0:T(8,128)(2,1)S(1)}, bf16[2,192,384]{2,1,0:T(8,128)(2,1)S(1)}, u32[]{:S(2)}, u32[]{:S(2)}) %collective-permute-start.58) | collective-permute-done | bytes 294944 | tf_op jit(solution)/shard_map/ppermute | solution.py:177
  273.4 1.9 collective-permute-done.52
  276.1 2.4 collective-permute-done.59
  (434 shorter events, 101.3 us)
Async XLA Ops:
  1.6 17.7 %collective-permute-start = (bf16[12,768]{1,0:T(8,128)(2,1)S(1)}, bf16[12,768]{1,0:T(8,128)(2,1)S(1)}, u32[]{:S(2)}, u32[]{:S(2)}) collective-permute-start(bf16[12,768]{1,0:T(8,128)(2,1)S(1)} %dynamic_update_slice.5), channel_id=1, source_target_pairs={{0,1},{1,0},{2,3},{3,2},{4,5},{5,4},{6,7},{7,6},{8,9},{9,8},{10,11... | collective-permute-start | bytes 55304 | tf_op jit(solution)/shard_map/ppermute | solution.py:177
  5.6 28.8 %collective-permute-start.4 = (bf16[48,1152]{1,0:T(8,128)(2,1)S(1)}, bf16[48,1152]{1,0:T(8,128)(2,1)S(1)}, u32[]{:S(2)}, u32[]{:S(2)}) collective-permute-start(bf16[48,1152]{1,0:T(8,128)(2,1)S(1)} %dynamic-slice_bitcast_fusion.11), channel_id=1, source_target_pairs={{0,4},{1,5},{2,6},{3,7},{4,0},{5,1},{6,2},{7,3},{8,12},{9,13},{10,... | collective-permute-start | bytes 331784 | tf_op jit(solution)/shard_map/ppermute | solution.py:177
  8.0 17.8 %collective-permute-start.11 = (bf16[48,384]{1,0:T(8,128)(2,1)S(1)}, bf16[48,384]{1,0:T(8,128)(2,1)S(1)}, u32[]{:S(2)}, u32[]{:S(2)}) collective-permute-start(bf16[48,384]{1,0:T(8,128)(2,1)S(1)} %dynamic-slice_bitcast_fusion.15), channel_id=1, source_target_pairs={{0,4},{1,5},{2,6},{3,7},{4,0},{5,1},{6,2},{7,3},{8,12},{9,13},{10,... | collective-permute-start | bytes 110600 | tf_op jit(solution)/shard_map/ppermute | solution.py:177
  9.4 39.3 %collective-permute-start.25 = (bf16[192,384]{1,0:T(8,128)(2,1)S(1)}, bf16[192,384]{1,0:T(8,128)(2,1)S(1)}, u32[]{:S(2)}, u32[]{:S(2)}) collective-permute-start(bf16[192,384]{1,0:T(8,128)(2,1)S(1)} %dynamic-slice_bitcast_fusion.8), channel_id=1, source_target_pairs={{0,4},{1,5},{2,6},{3,7},{4,0},{5,1},{6,2},{7,3},{8,12},{9,13},{10,... | collective-permute-start | bytes 442376 | tf_op jit(solution)/shard_map/ppermute | solution.py:177
  12.0 36.9 %collective-permute-start.18 = (bf16[48,1536]{1,0:T(8,128)(2,1)S(1)}, bf16[48,1536]{1,0:T(8,128)(2,1)S(1)}, u32[]{:S(2)}, u32[]{:S(2)}) collective-permute-start(bf16[48,1536]{1,0:T(8,128)(2,1)S(1)} %dynamic-slice_bitcast_fusion.9), channel_id=1, source_target_pairs={{0,4},{1,5},{2,6},{3,7},{4,0},{5,1},{6,2},{7,3},{8,12},{9,13},{10,... | collective-permute-start | bytes 442376 | tf_op jit(solution)/shard_map/ppermute | solution.py:177
  30.7 17.8 %collective-permute-start.12 = (bf16[2,48,384]{2,1,0:T(8,128)(2,1)S(1)}, bf16[2,48,384]{2,1,0:T(8,128)(2,1)S(1)}, u32[]{:S(2)}, u32[]{:S(2)}) collective-permute-start(bf16[2,48,384]{2,1,0:T(8,128)(2,1)S(1)} %pad_maximum_fusion.40), channel_id=1, source_target_pairs={{0,8},{1,9},{2,10},{3,11},{4,12},{5,13},{6,14},{7,15},{8,0},{9,1},... | collective-permute-start | bytes 221192 | tf_op jit(solution)/shard_map/ppermute | solution.py:177
  34.5 21.7 %collective-permute-start.5 = (bf16[2,48,1152]{2,1,0:T(8,128)(2,1)S(1)}, bf16[2,48,1152]{2,1,0:T(8,128)(2,1)S(1)}, u32[]{:S(2)}, u32[]{:S(2)}) collective-permute-start(bf16[2,48,1152]{2,1,0:T(8,128)(2,1)S(1)} %pad_maximum_fusion.36), channel_id=1, source_target_pairs={{0,8},{1,9},{2,10},{3,11},{4,12},{5,13},{6,14},{7,15},{8,0},{9,1},... | collective-permute-start | bytes 663560 | tf_op jit(solution)/shard_map/ppermute | solution.py:177
  48.6 5.5 %collective-permute-start.13 = (bf16[2,2,24,384]{3,2,1,0:T(8,128)(2,1)S(1)}, bf16[2,2,24,384]{3,2,1,0:T(8,128)(2,1)S(1)}, u32[]{:S(2)}, u32[]{:S(2)}) collective-permute-start(bf16[2,2,24,384]{3,2,1,0:T(8,128)(2,1)S(1)} %get-tuple-element.225), channel_id=1, source_target_pairs={{0,1},{1,0},{2,3},{3,2},{4,5},{5,4},{6,7},{7,6},{8,9},{9,8},{10,11... | collective-permute-start | bytes 221192 | tf_op jit(solution)/shard_map/ppermute | solution.py:177
  48.8 17.2 %collective-permute-start.26 = (bf16[2,192,384]{2,1,0:T(8,128)(2,1)S(1)}, bf16[2,192,384]{2,1,0:T(8,128)(2,1)S(1)}, u32[]{:S(2)}, u32[]{:S(2)}) collective-permute-start(bf16[2,192,384]{2,1,0:T(8,128)(2,1)S(1)} %pad_maximum_fusion.34), channel_id=1, source_target_pairs={{0,8},{1,9},{2,10},{3,11},{4,12},{5,13},{6,14},{7,15},{8,0},{9,1},... | collective-permute-start | bytes 884744 | tf_op jit(solution)/shard_map/ppermute | solution.py:177
  49.0 20.7 %collective-permute-start.19 = (bf16[2,48,1536]{2,1,0:T(8,128)(2,1)S(1)}, bf16[2,48,1536]{2,1,0:T(8,128)(2,1)S(1)}, u32[]{:S(2)}, u32[]{:S(2)}) collective-permute-start(bf16[2,48,1536]{2,1,0:T(8,128)(2,1)S(1)} %pad_maximum_fusion.33), channel_id=1, source_target_pairs={{0,8},{1,9},{2,10},{3,11},{4,12},{5,13},{6,14},{7,15},{8,0},{9,1},... | collective-permute-start | bytes 884744 | tf_op jit(solution)/shard_map/ppermute | solution.py:177
  56.3 14.0 %collective-permute-start.8 = (bf16[2,2,24,1152]{3,2,1,0:T(8,128)(2,1)S(1)}, bf16[2,2,24,1152]{3,2,1,0:T(8,128)(2,1)S(1)}, u32[]{:S(2)}, u32[]{:S(2)}) collective-permute-start(bf16[2,2,24,1152]{3,2,1,0:T(8,128)(2,1)S(1)} %get-tuple-element.202), channel_id=1, source_target_pairs={{0,2},{1,3},{2,0},{3,1},{4,6},{5,7},{6,4},{7,5},{8,10},{9,11},{10,... | collective-permute-start | bytes 663560 | tf_op jit(solution)/shard_map/ppermute | solution.py:177
  59.0 13.1 %collective-permute-start.6 = (bf16[2,2,24,1152]{3,2,1,0:T(8,128)(2,1)S(1)}, bf16[2,2,24,1152]{3,2,1,0:T(8,128)(2,1)S(1)}, u32[]{:S(2)}, u32[]{:S(2)}) collective-permute-start(bf16[2,2,24,1152]{3,2,1,0:T(8,128)(2,1)S(1)} %get-tuple-element.201), channel_id=1, source_target_pairs={{0,1},{1,0},{2,3},{3,2},{4,5},{5,4},{6,7},{7,6},{8,9},{9,8},{10,11... | collective-permute-start | bytes 663560 | tf_op jit(solution)/shard_map/ppermute | solution.py:177
  59.5 27.4 %collective-permute-start.17 = (bf16[768,384]{1,0:T(8,128)(2,1)S(1)}, bf16[768,384]{1,0:T(8,128)(2,1)S(1)}, u32[]{:S(2)}, u32[]{:S(2)}) collective-permute-start(bf16[768,384]{1,0:T(8,128)(2,1)S(1)} %bitcast.480), channel_id=1, source_target_pairs={{0,16},{16,0},{1,17},{17,1},{2,18},{18,2},{3,19},{19,3},{4,20},{20... | collective-permute-start | bytes 1769480 | tf_op jit(solution)/shard_map/ppermute | solution.py:181
  66.2 14.2 %collective-permute-start.29 = (bf16[2,2,96,384]{3,2,1,0:T(8,128)(2,1)S(1)}, bf16[2,2,96,384]{3,2,1,0:T(8,128)(2,1)S(1)}, u32[]{:S(2)}, u32[]{:S(2)}) collective-permute-start(bf16[2,2,96,384]{3,2,1,0:T(8,128)(2,1)S(1)} %get-tuple-element.191), channel_id=1, source_target_pairs={{0,2},{1,3},{2,0},{3,1},{4,6},{5,7},{6,4},{7,5},{8,10},{9,11},{10,... | collective-permute-start | bytes 884744 | tf_op jit(solution)/shard_map/ppermute | solution.py:177
  69.7 12.5 %collective-permute-start.27 = (bf16[2,2,96,384]{3,2,1,0:T(8,128)(2,1)S(1)}, bf16[2,2,96,384]{3,2,1,0:T(8,128)(2,1)S(1)}, u32[]{:S(2)}, u32[]{:S(2)}) collective-permute-start(bf16[2,2,96,384]{3,2,1,0:T(8,128)(2,1)S(1)} %get-tuple-element.190), channel_id=1, source_target_pairs={{0,1},{1,0},{2,3},{3,2},{4,5},{5,4},{6,7},{7,6},{8,9},{9,8},{10,11... | collective-permute-start | bytes 884744 | tf_op jit(solution)/shard_map/ppermute | solution.py:177
  70.4 9.0 %collective-permute-start.22 = (bf16[2,2,24,1536]{3,2,1,0:T(8,128)(2,1)S(1)}, bf16[2,2,24,1536]{3,2,1,0:T(8,128)(2,1)S(1)}, u32[]{:S(2)}, u32[]{:S(2)}) collective-permute-start(bf16[2,2,24,1536]{3,2,1,0:T(8,128)(2,1)S(1)} %get-tuple-element.183), channel_id=1, source_target_pairs={{0,2},{1,3},{2,0},{3,1},{4,6},{5,7},{6,4},{7,5},{8,10},{9,11},{10,... | collective-permute-start | bytes 884744 | tf_op jit(solution)/shard_map/ppermute | solution.py:177
  72.1 13.7 %collective-permute-start.20 = (bf16[2,2,24,1536]{3,2,1,0:T(8,128)(2,1)S(1)}, bf16[2,2,24,1536]{3,2,1,0:T(8,128)(2,1)S(1)}, u32[]{:S(2)}, u32[]{:S(2)}) collective-permute-start(bf16[2,2,24,1536]{3,2,1,0:T(8,128)(2,1)S(1)} %get-tuple-element.182), channel_id=1, source_target_pairs={{0,1},{1,0},{2,3},{3,2},{4,5},{5,4},{6,7},{7,6},{8,9},{9,8},{10,11... | collective-permute-start | bytes 884744 | tf_op jit(solution)/shard_map/ppermute | solution.py:177
  79.4 15.9 %collective-permute-start.9 = (bf16[2,2,2,24,1152]{4,3,2,1,0:T(8,128)(2,1)S(1)}, bf16[2,2,2,24,1152]{4,3,2,1,0:T(8,128)(2,1)S(1)}, u32[]{:S(2)}, u32[]{:S(2)}) collective-permute-start(bf16[2,2,2,24,1152]{4,3,2,1,0:T(8,128)(2,1)S(1)} %pad_maximum_fusion.29), channel_id=1, source_target_pairs={{0,1},{1,0},{2,3},{3,2},{4,5},{5,4},{6,7},{7,6},{8,9},{9,8},{10,11... | collective-permute-start | bytes 1327112 | tf_op jit(solution)/shard_map/ppermute | solution.py:177
  80.4 15.9 %collective-permute-start.7 = (bf16[2,2,2,24,1152]{4,3,1,0,2:T(8,128)(2,1)S(1)}, bf16[2,2,2,24,1152]{4,3,1,0,2:T(8,128)(2,1)S(1)}, u32[]{:S(2)}, u32[]{:S(2)}) collective-permute-start(bf16[2,2,2,24,1152]{4,3,1,0,2:T(8,128)(2,1)S(1)} %pad_maximum_fusion.28), channel_id=1, source_target_pairs={{0,2},{1,3},{2,0},{3,1},{4,6},{5,7},{6,4},{7,5},{8,10},{9,11},{10,... | collective-permute-start | bytes 1327112 | tf_op jit(solution)/shard_map/ppermute | solution.py:177
  82.3 25.6 %collective-permute-start.30 = (bf16[2,2,2,96,384]{4,3,2,1,0:T(8,128)(2,1)S(1)}, bf16[2,2,2,96,384]{4,3,2,1,0:T(8,128)(2,1)S(1)}, u32[]{:S(2)}, u32[]{:S(2)}) collective-permute-start(bf16[2,2,2,96,384]{4,3,2,1,0:T(8,128)(2,1)S(1)} %pad_maximum_fusion.26), channel_id=1, source_target_pairs={{0,1},{1,0},{2,3},{3,2},{4,5},{5,4},{6,7},{7,6},{8,9},{9,8},{10,11... | collective-permute-start | bytes 1769480 | tf_op jit(solution)/shard_map/ppermute | solution.py:177
  85.7 22.3 %collective-permute-start.28 = (bf16[2,2,2,96,384]{4,3,1,0,2:T(8,128)(2,1)S(1)}, bf16[2,2,2,96,384]{4,3,1,0,2:T(8,128)(2,1)S(1)}, u32[]{:S(2)}, u32[]{:S(2)}) collective-permute-start(bf16[2,2,2,96,384]{4,3,1,0,2:T(8,128)(2,1)S(1)} %pad_maximum_fusion.25), channel_id=1, source_target_pairs={{0,2},{1,3},{2,0},{3,1},{4,6},{5,7},{6,4},{7,5},{8,10},{9,11},{10,... | collective-permute-start | bytes 1769480 | tf_op jit(solution)/shard_map/ppermute | solution.py:177
  86.9 30.2 %collective-permute-start.23 = (bf16[2,2,2,24,1536]{4,3,2,1,0:T(8,128)(2,1)S(1)}, bf16[2,2,2,24,1536]{4,3,2,1,0:T(8,128)(2,1)S(1)}, u32[]{:S(2)}, u32[]{:S(2)}) collective-permute-start(bf16[2,2,2,24,1536]{4,3,2,1,0:T(8,128)(2,1)S(1)} %pad_maximum_fusion.24), channel_id=1, source_target_pairs={{0,1},{1,0},{2,3},{3,2},{4,5},{5,4},{6,7},{7,6},{8,9},{9,8},{10,11... | collective-permute-start | bytes 1769480 | tf_op jit(solution)/shard_map/ppermute | solution.py:177
  95.2 22.0 %collective-permute-start.21 = (bf16[2,2,2,24,1536]{4,3,1,0,2:T(8,128)(2,1)S(1)}, bf16[2,2,2,24,1536]{4,3,1,0,2:T(8,128)(2,1)S(1)}, u32[]{:S(2)}, u32[]{:S(2)}) collective-permute-start(bf16[2,2,2,24,1536]{4,3,1,0,2:T(8,128)(2,1)S(1)} %pad_maximum_fusion.23), channel_id=1, source_target_pairs={{0,2},{1,3},{2,0},{3,1},{4,6},{5,7},{6,4},{7,5},{8,10},{9,11},{10,... | collective-permute-start | bytes 1769480 | tf_op jit(solution)/shard_map/ppermute | solution.py:177
  96.6 22.4 %collective-permute-start.10 = (bf16[768,1152]{1,0:T(8,128)(2,1)S(1)}, bf16[768,1152]{1,0:T(8,128)(2,1)S(1)}, u32[]{:S(2)}, u32[]{:S(2)}) collective-permute-start(bf16[768,1152]{1,0:T(8,128)(2,1)S(1)} %bitcast.478), channel_id=1, source_target_pairs={{0,16},{16,0},{1,17},{17,1},{2,18},{18,2},{3,19},{19,3},{4,20},{20... | collective-permute-start | bytes 5308424 | tf_op jit(solution)/shard_map/ppermute | solution.py:181
  108.5 23.0 %collective-permute-start.31 = (bf16[3072,384]{1,0:T(8,128)(2,1)S(1)}, bf16[3072,384]{1,0:T(8,128)(2,1)}, u32[]{:S(2)}, u32[]{:S(2)}) collective-permute-start(bf16[3072,384]{1,0:T(8,128)(2,1)S(1)} %bitcast.477), channel_id=1, source_target_pairs={{0,16},{16,0},{1,17},{17,1},{2,18},{18,2},{3,19},{19,3},{4,20},{20... | collective-permute-start | bytes 7077896 | tf_op jit(solution)/shard_map/ppermute | solution.py:181
  119.0 8.9 %collective-permute-start.24 = (bf16[768,1536]{1,0:T(8,128)(2,1)}, bf16[768,1536]{1,0:T(8,128)(2,1)}, u32[]{:S(2)}, u32[]{:S(2)}) collective-permute-start(bf16[768,1536]{1,0:T(8,128)(2,1)} %bitcast.57), channel_id=1, source_target_pairs={{0,16},{16,0},{1,17},{17,1},{2,18},{18,2},{3,19},{19,3},{4,20},{20... | collective-permute-start | bytes 7077896 | tf_op jit(solution)/shard_map/ppermute | solution.py:181
  163.9 39.8 %collective-permute-start.32 = (bf16[768,1152]{1,0:T(8,128)(2,1)S(1)}, bf16[768,1152]{1,0:T(8,128)(2,1)S(1)}, u32[]{:S(2)}, u32[]{:S(2)}) collective-permute-start(bf16[768,1152]{1,0:T(8,128)(2,1)S(1)} %constant_dynamic-slice_fusion.21), channel_id=1, source_target_pairs={{0,16},{16,0},{1,17},{17,1},{2,18},{18,2},{3,19},{19,3},{4,20},{20... | collective-permute-start | bytes 5308424 | tf_op jit(solution)/shard_map/ppermute | solution.py:181
  168.4 13.5 %collective-permute-start.39 = (bf16[768,384]{1,0:T(8,128)(2,1)S(1)}, bf16[768,384]{1,0:T(8,128)(2,1)S(1)}, u32[]{:S(2)}, u32[]{:S(2)}) collective-permute-start(bf16[768,384]{1,0:T(8,128)(2,1)S(1)} %constant_dynamic-slice_fusion.16), channel_id=1, source_target_pairs={{0,16},{16,0},{1,17},{17,1},{2,18},{18,2},{3,19},{19,3},{4,20},{20... | collective-permute-start | bytes 1769480 | tf_op jit(solution)/shard_map/ppermute | solution.py:181
  175.8 44.2 %collective-permute-start.46 = (bf16[768,1536]{1,0:T(8,128)(2,1)S(1)}, bf16[768,1536]{1,0:T(8,128)(2,1)S(1)}, u32[]{:S(2)}, u32[]{:S(2)}) collective-permute-start(bf16[768,1536]{1,0:T(8,128)(2,1)S(1)} %constant_dynamic-slice_fusion.11), channel_id=1, source_target_pairs={{0,16},{16,0},{1,17},{17,1},{2,18},{18,2},{3,19},{19,3},{4,20},{20... | collective-permute-start | bytes 7077896 | tf_op jit(solution)/shard_map/ppermute | solution.py:181
  176.0 5.7 %collective-permute-start.64 = (f32[12,768]{1,0:T(8,128)S(1)}, f32[12,768]{1,0:T(8,128)S(1)}, u32[]{:S(2)}, u32[]{:S(2)}) collective-permute-start(f32[12,768]{1,0:T(8,128)S(1)} %add.514), channel_id=1, source_target_pairs={{0,8},{1,9},{2,10},{3,11},{4,12},{5,13},{6,14},{7,15},{8,0},{9,1},... | collective-permute-start | bytes 110600 | tf_op jit(solution)/shard_map/ppermute | solution.py:177
  179.7 44.0 %collective-permute-start.53 = (bf16[3072,384]{1,0:T(8,128)(2,1)S(1)}, bf16[3072,384]{1,0:T(8,128)(2,1)S(1)}, u32[]{:S(2)}, u32[]{:S(2)}) collective-permute-start(bf16[3072,384]{1,0:T(8,128)(2,1)S(1)} %constant_dynamic-slice_fusion.6), channel_id=1, source_target_pairs={{0,16},{16,0},{1,17},{17,1},{2,18},{18,2},{3,19},{19,3},{4,20},{20... | collective-permute-start | bytes 7077896 | tf_op jit(solution)/shard_map/ppermute | solution.py:181
  182.5 5.7 %collective-permute-start.40 = (bf16[2,2,2,24,384]{4,3,1,0,2:T(8,128)(2,1)S(1)}, bf16[2,2,2,24,384]{4,3,1,0,2:T(8,128)(2,1)S(1)}, u32[]{:S(2)}, u32[]{:S(2)}) collective-permute-start(bf16[2,2,2,24,384]{4,3,1,0,2:T(8,128)(2,1)S(1)} %bitcast.511), channel_id=1, source_target_pairs={{0,2},{1,3},{2,0},{3,1},{4,6},{5,7},{6,4},{7,5},{8,10},{9,11},{10,... | collective-permute-start | bytes 442376 | tf_op jit(solution)/shard_map/ppermute | solution.py:177
  183.3 5.7 %collective-permute-start.42 = (bf16[2,2,2,24,384]{4,3,1,0,2:T(8,128)(2,1)S(1)}, bf16[2,2,2,24,384]{4,3,1,0,2:T(8,128)(2,1)S(1)}, u32[]{:S(2)}, u32[]{:S(2)}) collective-permute-start(bf16[2,2,2,24,384]{4,3,1,0,2:T(8,128)(2,1)S(1)} %bitcast.512), channel_id=1, source_target_pairs={{0,1},{1,0},{2,3},{3,2},{4,5},{5,4},{6,7},{7,6},{8,9},{9,8},{10,11... | collective-permute-start | bytes 442376 | tf_op jit(solution)/shard_map/ppermute | solution.py:177
  204.6 9.0 %collective-permute-start.33 = (bf16[2,2,2,24,1152]{4,3,1,0,2:T(8,128)(2,1)S(1)}, bf16[2,2,2,24,1152]{4,3,1,0,2:T(8,128)(2,1)S(1)}, u32[]{:S(2)}, u32[]{:S(2)}) collective-permute-start(bf16[2,2,2,24,1152]{4,3,1,0,2:T(8,128)(2,1)S(1)} %bitcast.507), channel_id=1, source_target_pairs={{0,2},{1,3},{2,0},{3,1},{4,6},{5,7},{6,4},{7,5},{8,10},{9,11},{10,... | collective-permute-start | bytes 1327112 | tf_op jit(solution)/shard_map/ppermute | solution.py:177
  207.5 12.2 %collective-permute-start.35 = (bf16[2,2,2,24,1152]{4,3,1,0,2:T(8,128)(2,1)S(1)}, bf16[2,2,2,24,1152]{4,3,1,0,2:T(8,128)(2,1)S(1)}, u32[]{:S(2)}, u32[]{:S(2)}) collective-permute-start(bf16[2,2,2,24,1152]{4,3,1,0,2:T(8,128)(2,1)S(1)} %bitcast.508), channel_id=1, source_target_pairs={{0,1},{1,0},{2,3},{3,2},{4,5},{5,4},{6,7},{7,6},{8,9},{9,8},{10,11... | collective-permute-start | bytes 1327112 | tf_op jit(solution)/shard_map/ppermute | solution.py:177
  213.7 10.8 %collective-permute-start.34 = (bf16[2,2,24,1152]{3,2,1,0:T(8,128)(2,1)S(1)}, bf16[2,2,24,1152]{3,2,1,0:T(8,128)(2,1)S(1)}, u32[]{:S(2)}, u32[]{:S(2)}) collective-permute-start(bf16[2,2,24,1152]{3,2,1,0:T(8,128)(2,1)S(1)} %dynamic-slice_bitcast_fusion.5), channel_id=1, source_target_pairs={{0,1},{1,0},{2,3},{3,2},{4,5},{5,4},{6,7},{7,6},{8,9},{9,8},{10,11... | collective-permute-start | bytes 663560 | tf_op jit(solution)/shard_map/ppermute | solution.py:177
  219.9 8.4 %collective-permute-start.36 = (bf16[2,2,24,1152]{3,2,1,0:T(8,128)(2,1)S(1)}, bf16[2,2,24,1152]{3,2,1,0:T(8,128)(2,1)S(1)}, u32[]{:S(2)}, u32[]{:S(2)}) collective-permute-start(bf16[2,2,24,1152]{3,2,1,0:T(8,128)(2,1)S(1)} %dynamic-slice_bitcast_fusion.4), channel_id=1, source_target_pairs={{0,2},{1,3},{2,0},{3,1},{4,6},{5,7},{6,4},{7,5},{8,10},{9,11},{10,... | collective-permute-start | bytes 663560 | tf_op jit(solution)/shard_map/ppermute | solution.py:177
  221.2 23.1 %collective-permute-start.47 = (bf16[2,2,2,24,1536]{4,3,1,0,2:T(8,128)(2,1)S(1)}, bf16[2,2,2,24,1536]{4,3,1,0,2:T(8,128)(2,1)S(1)}, u32[]{:S(2)}, u32[]{:S(2)}) collective-permute-start(bf16[2,2,2,24,1536]{4,3,1,0,2:T(8,128)(2,1)S(1)} %bitcast.504), channel_id=1, source_target_pairs={{0,2},{1,3},{2,0},{3,1},{4,6},{5,7},{6,4},{7,5},{8,10},{9,11},{10,... | collective-permute-start | bytes 1769480 | tf_op jit(solution)/shard_map/ppermute | solution.py:177
  223.4 21.3 %collective-permute-start.49 = (bf16[2,2,2,24,1536]{4,3,1,0,2:T(8,128)(2,1)S(1)}, bf16[2,2,2,24,1536]{4,3,1,0,2:T(8,128)(2,1)S(1)}, u32[]{:S(2)}, u32[]{:S(2)}) collective-permute-start(bf16[2,2,2,24,1536]{4,3,1,0,2:T(8,128)(2,1)S(1)} %bitcast.503), channel_id=1, source_target_pairs={{0,1},{1,0},{2,3},{3,2},{4,5},{5,4},{6,7},{7,6},{8,9},{9,8},{10,11... | collective-permute-start | bytes 1769480 | tf_op jit(solution)/shard_map/ppermute | solution.py:177
  228.4 9.3 %collective-permute-start.37 = (bf16[2,48,1152]{2,1,0:T(8,128)(2,1)S(1)}, bf16[2,48,1152]{2,1,0:T(8,128)(2,1)S(1)}, u32[]{:S(2)}, u32[]{:S(2)}) collective-permute-start(bf16[2,48,1152]{2,1,0:T(8,128)(2,1)S(1)} %fusion.72), channel_id=1, source_target_pairs={{0,8},{1,9},{2,10},{3,11},{4,12},{5,13},{6,14},{7,15},{8,0},{9,1},... | collective-permute-start | bytes 663560 | tf_op jit(solution)/shard_map/ppermute | solution.py:177
  230.8 19.1 %collective-permute-start.54 = (bf16[2,2,2,96,384]{4,3,1,0,2:T(8,128)(2,1)S(1)}, bf16[2,2,2,96,384]{4,3,1,0,2:T(8,128)(2,1)S(1)}, u32[]{:S(2)}, u32[]{:S(2)}) collective-permute-start(bf16[2,2,2,96,384]{4,3,1,0,2:T(8,128)(2,1)S(1)} %bitcast.505), channel_id=1, source_target_pairs={{0,2},{1,3},{2,0},{3,1},{4,6},{5,7},{6,4},{7,5},{8,10},{9,11},{10,... | collective-permute-start | bytes 1769480 | tf_op jit(solution)/shard_map/ppermute | solution.py:177
  238.1 14.2 %collective-permute-start.56 = (bf16[2,2,2,96,384]{4,3,1,0,2:T(8,128)(2,1)S(1)}, bf16[2,2,2,96,384]{4,3,1,0,2:T(8,128)(2,1)S(1)}, u32[]{:S(2)}, u32[]{:S(2)}) collective-permute-start(bf16[2,2,2,96,384]{4,3,1,0,2:T(8,128)(2,1)S(1)} %bitcast.506), channel_id=1, source_target_pairs={{0,1},{1,0},{2,3},{3,2},{4,5},{5,4},{6,7},{7,6},{8,9},{9,8},{10,11... | collective-permute-start | bytes 1769480 | tf_op jit(solution)/shard_map/ppermute | solution.py:177
  244.5 11.0 %collective-permute-start.48 = (bf16[2,2,24,1536]{3,2,1,0:T(8,128)(2,1)S(1)}, bf16[2,2,24,1536]{3,2,1,0:T(8,128)(2,1)S(1)}, u32[]{:S(2)}, u32[]{:S(2)}) collective-permute-start(bf16[2,2,24,1536]{3,2,1,0:T(8,128)(2,1)S(1)} %dynamic-slice_bitcast_fusion.3), channel_id=1, source_target_pairs={{0,1},{1,0},{2,3},{3,2},{4,5},{5,4},{6,7},{7,6},{8,9},{9,8},{10,11... | collective-permute-start | bytes 884744 | tf_op jit(solution)/shard_map/ppermute | solution.py:177
  245.0 10.6 %collective-permute-start.50 = (bf16[2,2,24,1536]{3,2,1,0:T(8,128)(2,1)S(1)}, bf16[2,2,24,1536]{3,2,1,0:T(8,128)(2,1)S(1)}, u32[]{:S(2)}, u32[]{:S(2)}) collective-permute-start(bf16[2,2,24,1536]{3,2,1,0:T(8,128)(2,1)S(1)} %dynamic-slice_bitcast_fusion.2), channel_id=1, source_target_pairs={{0,2},{1,3},{2,0},{3,1},{4,6},{5,7},{6,4},{7,5},{8,10},{9,11},{10,... | collective-permute-start | bytes 884744 | tf_op jit(solution)/shard_map/ppermute | solution.py:177
  250.1 8.5 %collective-permute-start.55 = (bf16[2,2,96,384]{3,2,1,0:T(8,128)(2,1)S(1)}, bf16[2,2,96,384]{3,2,1,0:T(8,128)(2,1)S(1)}, u32[]{:S(2)}, u32[]{:S(2)}) collective-permute-start(bf16[2,2,96,384]{3,2,1,0:T(8,128)(2,1)S(1)} %dynamic-slice_bitcast_fusion.1), channel_id=1, source_target_pairs={{0,1},{1,0},{2,3},{3,2},{4,5},{5,4},{6,7},{7,6},{8,9},{9,8},{10,11... | collective-permute-start | bytes 884744 | tf_op jit(solution)/shard_map/ppermute | solution.py:177
  252.5 6.8 %collective-permute-start.57 = (bf16[2,2,96,384]{3,2,1,0:T(8,128)(2,1)S(1)}, bf16[2,2,96,384]{3,2,1,0:T(8,128)(2,1)S(1)}, u32[]{:S(2)}, u32[]{:S(2)}) collective-permute-start(bf16[2,2,96,384]{3,2,1,0:T(8,128)(2,1)S(1)} %dynamic-slice_bitcast_fusion), channel_id=1, source_target_pairs={{0,2},{1,3},{2,0},{3,1},{4,6},{5,7},{6,4},{7,5},{8,10},{9,11},{10,... | collective-permute-start | bytes 884744 | tf_op jit(solution)/shard_map/ppermute | solution.py:177
  255.7 14.2 %collective-permute-start.51 = (bf16[2,48,1536]{2,1,0:T(8,128)(2,1)S(1)}, bf16[2,48,1536]{2,1,0:T(8,128)(2,1)S(1)}, u32[]{:S(2)}, u32[]{:S(2)}) collective-permute-start(bf16[2,48,1536]{2,1,0:T(8,128)(2,1)S(1)} %fusion.59), channel_id=1, source_target_pairs={{0,8},{1,9},{2,10},{3,11},{4,12},{5,13},{6,14},{7,15},{8,0},{9,1},... | collective-permute-start | bytes 884744 | tf_op jit(solution)/shard_map/ppermute | solution.py:177
  259.5 13.6 %collective-permute-start.58 = (bf16[2,192,384]{2,1,0:T(8,128)(2,1)S(1)}, bf16[2,192,384]{2,1,0:T(8,128)(2,1)S(1)}, u32[]{:S(2)}, u32[]{:S(2)}) collective-permute-start(bf16[2,192,384]{2,1,0:T(8,128)(2,1)S(1)} %fusion.55), channel_id=1, source_target_pairs={{0,8},{1,9},{2,10},{3,11},{4,12},{5,13},{6,14},{7,15},{8,0},{9,1},... | collective-permute-start | bytes 884744 | tf_op jit(solution)/shard_map/ppermute | solution.py:177
  (88 other events, 789.1 us)

commit v2 on v0

v2 whole, which is shorter than its diff:
```python
import jax
import jax.numpy as jnp
from jax import lax
from jax.experimental import pallas as pl
from jax.experimental.pallas import tpu as pltpu
from jax.sharding import PartitionSpec as P

HEAD_DIM = 64
STEP_COUNT = 3


beta_one = 0.5
beta_two = 0.5
learning_rate = 0.02
small_rate = 0.25
weight_decay = 0.1
epsilon = 1e-08
norm_epsilon = 1e-05
curve = 0.7978845608028654
cubic = 0.044715
half_type = jnp.bfloat16
wide = jnp.float32


def matmul(left, right):
    return lax.dot_general(left, right, (((1,), (0,)), ((), ())), preferred_element_type=wide)


def outer_sum(left, right):
    return lax.dot_general(left, right, (((0,), (0,)), ((), ())), preferred_element_type=wide)


def times_back(left, right):
    return lax.dot_general(left, right, (((1,), (1,)), ((), ())), preferred_element_type=wide)


def norm_parts(stream):
    centred = stream - jnp.mean(stream, axis=-1, keepdims=True)
    spread = jnp.mean(centred * centred, axis=-1, keepdims=True)
    scale = lax.rsqrt(spread + norm_epsilon)
    return centred * scale, scale


def norm_back(unit, scale, gain, upstream):
    inner = upstream * gain
    mean_inner = jnp.mean(inner, axis=-1, keepdims=True)
    mean_cross = jnp.mean(inner * unit, axis=-1, keepdims=True)
    return scale * (inner - mean_inner - unit * mean_cross)


def after(value, *others):
    return lax.optimization_barrier((value, *others))[0]


class Grid:
    def __init__(self):
        self.size = lax.axis_size("fsdp")
        self.index = lax.axis_index("fsdp")
        self.core = lax.axis_index("dp")
        bits = self.size.bit_length() - 1
        side = bits // 3
        x_bits = tuple(range(side))
        y_bits = tuple(range(side, 2 * side))
        self.orders = (x_bits + y_bits, y_bits + x_bits)
        self.steps = 2 * side
        self.low_bits = tuple(range(2 * side, bits - 1))
        self.top_bit = bits - 1
        self.top = self.index >> self.top_bit

    def swap(self, value, bit):
        return lax.ppermute(value, "fsdp", [(i, i ^ (1 << bit)) for i in range(self.size)])

    def swap_step(self, value, step):
        pairs = []
        for core in range(2):
            bit = self.orders[core][step]
            for i in range(self.size):
                pairs.append((core * self.size + i, core * self.size + (i ^ (1 << bit))))
        return lax.ppermute(value, ("dp", "fsdp"), pairs)

    def swap_core(self, value):
        return lax.ppermute(value, "dp", [(0, 1), (1, 0)])

    def swap_owned(self, value, bit, owned):
        pairs = []
        for core in range(2):
            for i in range(self.size):
                if ((i >> self.top_bit) == core) == owned:
                    pairs.append((core * self.size + i, core * self.size + (i ^ (1 << bit))))
        return lax.ppermute(value, ("dp", "fsdp"), pairs)

    def flip_step(self, rels, step):
        masks = [1 << self.orders[core][step] for core in range(2)]
        return tuple((rel[0] ^ masks[0], rel[1] ^ masks[1]) for rel in rels)


def flip_bit(rels, bit):
    return tuple((rel[0] ^ (1 << bit), rel[1] ^ (1 << bit)) for rel in rels)


class Gather:
    def __init__(self, grid, block, owned):
        self.grid, self.owned = grid, owned
        self.value, self.rels = block[None], ((0, 0),)
        self.done, self.last = [], None

    def high(self):
        grid = self.grid
        if self.owned:
            got = grid.swap_owned(self.value, grid.top_bit, True)
            self.value = jnp.where(grid.top == grid.core, self.value, got)
        else:
            got = grid.swap(self.value, grid.top_bit)
            self.value = jnp.concatenate([self.value, got], axis=0)
            self.rels = self.rels + flip_bit(self.rels, grid.top_bit)

    def low(self, apart):
        grid = self.grid
        self.start = [(self.rels, self.value)]
        for bit in grid.low_bits:
            self.start += [
                (flip_bit(rels, bit), grid.swap(value, bit)) for rels, value in self.start
            ]
        if not apart:
            rels = sum((rels for rels, _ in self.start), ())
            self.start = [(rels, jnp.concatenate([value for _, value in self.start], axis=0))]

    def first(self, which):
        grid = self.grid
        rels, value = self.start[which]
        one = (grid.flip_step(rels, 0), grid.swap_step(value, 0))
        middle = grid.steps // 2
        two = (grid.flip_step(rels, middle), grid.swap_step(value, middle))
        return [(rels, value), one], two

    def second(self, state):
        grid = self.grid
        pieces, early = state
        middle = grid.steps // 2
        for step in range(1, grid.steps):
            new = []
            for place, (rels, value) in enumerate(pieces):
                if step == middle and place == 0:
                    new.append(early)
                else:
                    new.append((grid.flip_step(rels, step), grid.swap_step(value, step)))
            pieces = pieces + new
        return pieces


def pick(rel, core):
    return jnp.where(core == 0, rel[0], rel[1])


def assemble(grid, pieces, count):
    rows, width = pieces[0][1].shape[1:]
    whole = jnp.zeros((count, rows, width), pieces[0][1].dtype)
    for rels, piece in pieces:
        for place, rel in enumerate(rels):
            spot = (grid.index ^ pick(rel, grid.core)) & (count - 1)
            whole = lax.dynamic_update_slice(whole, piece[place : place + 1], (spot, 0, 0))
    return whole.reshape(count * rows, width)


def sum_all(grid, value):
    value = value + grid.swap_core(value)
    for bit in range(grid.top_bit + 1):
        value = value + grid.swap(value, bit)
    return value


def adamw(master, first, second, gradient, rate):
    first_new = beta_one * first + (1.0 - beta_one) * gradient
    second_new = beta_two * second + (1.0 - beta_two) * gradient * gradient
    first_hat = first_new / (1.0 - beta_one**STEP_COUNT)
    second_hat = second_new / (1.0 - beta_two**STEP_COUNT)
    master_new = master - rate * (
        first_hat / (jnp.sqrt(second_hat) + epsilon) + weight_decay * master
    )
    return (master_new, first_new, second_new, master_new.astype(jnp.bfloat16))


RAW, HELD, FETCH, PUT, SCALAR = "raw", "held", "fetch", "put", "scalar"
SPACES = {RAW: pltpu.HBM, HELD: pltpu.VMEM, FETCH: pltpu.HBM, PUT: pltpu.HBM, SCALAR: pltpu.SMEM}


def shaped(shape, dtype):
    return jax.ShapeDtypeStruct(shape, dtype)


class Fetched:
    def __init__(self, copy, room):
        self.copy, self.room, self.waited = copy, room, False

    def ready(self):
        if not self.waited:
            self.copy.wait()
            self.waited = True
        return self.room


def call(body, name, operands, kinds, outs, out_kinds, scratch):
    moved = [o for o, kind in zip(operands, kinds) if kind == FETCH]
    moved += [o for o, kind in zip(outs, out_kinds) if kind == PUT]
    rooms = [pltpu.VMEM(o.shape, o.dtype) for o in moved]
    scratch = list(scratch)

    def whole(*refs):
        ins = refs[: len(operands)]
        results = refs[len(operands) : len(operands) + len(outs)]
        own = refs[len(operands) + len(outs) :]
        own, rest = own[: len(scratch)], own[len(scratch) :]
        room = list(rest[: len(moved)])
        sems = rest[len(moved)] if moved else None
        taken, arrived, written, puts = 0, [], [], []
        for ref, kind in zip(ins, kinds):
            if kind == FETCH:
                copy = pltpu.make_async_copy(ref, room[taken], sems.at[taken])
                copy.start()
                arrived.append(Fetched(copy, room[taken]))
                taken += 1
            else:
                arrived.append(ref)
        for ref, kind in zip(results, out_kinds):
            if kind == PUT:
                puts.append(pltpu.make_async_copy(room[taken], ref, sems.at[taken]))
                written.append(room[taken])
                taken += 1
            else:
                written.append(ref)
        body(*arrived, *written, *own)
        for ref in arrived:
            if isinstance(ref, Fetched):
                ref.ready()
        start_all(puts)
        wait_all(puts)

    return pl.pallas_call(
        whole,
        name=name,
        out_shape=tuple(outs),
        in_specs=[pl.BlockSpec(memory_space=SPACES[kind]) for kind in kinds],
        out_specs=tuple(pl.BlockSpec(memory_space=SPACES[kind]) for kind in out_kinds),
        scratch_shapes=scratch
        + rooms
        + ([pltpu.SemaphoreType.DMA((len(moved),))] if moved else []),
        compiler_params=pltpu.CompilerParams(vmem_limit_bytes=(60 if name == "pack_blocks" else 48) << 20),
        cost_estimate=pl.CostEstimate(flops=int({'pack_blocks': 1.5, 'attend': 4.3, 'grow': 9.5, 'shrink_back': 6.4, 'expand_grads': 4.3, 'attend_back': 8.1, 'joint_back': 2.9, 'finish': 2.6}[name] * 1150000000), bytes_accessed=1, transcendentals=0),
    )(*operands)


class Layout:
    def __init__(self, count, rows, width):
        self.count, self.rows, self.width = count, rows, width
        self.direct = rows % 16 == 0

    def offset(self, index, core, rel):
        if rel[0] == rel[1]:
            spot = (index ^ rel[0]) & (self.count - 1)
        else:
            spot = (index ^ jnp.where(core == 0, rel[0], rel[1])) & (self.count - 1)
        return pl.multiple_of(spot * self.rows, 16)


class Loading:
    def __init__(self, pieces, refs, meta_ref, scratch):
        self.pieces, self.meta = pieces, meta_ref
        self.whole, self.room, self.sems = scratch
        self.copies, at = [], 0
        for place, ref in enumerate(refs):
            target = self.whole
            if pieces.rel_sets is not None:
                target = self.room.at[pl.ds(at, ref.shape[0])]
                at += ref.shape[0]
            self.copies.append(pltpu.make_async_copy(ref, target, self.sems.at[place]))
        start_all(self.copies)

    def ready(self):
        wait_all(self.copies)
        layout = self.pieces.layout
        if self.pieces.rel_sets is not None:
            rels = sum(self.pieces.rel_sets, ())
            for place, rel in enumerate(rels):
                spot = layout.offset(self.meta[0], self.meta[1], rel)
                self.whole[pl.ds(spot, layout.rows)] = self.room[place]
        return self.whole


class Storing:
    def __init__(self, parts, refs, meta_ref, scratch):
        self.parts, self.refs, self.meta = parts, refs, meta_ref
        self.room, self.sems = scratch
        self.copies = []

    def put(self, start, columns, value):
        layout = self.parts.layout
        value = value.astype(half_type)
        if not layout.direct:
            self.room[start : start + value.shape[0], columns] = value
            return
        for at in range(0, value.shape[0], layout.rows):
            place = self.parts.place((start + at) // layout.rows, self.meta)
            self.room[place, :, columns] = value[at : at + layout.rows]

    def send(self):
        if not self.parts.layout.direct:
            self.copies = [pltpu.make_async_copy(self.room, self.refs[0], self.sems.at[0])]
        else:
            quarter = self.parts.layout.count // 4
            starts = (2 * quarter, quarter, 0)
            self.copies = [
                pltpu.make_async_copy(
                    self.room.at[pl.ds(at, ref.shape[0])], ref, self.sems.at[place]
                )
                for place, (ref, at) in enumerate(zip(self.refs, starts))
            ]
        start_all(self.copies)

    def wait(self):
        wait_all(self.copies)


def start_all(copies):
    for copy in copies:
        copy.start()


def wait_all(copies):
    for copy in copies:
        copy.wait()


class Pieces:
    def __init__(self, grid, pieces, count):
        rows, width = pieces[0][1].shape[1:]
        self.layout = Layout(count, rows, width)
        if self.layout.direct:
            self.rel_sets = [rels for rels, _ in pieces]
            self.arrays = [piece for _, piece in pieces]
        else:
            self.rel_sets = None
            self.arrays = [assemble(grid, pieces, count)]

    def scratch(self):
        count, rows, width = self.layout.count, self.layout.rows, self.layout.width
        room = (count, rows, width) if self.rel_sets is not None else (1, 16, 128)
        return [
            pltpu.VMEM((count * rows, width), half_type),
            pltpu.VMEM(room, half_type),
            pltpu.SemaphoreType.DMA((len(self.arrays),)),
        ]


class Parts:
    def __init__(self, grid, layout, lasting):
        self.grid, self.layout = grid, layout
        count = layout.count
        self.bits = bits = [[*grid.orders[core], *lasting] for core in range(2)]
        rels = []
        for place in range(count):
            taken = [(place >> at) & 1 for at in range(len(bits[0]))][::-1]
            rels.append(
                tuple(
                    sum(1 << bit for bit, take in zip(bits[core], taken) if take)
                    for core in range(2)
                )
            )
        self.rels = tuple(rels)
        quarter = count // 4
        self.rel_sets = [rels[2 * quarter :], rels[quarter : 2 * quarter], rels[:quarter]]

    def shapes(self):
        rows, width = self.layout.rows, self.layout.width
        if self.layout.direct:
            return [shaped((len(rels), rows, width), half_type) for rels in self.rel_sets]
        return [shaped((self.layout.count * rows, width), half_type)]

    def scratch(self):
        count, rows, width = self.layout.count, self.layout.rows, self.layout.width
        shape = (count, rows, width) if self.layout.direct else (count * rows, width)
        return [pltpu.VMEM(shape, half_type), pltpu.SemaphoreType.DMA((3,))]

    def place(self, block, meta_ref):
        rel = (meta_ref[0] ^ block) & (self.layout.count - 1)
        spots = []
        for order in self.bits:
            last = len(order) - 1
            spots.append(sum(((rel >> bit) & 1) << (last - at) for at, bit in enumerate(order)))
        return jnp.where(meta_ref[1] == 0, spots[0], spots[1])

    def split_up(self, arrays):
        if self.layout.direct:
            return arrays
        grid, count = self.grid, self.layout.count
        blocks = arrays[0].reshape(count, self.layout.rows, self.layout.width)
        order = jnp.stack([(grid.index ^ pick(rel, grid.core)) & (count - 1) for rel in self.rels])
        blocks = jnp.take(blocks, order, axis=0, mode="clip")
        return blocks[count // 2 :], blocks[count // 4 : count // 2], blocks[: count // 4]

    def first(self, arrays):
        send, next_send, keep = self.split_up(arrays)
        got = self.grid.swap_step(send, 0)
        middle = got.shape[0] // 2
        return join(next_send, got[middle:]), join(keep, got[:middle])

    def second(self, state):
        send, keep = state
        for step in range(1, self.grid.steps):
            got = self.grid.swap_step(send, step)
            if step == self.grid.steps - 1:
                return keep, got
            middle = keep.shape[0] // 2
            send, keep = join(keep[middle:], got[middle:]), join(keep[:middle], got[:middle])


def join(keep, got):
    return (keep.astype(wide) + got.astype(wide)).astype(half_type)


def third_sum(grid, keep, got, owned=False):
    near, far = keep, got
    for bit in grid.low_bits[::-1]:
        middle = near.shape[0] // 2
        send, near = join(near[middle:], far[middle:]), join(near[:middle], far[:middle])
        far = grid.swap(send, bit)
    if owned:
        last = grid.swap_owned(join(near, far), grid.top_bit, False)
    else:
        middle = near.shape[0] // 2
        last = grid.swap(join(near[middle:], far[middle:]), grid.top_bit)
        near, far = near[:middle], far[:middle]
    return (near.astype(wide) + far.astype(wide) + last.astype(wide))[0]


def pack_blocks(meta, lengths, tokens, cot, joint, output, expand, gains, biases):
    rows = joint.shape[0]
    count, width = tokens.shape
    half = width // 2
    hidden = expand.shape[1] // 2
    small = gains.shape[0] + biases.shape[0]

    def body(meta_ref, lengths_ref, tokens_ref, cot_ref, joint_ref, output_ref, expand_ref, gain_ref, bias_ref, one_ref, two_ref, item_ref, room):
        core = meta_ref[1]
        side = pl.multiple_of(core * half, 128)
        gains_count = gain_ref.room.shape[0]
        room[...] = jnp.zeros_like(room)
        room[:gains_count, :rows] = gain_ref.ready()[...].astype(wide)
        room[gains_count:small, :rows] = bias_ref.ready()[...].astype(wide)
        one_ref[:, 4 * half :] = room[...].T[:rows].astype(half_type)
        mat = joint_ref.ready()
        for part in range(3):
            one_ref[:, part * half : (part + 1) * half] = mat[
                :, pl.ds(pl.multiple_of(part * width + side, 128), half)
            ]
        one_ref[:, 3 * half : 4 * half] = output_ref.ready()[:, pl.ds(side, half)]
        two_ref[...] = expand_ref.ready()[:, pl.ds(pl.multiple_of(core * hidden, 128), hidden)]
        line = (16, width)
        lane = lax.broadcasted_iota(jnp.int32, line, 1)
        value = jnp.where(lane == 0, lengths_ref[0], jnp.where(lane == 1, lengths_ref[1], 0))
        item_ref[:count] = tokens_ref.ready()[...]
        item_ref[count : 2 * count] = cot_ref.ready()[...]
        item_ref[2 * count :] = value.astype(wide).astype(half_type)

    return call(
        body,
        "pack_blocks",
        (meta, lengths, tokens, cot, joint, output, expand, gains, biases),
        (SCALAR, SCALAR) + (FETCH,) * 7,
        (
            shaped((rows, 4 * half + 128), half_type),
            shaped((rows, hidden), half_type),
            shaped((2 * count + 16, width), half_type),
        ),
        (PUT, PUT, PUT),
        (pltpu.VMEM((128, 128), wide),),
    )


def lane_is_low(shape):
    return lax.broadcasted_iota(jnp.int32, shape, 1) < HEAD_DIM


def two_heads(value, low):
    zero = jnp.zeros_like(value)
    return jnp.concatenate([jnp.where(low, value, zero), jnp.where(low, zero, value)], axis=0)


def one_of_two(value, low):
    rows = value.shape[0] // 2
    return jnp.where(low, value[:rows], value[rows:])


def attend(meta, lengths, tokens, item_got, joint):
    tokens_rows, width = tokens.shape
    half = width // 2
    rows = 2 * tokens_rows
    pairs = half // 128

    def body(meta_ref, lengths_ref, own_ref, item_ref, *rest):
        pieces = rest[: len(joint.arrays)]
        normed_ref, projected_ref, attention_ref, attended_ref, output_ref, small_ref = rest[
            len(joint.arrays) : len(joint.arrays) + 6
        ]
        core = meta_ref[1]
        loading = Loading(joint, pieces, meta_ref, rest[len(joint.arrays) + 6 :])
        sides = (own_ref.ready()[...], item_ref.ready()[:tokens_rows])
        units = [norm_parts(side.astype(wide))[0] for side in sides]
        mat = loading.ready()
        small_ref[...] = mat[:, 4 * half :].astype(wide).T[:16]
        output_ref[...] = mat[:, 3 * half : 4 * half]
        side = pl.multiple_of(core * half, 128)
        for item in range(2):
            normed_ref[item * tokens_rows : (item + 1) * tokens_rows] = (
                units[item] * small_ref[0:1] + small_ref[2:3]
            ).astype(half_type)
        normed = normed_ref[...]
        for part in range(3):
            spot = slice(part * half, (part + 1) * half)
            value = matmul(normed, mat[:, spot])
            if part != 1:
                row = 4 if part == 0 else 5
                value = value + small_ref[row : row + 1, pl.ds(side, half)]
            projected_ref[:, spot] = value.astype(half_type)
        low = lane_is_low((tokens_rows, 128))
        query = lax.broadcasted_iota(jnp.int32, (rows, tokens_rows), 0) % tokens_rows
        key = lax.broadcasted_iota(jnp.int32, (rows, tokens_rows), 1)
        for item in range(2):
            if item == 0:
                prefix, total = lengths_ref[0], lengths_ref[1]
            else:
                line = item_ref.room[2 * tokens_rows : 2 * tokens_rows + 16].astype(wide)
                prefix = line[0:1, 0:1].astype(jnp.int32)
                total = line[0:1, 1:2].astype(jnp.int32)
            visible = (key < total) & ((key <= query) | (key < prefix))
            take = slice(item * tokens_rows, (item + 1) * tokens_rows)
            for pair in range(pairs):
                spot = slice(pair * 128, (pair + 1) * 128)
                queries = two_heads(projected_ref[take, spot], low)
                keys = projected_ref[take, half + pair * 128 : half + (pair + 1) * 128]
                values = projected_ref[take, 2 * half + pair * 128 : 2 * half + (pair + 1) * 128]
                scores = times_back(queries, keys) * HEAD_DIM ** (-0.5)
                scores = jnp.where(visible, scores, -1e30)
                powers = jnp.exp(scores - jnp.max(scores, axis=-1, keepdims=True))
                attention = powers / jnp.sum(powers, axis=-1, keepdims=True)
                attention_ref[item * pairs + pair] = attention
                mixed = matmul(attention.astype(half_type), values)
                attended_ref[take, spot] = one_of_two(mixed, low).astype(half_type)

    return call(
        body,
        "attend",
        (meta, lengths, tokens, item_got, *joint.arrays),
        (SCALAR, SCALAR, FETCH, FETCH) + (RAW,) * len(joint.arrays),
        (
            shaped((rows, width), half_type),
            shaped((rows, 3 * half), half_type),
            shaped((2 * pairs, rows, tokens_rows), wide),
            shaped((rows, half), half_type),
            shaped((width, half), half_type),
            shaped((16, width), wide),
        ),
        (HELD, HELD, HELD, PUT, PUT, HELD),
        joint.scratch(),
    )


def flipped(ref):
    rows = ref.shape[0] // 2
    return jnp.concatenate([ref[rows:], ref[:rows]], axis=0)


def grow(meta, small, tokens, cot, item_got, attended, attended_got, output, output_got, expand, quarters):
    tokens_rows, width = tokens.shape
    half = width // 2
    rows = 2 * tokens_rows
    hidden = expand.layout.width
    shapes = quarters.shapes()
    step = 384

    def body(meta_ref, small_ref, own_ref, cot_ref, item_ref, attended_ref, attended_got_ref, output_ref, output_got_ref, *rest):
        pieces = rest[: len(expand.arrays)]
        rest = rest[len(expand.arrays) :]
        middle_ref, normed_ref, active_ref, slope_ref, mixed_ref = rest[:5]
        grads = rest[5 : 5 + len(shapes)]
        *scratch, upstream = rest[5 + len(shapes) :]
        core = meta_ref[1]
        loading = Loading(expand, pieces, meta_ref, scratch[:3])
        storing = Storing(quarters, grads, meta_ref, scratch[3:])
        mine = pl.ds(pl.multiple_of(core * half, 128), half)
        yours = pl.ds(pl.multiple_of((1 - core) * half, 128), half)
        mixed_ref[:, mine] = attended_ref.ready()[...]
        mixed_ref[:, yours] = flipped(attended_got_ref.ready())
        mixed = mixed_ref[...]
        middle_ref[:, mine] = matmul(mixed, output_ref.ready()[...])
        middle_ref[:, yours] = matmul(mixed, output_got_ref.ready()[...])
        sides = (own_ref.ready()[...], item_ref.ready()[:tokens_rows])
        for item, side in enumerate(sides):
            take = slice(item * tokens_rows, (item + 1) * tokens_rows)
            middle = side.astype(wide) + (middle_ref[take] + small_ref[6:7])
            middle_ref[take] = middle
            unit, _ = norm_parts(middle)
            normed_ref[take] = (unit * small_ref[1:2] + small_ref[3:4]).astype(half_type)
        upstream[:tokens_rows] = cot_ref.ready()[...]
        upstream[tokens_rows:] = item_ref.ready()[tokens_rows : 2 * tokens_rows]
        mat = loading.ready()
        normed = normed_ref[...]
        back = upstream[...]
        for at in range(0, hidden, step):
            spot = slice(at, at + step)
            row = 8 + core * (hidden // width) + at // width
            bias = small_ref[pl.ds(row, 1), at % width : at % width + step]
            value = matmul(normed, mat[:, spot]) + bias
            square = value * value
            bent = jnp.tanh(curve * (value + cubic * value * square))
            active = (0.5 * value * (1.0 + bent)).astype(half_type)
            active_ref[:, spot] = active
            slope_ref[:, spot] = 0.5 * (1.0 + bent) + 0.5 * value * (1.0 - bent * bent) * (
                curve * (1.0 + 3.0 * cubic * square)
            )
            storing.put(at, slice(None), outer_sum(active, back))
        storing.send()
        storing.wait()

    outs = (
        shaped((rows, width), wide),
        shaped((rows, width), half_type),
        shaped((rows, hidden), half_type),
        shaped((rows, hidden), wide),
        shaped((rows, width), half_type),
    ) + tuple(shapes)
    return call(
        body,
        "grow",
        (meta, small, tokens, cot, item_got, attended, attended_got, output, output_got, *expand.arrays),
        (SCALAR, HELD) + (FETCH,) * 7 + (RAW,) * len(expand.arrays),
        outs,
        (HELD,) * 5 + (RAW,) * len(shapes),
        (*expand.scratch(), *quarters.scratch(), pltpu.VMEM((rows, width), half_type)),
    )


def shrink_back(meta, cot, item_got, slope, shrink, expand):
    tokens_rows, width = cot.shape
    rows = 2 * tokens_rows
    hidden = expand.layout.width

    def body(meta_ref, cot_ref, item_ref, slope_ref, *rest):
        shrink_pieces = rest[: len(shrink.arrays)]
        rest = rest[len(shrink.arrays) :]
        expand_pieces = rest[: len(expand.arrays)]
        hidden_ref, part_ref, *scratch, upstream = rest[len(expand.arrays) :]
        first = Loading(shrink, shrink_pieces, meta_ref, scratch[:3])
        second = Loading(expand, expand_pieces, meta_ref, scratch[3:])
        upstream[:tokens_rows] = cot_ref.ready()[...]
        upstream[tokens_rows:] = item_ref.ready()[tokens_rows : 2 * tokens_rows]
        mat = first.ready()
        step = 384
        for at in range(0, hidden, step):
            spot = slice(at, at + step)
            value = times_back(upstream[...], mat[spot])
            hidden_ref[:, spot] = (value * slope_ref[:, spot]).astype(half_type)
        other = second.ready()
        part_ref[...] = times_back(hidden_ref[...], other[...])

    return call(
        body,
        "shrink_back",
        (meta, cot, item_got, slope, *shrink.arrays, *expand.arrays),
        (SCALAR, FETCH, FETCH, HELD) + (RAW,) * (len(shrink.arrays) + len(expand.arrays)),
        (shaped((rows, hidden), half_type), shaped((rows, width), wide)),
        (HELD, PUT),
        (*shrink.scratch(), *expand.scratch(), pltpu.VMEM((rows, width), half_type)),
    )


def expand_grads(meta, active, normed_two, back_hidden, shrink, quarters):
    rows, hidden = active.shape
    width = normed_two.shape[1]
    tokens_rows = rows // 2
    shapes = quarters.shapes()

    def body(meta_ref, active_ref, normed_ref, hidden_ref, *rest):
        pieces = rest[: len(shrink.arrays)]
        rest = rest[len(shrink.arrays) :]
        own_ref, other_ref, bias_ref = rest[:3]
        grads = rest[3 : 3 + len(shapes)]
        scratch = rest[3 + len(shapes) :]
        loading = Loading(shrink, pieces, meta_ref, scratch[:3])
        storing = Storing(quarters, grads, meta_ref, scratch[3:])
        step = 384
        for at in range(0, hidden, step):
            spot = slice(at, at + step)
            storing.put(0, spot, outer_sum(normed_ref[...], hidden_ref[:, spot]))
        storing.send()
        bias_ref[...] = jnp.sum(hidden_ref[...].astype(wide), axis=0, keepdims=True)
        mat = loading.ready()
        for ref, at in ((own_ref, 0), (other_ref, tokens_rows)):
            ref[...] = matmul(active_ref[at : at + tokens_rows], mat[...])
        storing.wait()

    outs = (
        shaped((tokens_rows, width), wide),
        shaped((tokens_rows, width), wide),
        shaped((1, hidden), wide),
    ) + tuple(shapes)
    return call(
        body,
        "expand_grads",
        (meta, active, normed_two, back_hidden, *shrink.arrays),
        (SCALAR, HELD, HELD, HELD) + (RAW,) * len(shrink.arrays),
        outs,
        (HELD, PUT, HELD) + (RAW,) * len(shapes),
        (*shrink.scratch(), *quarters.scratch()),
    )


def attend_back(meta, small, middle, cot, item_got, part, part_got, mixed, output, output_got, normed, projected, attention, quarters):
    rows, width = middle.shape
    half = width // 2
    tokens_rows = rows // 2
    pairs = half // 128
    shapes = quarters.shapes()

    def body(meta_ref, small_ref, middle_ref, cot_ref, item_ref, part_ref, part_got_ref, mixed_ref, output_ref, output_got_ref, normed_ref, projected_ref, attention_ref, back_middle_ref, back_projected_ref, sums_ref, *rest):
        grads = rest[: len(shapes)]
        *scratch, branch = rest[len(shapes) :]
        core = meta_ref[1]
        storing = Storing(quarters, grads, meta_ref, scratch)
        mine = pl.ds(pl.multiple_of(core * half, 128), half)
        yours = pl.ds(pl.multiple_of((1 - core) * half, 128), half)
        gain = jnp.zeros((1, width), wide)
        shift = jnp.zeros((1, width), wide)
        bias_branch = jnp.zeros((1, width), wide)
        bias_second = jnp.zeros((1, width), wide)
        sides = (cot_ref.ready()[...], item_ref.ready()[tokens_rows : 2 * tokens_rows])
        part_ref, part_got_ref = part_ref.ready(), part_got_ref.ready()
        output_ref, output_got_ref = output_ref.ready(), output_got_ref.ready()
        for item, side in enumerate(sides):
            take = slice(item * tokens_rows, (item + 1) * tokens_rows)
            across = slice((1 - item) * tokens_rows, (2 - item) * tokens_rows)
            unit, scale = norm_parts(middle_ref[take])
            upstream = side.astype(wide)
            back = part_ref[take] + part_got_ref[across].astype(wide)
            value = upstream + norm_back(unit, scale, small_ref[1:2], back)
            if item == 0:
                back_middle_ref[...] = value
            low_value = value.astype(half_type)
            branch[take] = low_value
            gain = gain + jnp.sum(back * unit, axis=0, keepdims=True)
            shift = shift + jnp.sum(back, axis=0, keepdims=True)
            bias_branch = bias_branch + jnp.sum(low_value.astype(wide), axis=0, keepdims=True)
            bias_second = bias_second + jnp.sum(upstream, axis=0, keepdims=True)
        sums_ref[...] = jnp.zeros_like(sums_ref)
        sums_ref[1:2] = 0.5 * gain
        sums_ref[3:4] = 0.5 * shift
        sums_ref[6:7] = 0.5 * bias_branch
        sums_ref[7:8] = 0.5 * bias_second
        storing.put(0, slice(3 * half, 4 * half), outer_sum(mixed_ref[...], branch[:, mine]))
        height = pl.ds(pl.multiple_of(core * half, 128), half)
        back_attended = (
            times_back(branch[:, mine], output_ref[height])
            + times_back(branch[:, yours], output_got_ref[height])
        ).astype(half_type)
        low = lane_is_low((tokens_rows, 128))
        for item in range(2):
            take = slice(item * tokens_rows, (item + 1) * tokens_rows)
            for pair in range(pairs):
                spot = slice(pair * 128, (pair + 1) * 128)
                queries = two_heads(projected_ref[take, spot], low)
                keys = projected_ref[take, half + pair * 128 : half + (pair + 1) * 128]
                values = projected_ref[take, 2 * half + pair * 128 : 2 * half + (pair + 1) * 128]
                upstream = two_heads(back_attended[take, spot], low)
                attention = attention_ref[item * pairs + pair]
                back_values = outer_sum(attention.astype(half_type), upstream)
                back_attention = times_back(upstream, values)
                inner = jnp.sum(attention * back_attention, axis=-1, keepdims=True)
                back_scores = (HEAD_DIM ** (-0.5) * attention * (back_attention - inner)).astype(half_type)
                back_queries = one_of_two(matmul(back_scores, keys), low)
                back_keys = outer_sum(back_scores, queries)
                for part_at, value in enumerate((back_queries, back_keys, back_values)):
                    start = part_at * half + pair * 128
                    back_projected_ref[take, start : start + 128] = value.astype(half_type)
        sums_ref[4:5, mine] = jnp.sum(back_projected_ref[:, :half].astype(wide), axis=0, keepdims=True)
        sums_ref[5:6, mine] = jnp.sum(
            back_projected_ref[:, 2 * half :].astype(wide), axis=0, keepdims=True
        )
        for part_at in range(3):
            spot = slice(part_at * half, (part_at + 1) * half)
            storing.put(0, spot, outer_sum(normed_ref[...], back_projected_ref[:, spot]))
        storing.send()
        storing.wait()

    outs = (
        shaped((tokens_rows, width), wide),
        shaped((rows, 3 * half), half_type),
        shaped((16, width), wide),
    ) + tuple(shapes)
    return call(
        body,
        "attend_back",
        (meta, small, middle, cot, item_got, part, part_got, mixed, output, output_got, normed, projected, attention),
        (SCALAR, HELD, HELD, FETCH, FETCH, FETCH, FETCH, HELD, FETCH, FETCH, HELD, HELD, HELD),
        outs,
        (HELD,) * 3 + (RAW,) * len(shapes),
        (*quarters.scratch(), pltpu.VMEM((rows, width), half_type)),
    )


def joint_back(meta, back_projected, joint, width):
    rows, depth = back_projected.shape
    tokens_rows = rows // 2

    def body(meta_ref, back_ref, *rest):
        pieces = rest[: len(joint.arrays)]
        own_ref, other_ref, *scratch = rest[len(joint.arrays) :]
        mat = Loading(joint, pieces, meta_ref, scratch).ready()
        other_ref[...] = times_back(back_ref[tokens_rows:], mat[:, :depth])
        own_ref[...] = times_back(back_ref[:tokens_rows], mat[:, :depth])

    return call(
        body,
        "joint_back",
        (meta, back_projected, *joint.arrays),
        (SCALAR, HELD) + (RAW,) * len(joint.arrays),
        (shaped((tokens_rows, width), wide), shaped((tokens_rows, width), wide)),
        (HELD, PUT),
        joint.scratch(),
    )


def finish(meta, small, tokens, middle, second, second_got, back_middle, back_one, back_got, sums, expand_bias):
    tokens_rows, width = tokens.shape
    hidden = expand_bias.shape[1]

    def body(meta_ref, small_ref, own_ref, middle_ref, second_ref, second_got_ref, back_middle_ref, back_ref, back_got_ref, sums_ref, bias_ref, result_ref, input_ref, total_ref):
        core = meta_ref[1]
        result_ref[...] = middle_ref[:tokens_rows] + (
            second_ref[...] + second_got_ref.ready()[...] + small_ref[7:8]
        )
        unit, scale = norm_parts(own_ref.ready()[...].astype(wide))
        back = back_ref[...] + back_got_ref.ready()[...]
        input_ref[...] = back_middle_ref[...] + norm_back(unit, scale, small_ref[0:1], back)
        total_ref[...] = sums_ref[...]
        total_ref[0:1] = jnp.sum(back * unit, axis=0, keepdims=True)
        total_ref[2:3] = jnp.sum(back, axis=0, keepdims=True)
        count = hidden // width
        for at in range(count):
            total_ref[pl.ds(8 + core * count + at, 1)] = bias_ref[:, at * width : (at + 1) * width]

    return call(
        body,
        "finish",
        (meta, small, tokens, middle, second, second_got, back_middle, back_one, back_got, sums, expand_bias),
        (SCALAR, HELD, FETCH, HELD, HELD, FETCH, HELD, HELD, FETCH, HELD, HELD),
        (shaped((tokens_rows, width), wide), shaped((tokens_rows, width), wide), shaped((16, width), wide)),
        (PUT, PUT, PUT),
        (),
    )


def local(
    tokens,
    cotangent,
    lengths,
    joint_weight,
    output_weight,
    expand_weight,
    shrink_weight,
    norm_gains,
    bias_rows,
    master_joint,
    master_output,
    master_expand,
    master_shrink,
    master_gains,
    master_biases,
    first_joint,
    first_output,
    first_expand,
    first_shrink,
    first_gains,
    first_biases,
    second_joint,
    second_output,
    second_expand,
    second_shrink,
    second_gains,
    second_biases,
):
    grid = Grid()
    core = grid.core
    size = grid.size
    width = tokens.shape[2]
    half = width // 2
    small_rows = norm_gains.shape[1] + bias_rows.shape[1]
    meta = jnp.stack([grid.index, core])
    lengths_own = lengths[0]
    tokens_own, cot = tokens[0], cotangent[0]
    joint_block, expand_block, item = pack_blocks(
        meta, lengths_own, tokens_own, cot,
        joint_weight[0], output_weight[0], expand_weight[0], norm_gains[0], bias_rows[0],
    )
    item_got = grid.swap_core(item)
    one = Gather(grid, joint_block, False)
    two = Gather(grid, expand_block, False)
    three = Gather(grid, after(shrink_weight[0], joint_block), True)
    one.high()
    two.value = after(two.value, one.value)
    two.high()
    three.value = after(three.value, two.value)
    three.high()
    one.low(True)
    one_near = one.first(0)
    two.value = after(two.value, one_near[0][1][1], one_near[1][1])
    two.low(False)
    three.low(False)
    one.start[1] = (one.start[1][0], after(one.start[1][1], one_near[0][1][1], one_near[1][1]))
    one_far = one.first(1)
    near_pieces = one.second(one_near)
    one_far[0][1] = (one_far[0][1][0], after(one_far[0][1][1], *[piece for _, piece in near_pieces], one_far[1][1]))
    joint = Pieces(grid, near_pieces + one.second(one_far), size)
    two.start[0] = (two.start[0][0], after(two.start[0][1], one_far[0][1][1], one_far[1][1]))
    two_all = two.first(0)
    expand = Pieces(grid, two.second(two_all), size)
    three.start[0] = (three.start[0][0], after(three.start[0][1], two_all[0][1][1]))
    three_all = three.first(0)
    shrink = Pieces(grid, three.second(three_all), size // 2)
    lasting = (*grid.low_bits[::-1], grid.top_bit)
    shrink_quarters = Parts(grid, shrink.layout, lasting[:-1])
    expand_quarters = Parts(grid, expand.layout, lasting)
    joint_quarters = Parts(grid, Layout(size, joint.layout.rows, 4 * half), lasting)

    normed, projected, attention, attended, output, small = attend(
        meta, lengths_own, tokens_own, item_got, joint
    )
    attended_got = after(grid.swap_core(attended), three_all[0][1][1])
    output_got = grid.swap_core(output)
    middle, normed_two, active, slope, mixed, *shrink_grads = grow(
        meta, small, tokens_own, cot, item_got, attended, attended_got,
        output, output_got, expand, shrink_quarters,
    )
    shrink_sum = third_sum(grid, *shrink_quarters.second(shrink_quarters.first(shrink_grads)), owned=True)
    back_hidden, part = shrink_back(meta, cot, item_got, slope, shrink, expand)
    part_got = grid.swap_core(part)
    second, second_other, expand_bias, *expand_grad = expand_grads(
        meta, active, normed_two, back_hidden, shrink, expand_quarters
    )
    expand_sum = third_sum(grid, *expand_quarters.second(expand_quarters.first(expand_grad)))
    second_got = grid.swap_core(second_other)
    back_middle, back_projected, sums, *joint_grad = attend_back(
        meta, small, middle, cot, item_got, part, part_got, mixed, output, output_got,
        normed, projected, attention, joint_quarters,
    )
    joint_first = joint_quarters.first(joint_grad)
    joint_sum_all = third_sum(grid, *joint_quarters.second(joint_first))
    back_one, back_other = joint_back(meta, after(back_projected, joint_first[0]), joint, width)
    back_got = grid.swap_core(back_other)
    result, input_grad, small_grads = finish(
        meta, small, tokens_own, middle, second, second_got, back_middle, back_one, back_got,
        sums, expand_bias,
    )
    small_sum = sum_all(grid, small_grads)
    own = norm_gains.shape[2]
    small_own = lax.dynamic_slice_in_dim(small_sum, grid.index * own, own, axis=1)
    gains_count = norm_gains.shape[1]

    third = [joint_sum_all[:, part_at * half : (part_at + 1) * half] for part_at in range(3)]
    joint_got = grid.swap_core(jnp.where(core == 0, third[2], third[0]))
    joint_sum = jnp.where(
        core == 0,
        jnp.concatenate([third[0], joint_got, third[1]], axis=1),
        jnp.concatenate([third[1], joint_got, third[2]], axis=1),
    )
    output_sum = joint_sum_all[:, 3 * half :]
    owner = grid.top == core
    side = shrink_sum.shape[1] // 2
    shrink_send = lax.dynamic_slice_in_dim(shrink_sum, (1 - core) * side, side, axis=1)
    shrink_keep = lax.dynamic_slice_in_dim(shrink_sum, core * side, side, axis=1)
    shrink_own = jnp.where(owner, shrink_keep, grid.swap_core(shrink_send))

    masters = (
        master_joint,
        master_output,
        master_expand,
        master_shrink,
        master_gains,
        master_biases,
    )
    firsts = (first_joint, first_output, first_expand, first_shrink, first_gains, first_biases)
    seconds = (
        second_joint,
        second_output,
        second_expand,
        second_shrink,
        second_gains,
        second_biases,
    )
    totals_all = (
        joint_sum[None],
        output_sum[None],
        expand_sum[None],
        shrink_own[None],
        small_own[None, :gains_count],
        small_own[None, gains_count:small_rows],
    )
    results = [result[None], input_grad[None]]
    for group_index in range(6):
        group_rate = learning_rate if group_index < 4 else small_rate
        new_master, new_first, new_second, new_copy = adamw(
            masters[group_index],
            firsts[group_index],
            seconds[group_index],
            totals_all[group_index],
            group_rate,
        )
        results.extend([totals_all[group_index], new_master, new_first, new_second, new_copy])
    return tuple(results)


def solution(mesh):
    placed = (
        P(("dp", "fsdp"), None, None),
        P(("dp", "fsdp"), None, None),
        P(("dp", "fsdp"), None),
        P(None, "fsdp", None),
        P(None, "fsdp", None),
        P(None, "fsdp", None),
        P(None, "fsdp", None),
        P(None, None, "fsdp"),
        P(None, None, "fsdp"),
        P(None, "fsdp", "dp"),
        P(None, "fsdp", "dp"),
        P(None, "fsdp", "dp"),
        P(None, "fsdp", "dp"),
        P(None, None, "fsdp"),
        P(None, None, "fsdp"),
        P(None, "fsdp", "dp"),
        P(None, "fsdp", "dp"),
        P(None, "fsdp", "dp"),
        P(None, "fsdp", "dp"),
        P(None, None, "fsdp"),
        P(None, None, "fsdp"),
        P(None, "fsdp", "dp"),
        P(None, "fsdp", "dp"),
        P(None, "fsdp", "dp"),
        P(None, "fsdp", "dp"),
        P(None, None, "fsdp"),
        P(None, None, "fsdp"),
    )
    return jax.shard_map(
        local,
        mesh=mesh,
        in_specs=placed,
        out_specs=(
            P(("dp", "fsdp"), None, None),
            P(("dp", "fsdp"), None, None),
            P(None, "fsdp", "dp"),
            P(None, "fsdp", "dp"),
            P(None, "fsdp", "dp"),
            P(None, "fsdp", "dp"),
            P(None, "fsdp", "dp"),
            P(None, "fsdp", "dp"),
            P(None, "fsdp", "dp"),
            P(None, "fsdp", "dp"),
            P(None, "fsdp", "dp"),
            P(None, "fsdp", "dp"),
            P(None, "fsdp", "dp"),
            P(None, "fsdp", "dp"),
            P(None, "fsdp", "dp"),
            P(None, "fsdp", "dp"),
            P(None, "fsdp", "dp"),
            P(None, "fsdp", "dp"),
            P(None, "fsdp", "dp"),
            P(None, "fsdp", "dp"),
            P(None, "fsdp", "dp"),
            P(None, "fsdp", "dp"),
            P(None, None, "fsdp"),
            P(None, None, "fsdp"),
            P(None, None, "fsdp"),
            P(None, None, "fsdp"),
            P(None, None, "fsdp"),
            P(None, None, "fsdp"),
            P(None, None, "fsdp"),
            P(None, None, "fsdp"),
            P(None, None, "fsdp"),
            P(None, None, "fsdp"),
        ),
        check_vma=False,
    )
```

time: 1270 us -> 197 us (0.16)
  waiting for transfers between devices: 1060 us -> 85.2 us
  blocking collectives: 87.5 us -> 0 us
  matrix products: 50.7 us -> 0 us
  Pallas kernels: 0 us -> 41.1 us
  starting transfers between devices: 0.77 us -> 40.7 us
  local copies, waits for them, and re-layouts: 31.1 us -> 11.5 us
  between operations: 14.7 us -> 1.38 us
    reduce_scatter x8 -> x0, waiting for transfers between devices: 628 us -> none  [the longest x1 176 us: local(): lax.psum_scatter(matrices[2], 'fsdp', scatter_dimension=0, tiled=True)]
    unnamed x16 -> x0, waiting for transfers between devices: 249 us -> none
    all_gather x4 -> x0, waiting for transfers between devices: 184 us -> none  [the longest x1 80.2 us: local(): lax.all_gather(expand_weight[layer_index], 'fsdp', axis=0, tiled=True)]
    ppermute x0 -> x43, waiting for transfers between devices: none -> 85.2 us  [the longest x14 44.7 us: swap(): lax.ppermute(value, 'fsdp', [(i, i ^ 1 << bit) for i in range(self.size)])]
    all_gather x2 -> x0, blocking collectives: 85.1 us -> none  [the longest x1 45.5 us: local(): lax.all_gather(bias_rows[layer_index], 'fsdp', axis=1, tiled=True)]
    dot_general x17 -> x0, matrix products: 49.4 us -> none  [the longest x4 17.9 us: outer_sum(): lax.dot_general(left, right, (((0,), (0,)), ((), ())), preferred_element_...]
    pallas_call x0 -> x8, Pallas kernels: none -> 41.1 us  [call(): pl.pallas_call(whole, name=name, out_shape=tuple(outs), in_specs=[pl.Bloc...]
    ppermute x0 -> x43, starting transfers between devices: none -> 40.7 us  [the longest x14 20.1 us: swap(): lax.ppermute(value, 'fsdp', [(i, i ^ 1 << bit) for i in range(self.size)])]
  transfers between devices with their start and end apart: 14 -> 43, of which waited for: 13 -> 26; matrix products, arithmetic and copies ran while one was open for 7% -> 9% of each run, Pallas kernels for 0% -> 19%
where the time goes in v2:
time: 197 us; the launch traced here: 196 us
  waiting for transfers between devices  85.2 us (43%)
  Pallas kernels  41.1 us (21%)
  starting transfers between devices  40.7 us (21%)
  other arithmetic  16.2 us (8%)
  local copies, waits for them, and re-layouts  11.5 us (6%)
    ppermute x14, waiting for transfers between devices, swap(): lax.ppermute(value, 'fsdp', [(i, i ^ 1 << bit) for i in range(self.size)])  44.7 us
    pallas_call x8, Pallas kernels, call(): pl.pallas_call(whole, name=name, out_shape=tuple(outs), in_specs=[pl.Bloc...  41.1 us
    ppermute x18, waiting for transfers between devices, swap_step(): return lax.ppermute(value, ('dp', 'fsdp'), pairs)  37.8 us
    ppermute x14, starting transfers between devices, swap(): lax.ppermute(value, 'fsdp', [(i, i ^ 1 << bit) for i in range(self.size)])  20.1 us
    ppermute x18, starting transfers between devices, swap_step(): return lax.ppermute(value, ('dp', 'fsdp'), pairs)  17 us
    unnamed x111, local copies, waits for them, and re-layouts  10.9 us
    convert_element_type x9, other arithmetic, join(): return (keep.astype(wide) + got.astype(wide)).astype(half_type)  7.24 us
    convert_element_type x6, other arithmetic, adamw(): return (master_new, first_new, second_new, master_new.astype(jnp.bfloat16))  5.24 us
  transfers between devices with their start and end apart: 43, of which 26 were waited for; matrix products, arithmetic and copies ran while one was open for 9% of the time, Pallas kernels for 19%

profile of v2, /device:TPU:0, one launch (start us, length us, event | category | flops | bytes accessed | tf_op | source)
XLA Modules:
  0.0 196.1 jit_solution(9348636395656496845)
XLA Ops:
  1.3 2.9 %pack_blocks.1 = (bf16[48,1664]{1,0:T(8,128)(2,1)}, bf16[48,1536]{1,0:T(8,128)(2,1)}, bf16[272,768]{1,0:T(8,128)(2,1)}) custom-call(s32[2]{0:T(128)} %pad_add_fusion.refs_0_, s32[2]{0:T(128)} %bitcast.85, bf16[128,768]{1,0:T(8,128)(2,1)} %bitcast.81, bf16[128,768]{1,0:T(8,128)(2,1)} %bitcast.77, bf16[48,2304]{1,0:T(8,128)(2,1)} %bitcast.94, ...), custom_call_target="tpu_custom_call" | custom-call | flops 1724999936 | bytes 1 | tf_op jit(solution)/shard_map/pack_blocks/pallas_call | solution.py:238
  4.2 4.1 %collective-permute-start.1 = (bf16[1,48,1664]{2,1,0:T(8,128)(2,1)}, bf16[1,48,1664]{2,1,0:T(8,128)(2,1)S(1)}, u32[]{:S(2)}, u32[]{:S(2)}) collective-permute-start(bf16[1,48,1664]{2,1,0:T(8,128)(2,1)} %bitcast.88), channel_id=1, source_target_pairs={{0,8},{1,9},{2,10},{3,11},{4,12},{5,13},{6,14},{7,15},{8,0},{9,1},... | collective-permute-start | bytes 479240 | tf_op jit(solution)/shard_map/ppermute | solution.py:71
  8.3 7.7 %collective-permute-done.1 = bf16[1,48,1664]{2,1,0:T(8,128)(2,1)S(1)} collective-permute-done((bf16[1,48,1664]{2,1,0:T(8,128)(2,1)}, bf16[1,48,1664]{2,1,0:T(8,128)(2,1)S(1)}, u32[]{:S(2)}, u32[]{:S(2)}) %collective-permute-start.1) | collective-permute-done | bytes 159776 | tf_op jit(solution)/shard_map/ppermute | solution.py:71
  17.0 1.6 collective-permute-start.2
  18.6 1.5 collective-permute-start.3
  20.9 3.3 %collective-permute-start.10 = (bf16[1,48,1536]{2,1,0:T(8,128)(2,1)}, bf16[1,48,1536]{2,1,0:T(8,128)(2,1)S(1)}, u32[]{:S(2)}, u32[]{:S(2)}) collective-permute-start(bf16[1,48,1536]{2,1,0:T(8,128)(2,1)} %bitcast.90), channel_id=1, source_target_pairs={{0,8},{1,9},{2,10},{3,11},{4,12},{5,13},{6,14},{7,15},{8,0},{9,1},... | collective-permute-start | bytes 442376 | tf_op jit(solution)/shard_map/ppermute | solution.py:71
  25.2 5.4 %collective-permute-done.10 = bf16[1,48,1536]{2,1,0:T(8,128)(2,1)S(1)} collective-permute-done((bf16[1,48,1536]{2,1,0:T(8,128)(2,1)}, bf16[1,48,1536]{2,1,0:T(8,128)(2,1)S(1)}, u32[]{:S(2)}, u32[]{:S(2)}) %collective-permute-start.10) | collective-permute-done | bytes 147488 | tf_op jit(solution)/shard_map/ppermute | solution.py:71
  30.7 4.0 %collective-permute-start.13 = (bf16[2,48,1536]{2,1,0:T(8,128)(2,1)S(1)}, bf16[2,48,1536]{2,1,0:T(8,128)(2,1)S(1)}, u32[]{:S(2)}, u32[]{:S(2)}) collective-permute-start(bf16[2,48,1536]{2,1,0:T(8,128)(2,1)S(1)} %constant_dynamic-update-slice_fusion), channel_id=1, source_target_pairs={{0,4},{1,5},{2,6},{3,7},{4,0},{5,1},{6,2},{7,3},{8,12},{9,13},{10,... | collective-permute-start | bytes 884744 | tf_op jit(solution)/shard_map/ppermute | solution.py:71
  35.7 1.5 collective-permute-start.7
  37.2 1.6 collective-permute-start.11
  38.8 2.2 %collective-permute-done.13 = bf16[2,48,1536]{2,1,0:T(8,128)(2,1)S(1)} collective-permute-done((bf16[2,48,1536]{2,1,0:T(8,128)(2,1)S(1)}, bf16[2,48,1536]{2,1,0:T(8,128)(2,1)S(1)}, u32[]{:S(2)}, u32[]{:S(2)}) %collective-permute-start.13) | collective-permute-done | bytes 294944 | tf_op jit(solution)/shard_map/ppermute | solution.py:71
  41.1 1.8 collective-permute-done.4.refs_7_.refs_5_
  42.9 2.7 %collective-permute-done.6.refs_9_.refs_7_ = bf16[2,48,1664]{2,1,0:T(8,128)(2,1)S(1)} collective-permute-done((bf16[2,48,1664]{2,1,0:T(8,128)(2,1)S(1)}, bf16[2,48,1664]{2,1,0:T(8,128)(2,1)S(1)}, u32[]{:S(2)}, u32[]{:S(2)}) %collective-permute-start.6) | collective-permute-done | bytes 319520 | tf_op jit(solution)/shard_map/ppermute | solution.py:79
  46.3 1.5 collective-permute-start.14
  48.8 1.5 collective-permute-start.17
  50.3 5.0 %collective-permute-done.12 = bf16[1,192,768]{2,1,0:T(8,128)(2,1)S(1)} collective-permute-done((bf16[1,192,768]{2,1,0:T(8,128)(2,1)S(1)}, bf16[1,192,768]{2,1,0:T(8,128)(2,1)S(1)}, u32[]{:S(2)}, u32[]{:S(2)}) %collective-permute-start.12) | collective-permute-done | bytes 294944 | tf_op jit(solution)/shard_map/ppermute | solution.py:71
  55.4 5.5 %collective-permute-done.14.refs_10_.refs_9_ = bf16[4,48,1536]{2,1,0:T(8,128)(2,1)S(1)} collective-permute-done((bf16[4,48,1536]{2,1,0:T(8,128)(2,1)S(1)}, bf16[4,48,1536]{2,1,0:T(8,128)(2,1)S(1)}, u32[]{:S(2)}, u32[]{:S(2)}) %collective-permute-start.14) | collective-permute-done | bytes 589856 | tf_op jit(solution)/shard_map/ppermute | solution.py:79
  61.0 2.2 %collective-permute-start.15 = (bf16[2,192,768]{2,1,0:T(8,128)(2,1)S(1)}, bf16[2,192,768]{2,1,0:T(8,128)(2,1)S(1)}, u32[]{:S(2)}, u32[]{:S(2)}) collective-permute-start(bf16[2,192,768]{2,1,0:T(8,128)(2,1)S(1)} %pad_maximum_fusion.refs_4_), channel_id=1, source_target_pairs={{0,1},{1,0},{2,3},{3,2},{4,5},{5,4},{6,7},{7,6},{8,9},{9,8},{10,11... | collective-permute-start | bytes 1769480 | tf_op jit(solution)/shard_map/ppermute | solution.py:79
  64.1 4.3 %attend.1 = (bf16[256,768]{1,0:T(8,128)(2,1)S(1)}, bf16[256,1152]{1,0:T(8,128)(2,1)S(1)}, f32[6,256,128]{2,1,0:T(8,128)S(1)}, bf16[256,384]{1,0:T(8,128)(2,1)S(1...) custom-call(s32[2]{0:T(128)S(1)} %copy-done.19, s32[2]{0:T(128)S(1)} %bitcast.86, bf16[128,768]{1,0:T(8,128)(2,1)S(1)} %bitcast.82, ...), custom_call_target="tpu_custom_call" | custom-call | flops 4944999936 | bytes 1 | tf_op jit(solution)/shard_map/attend/pallas_call | solution.py:238
  69.9 1.8 collective-permute-done.9.refs_6_
  71.7 1.2 collective-permute-start.19
  73.7 5.6 %collective-permute-done.18.refs_12_.refs_11_ = bf16[4,48,1536]{2,1,0:T(8,128)(2,1)S(1)} collective-permute-done((bf16[4,48,1536]{2,1,0:T(8,128)(2,1)S(1)}, bf16[4,48,1536]{2,1,0:T(8,128)(2,1)S(1)}, u32[]{:S(2)}, u32[]{:S(2)}) %collective-permute-start.18) | collective-permute-done | bytes 589856 | tf_op jit(solution)/shard_map/ppermute | solution.py:79
  80.1 9.5 %grow.1 = (f32[256,768]{1,0:T(8,128)}, bf16[256,768]{1,0:T(8,128)(2,1)S(1)}, bf16[256,1536]{1,0:T(8,128)(2,1)}, f32[256,1536]{1,0:T(8,128)}, bf16[256,768]{1,0:T...) custom-call(s32[2]{0:T(128)S(1)} %copy-done.19, ...), custom_call_target="tpu_custom_call" | custom-call | flops 10924999680 | bytes 1 | tf_op jit(solution)/shard_map/grow/pallas_call | solution.py:238
  89.7 2.3 %collective-permute-done.20.refs_7_ = bf16[2,192,768]{2,1,0:T(8,128)(2,1)S(1)} collective-permute-done((bf16[2,192,768]{2,1,0:T(8,128)(2,1)S(1)}, bf16[2,192,768]{2,1,0:T(8,128)(2,1)S(1)}, u32[]{:S(2)}, u32[]{:S(2)}) %collective-permute-start.20) | collective-permute-done | bytes 589856 | tf_op jit(solution)/shard_map/ppermute | solution.py:79
  93.0 6.3 %shrink_back.1 = (bf16[256,1536]{1,0:T(8,128)(2,1)S(1)}, f32[256,768]{1,0:T(8,128)}) custom-call(s32[2]{0:T(128)S(1)} %copy-done.19, bf16[128,768]{1,0:T(8,128)(2,1)S(1)} %bitcast.79, bf16[272,768]{1,0:T(8,128)(2,1)S(1)} %collective-permute-done.refs_3_.refs_4_.refs_2_, f32[256,1536]{1,0:T(8,128)} %get-tuple-element.96.refs_3_, ...), custom_call_target="tpu_custom_call" | custom-call | flops 7360000000 | bytes 1 | tf_op jit(solution)/shard_map/shrink_back/pallas_call | solution.py:238
  100.3 4.3 %expand_grads.1 = (f32[128,768]{1,0:T(8,128)S(1)}, f32[128,768]{1,0:T(8,128)S(1)}, f32[1,1536]{1,0:T(1,128)S(1)}, bf16[8,48,1536]{2,1,0:T(8,128)(2,1)}, bf16[4,4...) custom-call(s32[2]{0:T(128)S(1)} %copy-done.19, bf16[256,1536]{1,0:T(8,128)(2,1)S(1)} %copy-done.28, ...), custom_call_target="tpu_custom_call" | custom-call | flops 4944999936 | bytes 1 | tf_op jit(solution)/shard_map/expand_grads/pallas_call | solution.py:238
  106.1 1.3 add_convert_fusion.1
  108.8 8.2 %attend_back.1 = (f32[128,768]{1,0:T(8,128)S(1)}, bf16[256,1152]{1,0:T(8,128)(2,1)S(1)}, f32[16,768]{1,0:T(8,128)S(1)}, bf16[8,48,1536]{2,1,0:T(8,128)(2,1)}, bf...) custom-call(s32[2]{0:T(128)S(1)} %copy-done.19, f32[16,768]{1,0:T(8,128)S(1)} %get-tuple-element.82.refs_1_, ...), custom_call_target="tpu_custom_call" | custom-call | flops 9315000320 | bytes 1 | tf_op jit(solution)/shard_map/attend_back/pallas_call | solution.py:238
  119.2 4.7 %collective-permute-done.34 = bf16[2,192,768]{2,1,0:T(8,128)(2,1)} collective-permute-done((bf16[2,192,768]{2,1,0:T(8,128)(2,1)}, bf16[2,192,768]{2,1,0:T(8,128)(2,1)}, u32[]{:S(2)}, u32[]{:S(2)}) %collective-permute-start.34) | collective-permute-done | bytes 589856 | tf_op jit(solution)/shard_map/ppermute | solution.py:79
  125.3 2.2 %collective-permute-done.29 = bf16[8,48,1536]{2,1,0:T(8,128)(2,1)} collective-permute-done((bf16[8,48,1536]{2,1,0:T(8,128)(2,1)}, bf16[8,48,1536]{2,1,0:T(8,128)(2,1)}, u32[]{:S(2)}, u32[]{:S(2)}) %collective-permute-start.29) | collective-permute-done | bytes 1179680 | tf_op jit(solution)/shard_map/ppermute | solution.py:79
  127.5 1.6 add_convert_fusion.3
  129.8 2.8 %collective-permute-done.35 = bf16[1,192,768]{2,1,0:T(8,128)(2,1)S(1)} collective-permute-done((bf16[1,192,768]{2,1,0:T(8,128)(2,1)S(1)}, bf16[1,192,768]{2,1,0:T(8,128)(2,1)S(1)}, u32[]{:S(2)}, u32[]{:S(2)}) %collective-permute-start.35) | collective-permute-done | bytes 294944 | tf_op jit(solution)/shard_map/ppermute | solution.py:71
  133.6 1.3 collective-permute-start.36
  134.9 11.6 %collective-permute-done.23 = bf16[8,48,1536]{2,1,0:T(8,128)(2,1)} collective-permute-done((bf16[8,48,1536]{2,1,0:T(8,128)(2,1)}, bf16[8,48,1536]{2,1,0:T(8,128)(2,1)}, u32[]{:S(2)}, u32[]{:S(2)}) %collective-permute-start.23) | collective-permute-done | bytes 1179680 | tf_op jit(solution)/shard_map/ppermute | solution.py:79
  146.5 1.7 add_convert_fusion.4
  148.5 3.0 %joint_back.1 = (f32[128,768]{1,0:T(8,128)S(1)}, f32[128,768]{1,0:T(8,128)S(1)}) custom-call(s32[2]{0:T(128)S(1)} %copy-done.19, bf16[256,1152]{1,0:T(8,128)(2,1)S(1)} %copy-done.23, bf16[2,48,1664]{2,1,0:T(8,128)(2,1)S(1)} %pad_maximum_fusion.2.refs_4_.refs_2_, bf16[2,48,1664]{2,1,0:T(8,128)(2,1)S(1)} %collective-permute-done.2.refs_5_.refs_3_, ...), custom_call_target="tpu_custom_call" | custom-call | flops 3335000064 | bytes 1 | tf_op jit(solution)/shard_map/joint_back/pallas_call | solution.py:238
  151.9 1.2 convert_add_fusion
  153.3 2.6 %finish.1 = (f32[128,768]{1,0:T(8,128)}, f32[128,768]{1,0:T(8,128)}, f32[16,768]{1,0:T(8,128)S(1)}) custom-call(s32[2]{0:T(128)S(1)} %copy-done.19, f32[16,768]{1,0:T(8,128)S(1)} %get-tuple-element.82.refs_1_, bf16[128,768]{1,0:T(8,128)(2,1)S(1)} %bitcast.84, f32[256,768]{1,0:T(8,128)S(1)} %copy-done.21, f32[128,768]{1,0:T(8,128)S(1)} %copy-done.25, ...), custom_call_target="tpu_custom_call" | custom-call | flops 2990000128 | bytes 1 | tf_op jit(solution)/shard_map/finish/pallas_call | solution.py:238
  157.4 1.2 collective-permute-start.39
  158.5 2.7 %collective-permute-done.31 = bf16[2,48,1536]{2,1,0:T(8,128)(2,1)S(1)} collective-permute-done((bf16[2,48,1536]{2,1,0:T(8,128)(2,1)S(1)}, bf16[2,48,1536]{2,1,0:T(8,128)(2,1)S(1)}, u32[]{:S(2)}, u32[]{:S(2)}) %collective-permute-start.31) | collective-permute-done | bytes 294944 | tf_op jit(solution)/shard_map/ppermute | solution.py:71
  162.0 1.5 collective-permute-start.40
  164.7 2.4 %collective-permute-done.40 = f32[16,768]{1,0:T(8,128)S(1)} collective-permute-done((f32[16,768]{1,0:T(8,128)S(1)}, f32[16,768]{1,0:T(8,128)S(1)}, u32[]{:S(2)}, u32[]{:S(2)}) %collective-permute-start.40) | collective-permute-done | bytes 49184 | tf_op jit(solution)/shard_map/ppermute | solution.py:71
  167.0 1.8 collective-permute-start.41
  168.8 2.0 %collective-permute-done.32 = bf16[1,48,1536]{2,1,0:T(8,128)(2,1)S(1)} collective-permute-done((bf16[1,48,1536]{2,1,0:T(8,128)(2,1)S(1)}, bf16[1,48,1536]{2,1,0:T(8,128)(2,1)S(1)}, u32[]{:S(2)}, u32[]{:S(2)}) %collective-permute-start.32) | collective-permute-done | bytes 147488 | tf_op jit(solution)/shard_map/ppermute | solution.py:71
  173.7 4.8 %collective-permute-done.42 = f32[16,768]{1,0:T(8,128)S(1)} collective-permute-done((f32[16,768]{1,0:T(8,128)S(1)}, f32[16,768]{1,0:T(8,128)S(1)}, u32[]{:S(2)}, u32[]{:S(2)}) %collective-permute-start.42) | collective-permute-done | bytes 49184 | tf_op jit(solution)/shard_map/ppermute | solution.py:71
  182.2 1.6 collective-permute-done.26
  183.8 1.3 collective-permute-start.27
  185.7 7.4 %collective-permute-done.27 = bf16[1,48,1536]{2,1,0:T(8,128)(2,1)S(1)} collective-permute-done((bf16[1,48,1536]{2,1,0:T(8,128)(2,1)S(1)}, bf16[1,48,1536]{2,1,0:T(8,128)(2,1)S(1)}, u32[]{:S(2)}, u32[]{:S(2)}) %collective-permute-start.27) | collective-permute-done | bytes 147488 | tf_op jit(solution)/shard_map/ppermute | solution.py:71
  (189 shorter events, 34.6 us)
Async XLA Ops:
  4.2 33.0 %copy-start.35 = (bf16[1,192,768]{2,1,0:T(8,128)(2,1)S(1)}, bf16[1,192,768]{2,1,0:T(8,128)(2,1)}, u32[]{:S(2)}) copy-start(bf16[1,192,768]{2,1,0:T(8,128)(2,1)} %param.33) | copy-start | bytes 884740
  4.2 11.8 %collective-permute-start.1 = (bf16[1,48,1664]{2,1,0:T(8,128)(2,1)}, bf16[1,48,1664]{2,1,0:T(8,128)(2,1)S(1)}, u32[]{:S(2)}, u32[]{:S(2)}) collective-permute-start(bf16[1,48,1664]{2,1,0:T(8,128)(2,1)} %bitcast.88), channel_id=1, source_target_pairs={{0,8},{1,9},{2,10},{3,11},{4,12},{5,13},{6,14},{7,15},{8,0},{9,1},... | collective-permute-start | bytes 479240 | tf_op jit(solution)/shard_map/ppermute | solution.py:71
  17.0 13.6 %collective-permute-start.2 = (bf16[2,48,1664]{2,1,0:T(8,128)(2,1)S(1)}, bf16[2,48,1664]{2,1,0:T(8,128)(2,1)S(1)}, u32[]{:S(2)}, u32[]{:S(2)}) collective-permute-start(bf16[2,48,1664]{2,1,0:T(8,128)(2,1)S(1)} %pad_maximum_fusion.2.refs_4_.refs_2_), channel_id=1, source_target_pairs={{0,1},{1,0},{2,3},{3,2},{4,5},{5,4},{6,7},{7,6},{8,9},{9,8},{10,11... | collective-permute-start | bytes 958472 | tf_op jit(solution)/shard_map/ppermute | solution.py:79
  18.6 12.0 %collective-permute-start.3 = (bf16[2,48,1664]{2,1,0:T(8,128)(2,1)S(1)}, bf16[2,48,1664]{2,1,0:T(8,128)(2,1)S(1)}, u32[]{:S(2)}, u32[]{:S(2)}) collective-permute-start(bf16[2,48,1664]{2,1,0:T(8,128)(2,1)S(1)} %pad_maximum_fusion.2.refs_4_.refs_2_), channel_id=1, source_target_pairs={{0,2},{1,3},{2,0},{3,1},{4,6},{5,7},{6,4},{7,5},{8,10},{9,11},{10,... | collective-permute-start | bytes 958472 | tf_op jit(solution)/shard_map/ppermute | solution.py:79
  20.2 14.5 %collective-permute-start.5 = (bf16[2,48,1664]{2,1,0:T(8,128)(2,1)S(1)}, bf16[2,48,1664]{2,1,0:T(8,128)(2,1)S(1)}, u32[]{:S(2)}, u32[]{:S(2)}) collective-permute-start(bf16[2,48,1664]{2,1,0:T(8,128)(2,1)S(1)} %pad_maximum_fusion.2.refs_4_.refs_2_), channel_id=1, source_target_pairs={{0,4},{1,5},{2,6},{3,7},{4,0},{5,1},{6,2},{7,3},{8,12},{9,13},{10,... | collective-permute-start | bytes 958472 | tf_op jit(solution)/shard_map/ppermute | solution.py:71
  20.9 9.7 %collective-permute-start.10 = (bf16[1,48,1536]{2,1,0:T(8,128)(2,1)}, bf16[1,48,1536]{2,1,0:T(8,128)(2,1)S(1)}, u32[]{:S(2)}, u32[]{:S(2)}) collective-permute-start(bf16[1,48,1536]{2,1,0:T(8,128)(2,1)} %bitcast.90), channel_id=1, source_target_pairs={{0,8},{1,9},{2,10},{3,11},{4,12},{5,13},{6,14},{7,15},{8,0},{9,1},... | collective-permute-start | bytes 442376 | tf_op jit(solution)/shard_map/ppermute | solution.py:71
  30.6 32.5 %copy-start.2 = (bf16[2,48,1664]{2,1,0:T(8,128)(2,1)}, bf16[2,48,1664]{2,1,0:T(8,128)(2,1)S(1)}, u32[]{:S(2)}) copy-start(bf16[2,48,1664]{2,1,0:T(8,128)(2,1)S(1)} %collective-permute-done.3.refs_6_.refs_4_) | copy-start | bytes 958468
  30.7 10.4 %collective-permute-start.13 = (bf16[2,48,1536]{2,1,0:T(8,128)(2,1)S(1)}, bf16[2,48,1536]{2,1,0:T(8,128)(2,1)S(1)}, u32[]{:S(2)}, u32[]{:S(2)}) collective-permute-start(bf16[2,48,1536]{2,1,0:T(8,128)(2,1)S(1)} %constant_dynamic-update-slice_fusion), channel_id=1, source_target_pairs={{0,4},{1,5},{2,6},{3,7},{4,0},{5,1},{6,2},{7,3},{8,12},{9,13},{10,... | collective-permute-start | bytes 884744 | tf_op jit(solution)/shard_map/ppermute | solution.py:71
  34.6 28.5 %copy-start.4 = (bf16[2,48,1664]{2,1,0:T(8,128)(2,1)}, bf16[2,48,1664]{2,1,0:T(8,128)(2,1)S(1)}, u32[]{:S(2)}) copy-start(bf16[2,48,1664]{2,1,0:T(8,128)(2,1)S(1)} %collective-permute-done.5.refs_8_.refs_6_) | copy-start | bytes 958468
  34.6 8.3 %collective-permute-start.4 = (bf16[2,48,1664]{2,1,0:T(8,128)(2,1)S(1)}, bf16[2,48,1664]{2,1,0:T(8,128)(2,1)S(1)}, u32[]{:S(2)}, u32[]{:S(2)}) collective-permute-start(bf16[2,48,1664]{2,1,0:T(8,128)(2,1)S(1)} %collective-permute-done.2.refs_5_.refs_3_), channel_id=1, source_target_pairs={{0,2},{1,3},{2,0},{3,1},{4,6},{5,7},{6,4},{7,5},{8,10},{9,11},{10,... | collective-permute-start | bytes 958472 | tf_op jit(solution)/shard_map/ppermute | solution.py:79
  35.1 10.5 %collective-permute-start.6 = (bf16[2,48,1664]{2,1,0:T(8,128)(2,1)S(1)}, bf16[2,48,1664]{2,1,0:T(8,128)(2,1)S(1)}, u32[]{:S(2)}, u32[]{:S(2)}) collective-permute-start(bf16[2,48,1664]{2,1,0:T(8,128)(2,1)S(1)} %collective-permute-done.5.refs_8_.refs_6_), channel_id=1, source_target_pairs={{0,1},{1,0},{2,3},{3,2},{4,5},{5,4},{6,7},{7,6},{8,9},{9,8},{10,11... | collective-permute-start | bytes 958472 | tf_op jit(solution)/shard_map/ppermute | solution.py:79
  35.7 10.6 %collective-permute-start.7 = (bf16[2,48,1664]{2,1,0:T(8,128)(2,1)S(1)}, bf16[2,48,1664]{2,1,0:T(8,128)(2,1)S(1)}, u32[]{:S(2)}, u32[]{:S(2)}) collective-permute-start(bf16[2,48,1664]{2,1,0:T(8,128)(2,1)S(1)} %collective-permute-done.5.refs_8_.refs_6_), channel_id=1, source_target_pairs={{0,2},{1,3},{2,0},{3,1},{4,6},{5,7},{6,4},{7,5},{8,10},{9,11},{10,... | collective-permute-start | bytes 958472 | tf_op jit(solution)/shard_map/ppermute | solution.py:79
  37.2 10.6 %collective-permute-start.11 = (bf16[1,192,768]{2,1,0:T(8,128)(2,1)S(1)}, bf16[1,192,768]{2,1,0:T(8,128)(2,1)S(1)}, u32[]{:S(2)}, u32[]{:S(2)}) collective-permute-start(bf16[1,192,768]{2,1,0:T(8,128)(2,1)S(1)} %copy-done.35), channel_id=1, source_target_pairs={{0,8},{1,9},{2,10},{3,11},{4,12},{5,13},{6,14},{7,15},{24,16},{25,... | collective-permute-start | bytes 884744 | tf_op jit(solution)/shard_map/ppermute | solution.py:90
  42.9 25.6 %copy-start.6 = (bf16[2,48,1664]{2,1,0:T(8,128)(2,1)}, bf16[2,48,1664]{2,1,0:T(8,128)(2,1)S(1)}, u32[]{:S(2)}) copy-start(bf16[2,48,1664]{2,1,0:T(8,128)(2,1)S(1)} %collective-permute-done.4.refs_7_.refs_5_) | copy-start | bytes 958468
  46.3 14.6 %collective-permute-start.14 = (bf16[4,48,1536]{2,1,0:T(8,128)(2,1)S(1)}, bf16[4,48,1536]{2,1,0:T(8,128)(2,1)S(1)}, u32[]{:S(2)}, u32[]{:S(2)}) collective-permute-start(bf16[4,48,1536]{2,1,0:T(8,128)(2,1)S(1)} %pad_maximum_fusion.1.refs_9_.refs_8_), channel_id=1, source_target_pairs={{0,1},{1,0},{2,3},{3,2},{4,5},{5,4},{6,7},{7,6},{8,9},{9,8},{10,11... | collective-permute-start | bytes 1769480 | tf_op jit(solution)/shard_map/ppermute | solution.py:79
  47.9 7.5 %collective-permute-start.12 = (bf16[1,192,768]{2,1,0:T(8,128)(2,1)S(1)}, bf16[1,192,768]{2,1,0:T(8,128)(2,1)S(1)}, u32[]{:S(2)}, u32[]{:S(2)}) collective-permute-start(bf16[1,192,768]{2,1,0:T(8,128)(2,1)S(1)} %broadcast_select_fusion), channel_id=1, source_target_pairs={{0,4},{1,5},{2,6},{3,7},{4,0},{5,1},{6,2},{7,3},{8,12},{9,13},{10,... | collective-permute-start | bytes 884744 | tf_op jit(solution)/shard_map/ppermute | solution.py:71
  48.3 14.8 %collective-permute-start = (bf16[272,768]{1,0:T(8,128)(2,1)S(1)}, bf16[272,768]{1,0:T(8,128)(2,1)S(1)}, u32[]{:S(2)}, u32[]{:S(2)}) collective-permute-start(bf16[272,768]{1,0:T(8,128)(2,1)S(1)} %copy-done.52), channel_id=1, source_target_pairs={{0,16},{16,0},{1,17},{17,1},{2,18},{18,2},{3,19},{19,3},{4,20},{20... | collective-permute-start | bytes 1253384 | tf_op jit(solution)/shard_map/ppermute | solution.py:82
  48.3 14.8 %collective-permute-start.8 = (bf16[2,48,1664]{2,1,0:T(8,128)(2,1)S(1)}, bf16[2,48,1664]{2,1,0:T(8,128)(2,1)S(1)}, u32[]{:S(2)}, u32[]{:S(2)}) collective-permute-start(bf16[2,48,1664]{2,1,0:T(8,128)(2,1)S(1)} %collective-permute-done.6.refs_9_.refs_7_), channel_id=1, source_target_pairs={{0,2},{1,3},{2,0},{3,1},{4,6},{5,7},{6,4},{7,5},{8,10},{9,11},{10,... | collective-permute-start | bytes 958472 | tf_op jit(solution)/shard_map/ppermute | solution.py:79
  48.8 24.9 %collective-permute-start.17 = (bf16[4,48,1536]{2,1,0:T(8,128)(2,1)S(1)}, bf16[4,48,1536]{2,1,0:T(8,128)(2,1)S(1)}, u32[]{:S(2)}, u32[]{:S(2)}) collective-permute-start(bf16[4,48,1536]{2,1,0:T(8,128)(2,1)S(1)} %pad_maximum_fusion.1.refs_9_.refs_8_), channel_id=1, source_target_pairs={{0,2},{1,3},{2,0},{3,1},{4,6},{5,7},{6,4},{7,5},{8,10},{9,11},{10,... | collective-permute-start | bytes 1769480 | tf_op jit(solution)/shard_map/ppermute | solution.py:79
  55.4 24.7 %copy-start.15 = (bf16[1,128,768]{2,1,0:T(8,128)(2,1)S(1)}, bf16[1,128,768]{2,1,0:T(8,128)(2,1)}, u32[]{:S(2)}) copy-start(bf16[1,128,768]{2,1,0:T(8,128)(2,1)} %param.28) | copy-start | bytes 589828
  61.0 11.9 %collective-permute-start.15 = (bf16[2,192,768]{2,1,0:T(8,128)(2,1)S(1)}, bf16[2,192,768]{2,1,0:T(8,128)(2,1)S(1)}, u32[]{:S(2)}, u32[]{:S(2)}) collective-permute-start(bf16[2,192,768]{2,1,0:T(8,128)(2,1)S(1)} %pad_maximum_fusion.refs_4_), channel_id=1, source_target_pairs={{0,1},{1,0},{2,3},{3,2},{4,5},{5,4},{6,7},{7,6},{8,9},{9,8},{10,11... | collective-permute-start | bytes 1769480 | tf_op jit(solution)/shard_map/ppermute | solution.py:79
  69.4 4.3 %collective-permute-start.16 = (bf16[768,384]{1,0:T(8,128)(2,1)S(1)}, bf16[768,384]{1,0:T(8,128)(2,1)S(1)}, u32[]{:S(2)}, u32[]{:S(2)}) collective-permute-start(bf16[768,384]{1,0:T(8,128)(2,1)S(1)} %get-tuple-element.92.refs_7_.refs_8_), channel_id=1, source_target_pairs={{0,16},{16,0},{1,17},{17,1},{2,18},{18,2},{3,19},{19,3},{4,20},{20... | collective-permute-start | bytes 1769480 | tf_op jit(solution)/shard_map/ppermute | solution.py:82
  69.4 9.9 %collective-permute-start.18 = (bf16[4,48,1536]{2,1,0:T(8,128)(2,1)S(1)}, bf16[4,48,1536]{2,1,0:T(8,128)(2,1)S(1)}, u32[]{:S(2)}, u32[]{:S(2)}) collective-permute-start(bf16[4,48,1536]{2,1,0:T(8,128)(2,1)S(1)} %collective-permute-done.14.refs_10_.refs_9_), channel_id=1, source_target_pairs={{0,2},{1,3},{2,0},{3,1},{4,6},{5,7},{6,4},{7,5},{8,10},{9,11},{10,... | collective-permute-start | bytes 1769480 | tf_op jit(solution)/shard_map/ppermute | solution.py:79
  69.9 1.8 collective-permute-start.9
  71.7 18.0 %collective-permute-start.19 = (bf16[2,192,768]{2,1,0:T(8,128)(2,1)S(1)}, bf16[2,192,768]{2,1,0:T(8,128)(2,1)S(1)}, u32[]{:S(2)}, u32[]{:S(2)}) collective-permute-start(bf16[2,192,768]{2,1,0:T(8,128)(2,1)S(1)} %pad_maximum_fusion.refs_4_), channel_id=1, source_target_pairs={{0,2},{1,3},{2,0},{3,1},{4,6},{5,7},{6,4},{7,5},{8,10},{9,11},{10,... | collective-permute-start | bytes 1769480 | tf_op jit(solution)/shard_map/ppermute | solution.py:79
  72.9 19.1 %collective-permute-start.20 = (bf16[2,192,768]{2,1,0:T(8,128)(2,1)S(1)}, bf16[2,192,768]{2,1,0:T(8,128)(2,1)S(1)}, u32[]{:S(2)}, u32[]{:S(2)}) collective-permute-start(bf16[2,192,768]{2,1,0:T(8,128)(2,1)S(1)} %collective-permute-done.15.refs_5_), channel_id=1, source_target_pairs={{0,2},{1,3},{2,0},{3,1},{4,6},{5,7},{6,4},{7,5},{8,10},{9,11},{10,... | collective-permute-start | bytes 1769480 | tf_op jit(solution)/shard_map/ppermute | solution.py:79
  89.6 16.5 %collective-permute-start.33 = (bf16[4,192,768]{2,1,0:T(8,128)(2,1)}, bf16[4,192,768]{2,1,0:T(8,128)(2,1)S(1)}, u32[]{:S(2)}, u32[]{:S(2)}) collective-permute-start(bf16[4,192,768]{2,1,0:T(8,128)(2,1)} %get-tuple-element.121), channel_id=1, source_target_pairs={{0,1},{1,0},{2,3},{3,2},{4,5},{5,4},{6,7},{7,6},{8,9},{9,8},{10,11... | collective-permute-start | bytes 3538952 | tf_op jit(solution)/shard_map/ppermute | solution.py:79
  100.3 7.6 %collective-permute-start.22 = (f32[256,768]{1,0:T(8,128)}, f32[256,768]{1,0:T(8,128)S(1)}, u32[]{:S(2)}, u32[]{:S(2)}) collective-permute-start(f32[256,768]{1,0:T(8,128)} %get-tuple-element.100.refs_5_), channel_id=1, source_target_pairs={{0,16},{16,0},{1,17},{17,1},{2,18},{18,2},{3,19},{19,3},{4,20},{20... | collective-permute-start | bytes 2359304 | tf_op jit(solution)/shard_map/ppermute | solution.py:82
  104.6 22.9 %collective-permute-start.29 = (bf16[8,48,1536]{2,1,0:T(8,128)(2,1)}, bf16[8,48,1536]{2,1,0:T(8,128)(2,1)}, u32[]{:S(2)}, u32[]{:S(2)}) collective-permute-start(bf16[8,48,1536]{2,1,0:T(8,128)(2,1)} %get-tuple-element.118), channel_id=1, source_target_pairs={{0,1},{1,0},{2,3},{3,2},{4,5},{5,4},{6,7},{7,6},{8,9},{9,8},{10,11... | collective-permute-start | bytes 3538952 | tf_op jit(solution)/shard_map/ppermute | solution.py:79
  107.4 16.6 %collective-permute-start.34 = (bf16[2,192,768]{2,1,0:T(8,128)(2,1)}, bf16[2,192,768]{2,1,0:T(8,128)(2,1)}, u32[]{:S(2)}, u32[]{:S(2)}) collective-permute-start(bf16[2,192,768]{2,1,0:T(8,128)(2,1)} %get-tuple-element.184), channel_id=1, source_target_pairs={{0,2},{1,3},{2,0},{3,1},{4,6},{5,7},{6,4},{7,5},{8,10},{9,11},{10,... | collective-permute-start | bytes 1769480 | tf_op jit(solution)/shard_map/ppermute | solution.py:79
  118.5 28.0 %collective-permute-start.23 = (bf16[8,48,1536]{2,1,0:T(8,128)(2,1)}, bf16[8,48,1536]{2,1,0:T(8,128)(2,1)}, u32[]{:S(2)}, u32[]{:S(2)}) collective-permute-start(bf16[8,48,1536]{2,1,0:T(8,128)(2,1)} %get-tuple-element.108), channel_id=1, source_target_pairs={{0,1},{1,0},{2,3},{3,2},{4,5},{5,4},{6,7},{7,6},{8,9},{9,8},{10,11... | collective-permute-start | bytes 3538952 | tf_op jit(solution)/shard_map/ppermute | solution.py:79
  119.2 33.9 %collective-permute-start.21 = (f32[128,768]{1,0:T(8,128)S(1)}, f32[128,768]{1,0:T(8,128)S(1)}, u32[]{:S(2)}, u32[]{:S(2)}) collective-permute-start(f32[128,768]{1,0:T(8,128)S(1)} %get-tuple-element.99), channel_id=1, source_target_pairs={{0,16},{16,0},{1,17},{17,1},{2,18},{18,2},{3,19},{19,3},{4,20},{20... | collective-permute-start | bytes 1179656 | tf_op jit(solution)/shard_map/ppermute | solution.py:82
  125.1 7.5 %collective-permute-start.35 = (bf16[1,192,768]{2,1,0:T(8,128)(2,1)S(1)}, bf16[1,192,768]{2,1,0:T(8,128)(2,1)S(1)}, u32[]{:S(2)}, u32[]{:S(2)}) collective-permute-start(bf16[1,192,768]{2,1,0:T(8,128)(2,1)S(1)} %add_convert_fusion.6), channel_id=1, source_target_pairs={{0,4},{1,5},{2,6},{3,7},{4,0},{5,1},{6,2},{7,3},{8,12},{9,13},{10,... | collective-permute-start | bytes 884744 | tf_op jit(solution)/shard_map/ppermute | solution.py:71
  129.2 22.4 %collective-permute-start.30 = (bf16[4,48,1536]{2,1,0:T(8,128)(2,1)S(1)}, bf16[4,48,1536]{2,1,0:T(8,128)(2,1)S(1)}, u32[]{:S(2)}, u32[]{:S(2)}) collective-permute-start(bf16[4,48,1536]{2,1,0:T(8,128)(2,1)S(1)} %get-tuple-element.188), channel_id=1, source_target_pairs={{0,2},{1,3},{2,0},{3,1},{4,6},{5,7},{6,4},{7,5},{8,10},{9,11},{10,... | collective-permute-start | bytes 1769480 | tf_op jit(solution)/shard_map/ppermute | solution.py:79
  133.6 18.3 %collective-permute-start.36 = (bf16[1,192,768]{2,1,0:T(8,128)(2,1)S(1)}, bf16[1,192,768]{2,1,0:T(8,128)(2,1)S(1)}, u32[]{:S(2)}, u32[]{:S(2)}) collective-permute-start(bf16[1,192,768]{2,1,0:T(8,128)(2,1)S(1)} %fusion), channel_id=1, source_target_pairs={{8,0},{9,1},{10,2},{11,3},{12,4},{13,5},{14,6},{15,7},{16,24},{17,... | collective-permute-start | bytes 884744 | tf_op jit(solution)/shard_map/ppermute | solution.py:90
  151.5 1.8 collective-permute-start.24
  151.8 9.5 %collective-permute-start.31 = (bf16[2,48,1536]{2,1,0:T(8,128)(2,1)S(1)}, bf16[2,48,1536]{2,1,0:T(8,128)(2,1)S(1)}, u32[]{:S(2)}, u32[]{:S(2)}) collective-permute-start(bf16[2,48,1536]{2,1,0:T(8,128)(2,1)S(1)} %get-tuple-element.186), channel_id=1, source_target_pairs={{0,4},{1,5},{2,6},{3,7},{4,0},{5,1},{6,2},{7,3},{8,12},{9,13},{10,... | collective-permute-start | bytes 884744 | tf_op jit(solution)/shard_map/ppermute | solution.py:71
  155.9 1.4 collective-permute-start.38
  156.5 7.0 %collective-permute-start.37 = (f32[192,384]{1,0:T(8,128)S(1)}, f32[192,384]{1,0:T(8,128)S(1)}, u32[]{:S(2)}, u32[]{:S(2)}) collective-permute-start(f32[192,384]{1,0:T(8,128)S(1)} %dynamic-slice_bitcast_fusion), channel_id=1, source_target_pairs={{0,16},{16,0},{1,17},{17,1},{2,18},{18,2},{3,19},{19,3},{4,20},{20... | collective-permute-start | bytes 884744 | tf_op jit(solution)/shard_map/ppermute | solution.py:82
  156.6 16.1 %collective-permute-start.25 = (bf16[4,48,1536]{2,1,0:T(8,128)(2,1)S(1)}, bf16[4,48,1536]{2,1,0:T(8,128)(2,1)S(1)}, u32[]{:S(2)}, u32[]{:S(2)}) collective-permute-start(bf16[4,48,1536]{2,1,0:T(8,128)(2,1)S(1)} %get-tuple-element.192), channel_id=1, source_target_pairs={{0,2},{1,3},{2,0},{3,1},{4,6},{5,7},{6,4},{7,5},{8,10},{9,11},{10,... | collective-permute-start | bytes 1769480 | tf_op jit(solution)/shard_map/ppermute | solution.py:79
  157.4 4.6 %collective-permute-start.39 = (f32[16,768]{1,0:T(8,128)S(1)}, f32[16,768]{1,0:T(8,128)S(1)}, u32[]{:S(2)}, u32[]{:S(2)}) collective-permute-start(f32[16,768]{1,0:T(8,128)S(1)} %add.217), channel_id=1, source_target_pairs={{0,1},{1,0},{2,3},{3,2},{4,5},{5,4},{6,7},{7,6},{8,9},{9,8},{10,11... | collective-permute-start | bytes 147464 | tf_op jit(solution)/shard_map/ppermute | solution.py:71
  161.3 9.5 %collective-permute-start.32 = (bf16[1,48,1536]{2,1,0:T(8,128)(2,1)S(1)}, bf16[1,48,1536]{2,1,0:T(8,128)(2,1)S(1)}, u32[]{:S(2)}, u32[]{:S(2)}) collective-permute-start(bf16[1,48,1536]{2,1,0:T(8,128)(2,1)S(1)} %add_convert_fusion.12), channel_id=1, source_target_pairs={{0,8},{1,9},{2,10},{3,11},{4,12},{5,13},{6,14},{7,15},{8,0},{9,1},... | collective-permute-start | bytes 442376 | tf_op jit(solution)/shard_map/ppermute | solution.py:71
  162.0 5.0 %collective-permute-start.40 = (f32[16,768]{1,0:T(8,128)S(1)}, f32[16,768]{1,0:T(8,128)S(1)}, u32[]{:S(2)}, u32[]{:S(2)}) collective-permute-start(f32[16,768]{1,0:T(8,128)S(1)} %add.218), channel_id=1, source_target_pairs={{0,2},{1,3},{2,0},{3,1},{4,6},{5,7},{6,4},{7,5},{8,10},{9,11},{10,... | collective-permute-start | bytes 147464 | tf_op jit(solution)/shard_map/ppermute | solution.py:71
  167.0 5.0 %collective-permute-start.41 = (f32[16,768]{1,0:T(8,128)S(1)}, f32[16,768]{1,0:T(8,128)S(1)}, u32[]{:S(2)}, u32[]{:S(2)}) collective-permute-start(f32[16,768]{1,0:T(8,128)S(1)} %add.219), channel_id=1, source_target_pairs={{0,4},{1,5},{2,6},{3,7},{4,0},{5,1},{6,2},{7,3},{8,12},{9,13},{10,... | collective-permute-start | bytes 147464 | tf_op jit(solution)/shard_map/ppermute | solution.py:71
  172.1 6.4 %collective-permute-start.42 = (f32[16,768]{1,0:T(8,128)S(1)}, f32[16,768]{1,0:T(8,128)S(1)}, u32[]{:S(2)}, u32[]{:S(2)}) collective-permute-start(f32[16,768]{1,0:T(8,128)S(1)} %add.220), channel_id=1, source_target_pairs={{0,8},{1,9},{2,10},{3,11},{4,12},{5,13},{6,14},{7,15},{8,0},{9,1},... | collective-permute-start | bytes 147464 | tf_op jit(solution)/shard_map/ppermute | solution.py:71
  172.9 10.9 %collective-permute-start.26 = (bf16[2,48,1536]{2,1,0:T(8,128)(2,1)S(1)}, bf16[2,48,1536]{2,1,0:T(8,128)(2,1)S(1)}, u32[]{:S(2)}, u32[]{:S(2)}) collective-permute-start(bf16[2,48,1536]{2,1,0:T(8,128)(2,1)S(1)} %get-tuple-element.190), channel_id=1, source_target_pairs={{0,4},{1,5},{2,6},{3,7},{4,0},{5,1},{6,2},{7,3},{8,12},{9,13},{10,... | collective-permute-start | bytes 884744 | tf_op jit(solution)/shard_map/ppermute | solution.py:71
  183.8 9.2 %collective-permute-start.27 = (bf16[1,48,1536]{2,1,0:T(8,128)(2,1)S(1)}, bf16[1,48,1536]{2,1,0:T(8,128)(2,1)S(1)}, u32[]{:S(2)}, u32[]{:S(2)}) collective-permute-start(bf16[1,48,1536]{2,1,0:T(8,128)(2,1)S(1)} %add_convert_fusion.13), channel_id=1, source_target_pairs={{0,8},{1,9},{2,10},{3,11},{4,12},{5,13},{6,14},{7,15},{8,0},{9,1},... | collective-permute-start | bytes 442376 | tf_op jit(solution)/shard_map/ppermute | solution.py:71
  193.8 1.3 collective-permute-start.28
  (48 other events, 350.4 us)

commit v3 on v2

--- a/solution.py
+++ b/solution.py
@@ -162,13 +162,6 @@
     return whole.reshape(count * rows, width)
 
 
-def sum_all(grid, value):
-    value = value + grid.swap_core(value)
-    for bit in range(grid.top_bit + 1):
-        value = value + grid.swap(value, bit)
-    return value
-
-
 def adamw(master, first, second, gradient, rate):
     first_new = beta_one * first + (1.0 - beta_one) * gradient
     second_new = beta_two * second + (1.0 - beta_two) * gradient * gradient
@@ -181,7 +174,7 @@
 
 
 RAW, HELD, FETCH, PUT, SCALAR = "raw", "held", "fetch", "put", "scalar"
-SPACES = {RAW: pltpu.HBM, HELD: pltpu.VMEM, FETCH: pltpu.HBM, PUT: pltpu.HBM, SCALAR: pltpu.SMEM}
+SPACES = {RAW: pl.ANY, HELD: pltpu.VMEM, FETCH: pl.ANY, PUT: pl.ANY, SCALAR: pltpu.SMEM}
 
 
 def shaped(shape, dtype):
@@ -244,8 +237,8 @@
         scratch_shapes=scratch
         + rooms
         + ([pltpu.SemaphoreType.DMA((len(moved),))] if moved else []),
-        compiler_params=pltpu.CompilerParams(vmem_limit_bytes=(60 if name == "pack_blocks" else 48) << 20),
-        cost_estimate=pl.CostEstimate(flops=int({'pack_blocks': 1.5, 'attend': 4.3, 'grow': 9.5, 'shrink_back': 6.4, 'expand_grads': 4.3, 'attend_back': 8.1, 'joint_back': 2.9, 'finish': 2.6}[name] * 1150000000), bytes_accessed=1, transcendentals=0),
+        compiler_params=pltpu.CompilerParams(vmem_limit_bytes=(60 if name == "pack_blocks" else 28) << 20),
+        cost_estimate=pl.CostEstimate(flops=int({'pack_blocks': 1.5, 'attend': 4.3, 'grow': 9.5, 'shrink_back': 6.4, 'expand_grads': 4.3, 'attend_back': 9.0, 'finish': 2.6}[name] * 1150000000), bytes_accessed=1, transcendentals=0),
     )(*operands)
 
 
@@ -639,16 +632,16 @@
     )
 
 
-def shrink_back(meta, cot, item_got, slope, shrink, expand):
+def shrink_back(meta, cot, item_got, slope, active, shrink, expand):
     tokens_rows, width = cot.shape
     rows = 2 * tokens_rows
     hidden = expand.layout.width
 
-    def body(meta_ref, cot_ref, item_ref, slope_ref, *rest):
+    def body(meta_ref, cot_ref, item_ref, slope_ref, active_ref, *rest):
         shrink_pieces = rest[: len(shrink.arrays)]
         rest = rest[len(shrink.arrays) :]
         expand_pieces = rest[: len(expand.arrays)]
-        hidden_ref, part_ref, *scratch, upstream = rest[len(expand.arrays) :]
+        hidden_ref, part_ref, second_ref, other_ref, *scratch, upstream = rest[len(expand.arrays) :]
         first = Loading(shrink, shrink_pieces, meta_ref, scratch[:3])
         second = Loading(expand, expand_pieces, meta_ref, scratch[3:])
         upstream[:tokens_rows] = cot_ref.ready()[...]
@@ -659,73 +652,69 @@
             spot = slice(at, at + step)
             value = times_back(upstream[...], mat[spot])
             hidden_ref[:, spot] = (value * slope_ref[:, spot]).astype(half_type)
+        for ref, at in ((second_ref, 0), (other_ref, tokens_rows)):
+            ref[...] = matmul(active_ref[at : at + tokens_rows], mat[...])
         other = second.ready()
         part_ref[...] = times_back(hidden_ref[...], other[...])
 
     return call(
         body,
         "shrink_back",
-        (meta, cot, item_got, slope, *shrink.arrays, *expand.arrays),
-        (SCALAR, FETCH, FETCH, HELD) + (RAW,) * (len(shrink.arrays) + len(expand.arrays)),
-        (shaped((rows, hidden), half_type), shaped((rows, width), wide)),
-        (HELD, PUT),
+        (meta, cot, item_got, slope, active, *shrink.arrays, *expand.arrays),
+        (SCALAR, FETCH, FETCH, HELD, HELD) + (RAW,) * (len(shrink.arrays) + len(expand.arrays)),
+        (
+            shaped((rows, hidden), half_type),
+            shaped((rows, width), wide),
+            shaped((tokens_rows, width), wide),
+            shaped((tokens_rows, width), wide),
+        ),
+        (HELD, PUT, HELD, PUT),
         (*shrink.scratch(), *expand.scratch(), pltpu.VMEM((rows, width), half_type)),
     )
 
 
-def expand_grads(meta, active, normed_two, back_hidden, shrink, quarters):
-    rows, hidden = active.shape
+def expand_grads(meta, normed_two, back_hidden, quarters):
     width = normed_two.shape[1]
-    tokens_rows = rows // 2
+    hidden = back_hidden.shape[1]
     shapes = quarters.shapes()
 
-    def body(meta_ref, active_ref, normed_ref, hidden_ref, *rest):
-        pieces = rest[: len(shrink.arrays)]
-        rest = rest[len(shrink.arrays) :]
-        own_ref, other_ref, bias_ref = rest[:3]
-        grads = rest[3 : 3 + len(shapes)]
-        scratch = rest[3 + len(shapes) :]
-        loading = Loading(shrink, pieces, meta_ref, scratch[:3])
-        storing = Storing(quarters, grads, meta_ref, scratch[3:])
+    def body(meta_ref, normed_ref, hidden_ref, bias_ref, *rest):
+        storing = Storing(quarters, rest[: len(shapes)], meta_ref, rest[len(shapes) :])
         step = 384
         for at in range(0, hidden, step):
             spot = slice(at, at + step)
             storing.put(0, spot, outer_sum(normed_ref[...], hidden_ref[:, spot]))
         storing.send()
         bias_ref[...] = jnp.sum(hidden_ref[...].astype(wide), axis=0, keepdims=True)
-        mat = loading.ready()
-        for ref, at in ((own_ref, 0), (other_ref, tokens_rows)):
-            ref[...] = matmul(active_ref[at : at + tokens_rows], mat[...])
         storing.wait()
 
-    outs = (
-        shaped((tokens_rows, width), wide),
-        shaped((tokens_rows, width), wide),
-        shaped((1, hidden), wide),
-    ) + tuple(shapes)
     return call(
         body,
         "expand_grads",
-        (meta, active, normed_two, back_hidden, *shrink.arrays),
-        (SCALAR, HELD, HELD, HELD) + (RAW,) * len(shrink.arrays),
-        outs,
-        (HELD, PUT, HELD) + (RAW,) * len(shapes),
-        (*shrink.scratch(), *quarters.scratch()),
-    )
-
-
-def attend_back(meta, small, middle, cot, item_got, part, part_got, mixed, output, output_got, normed, projected, attention, quarters):
+        (meta, normed_two, back_hidden),
+        (SCALAR, HELD, HELD),
+        (shaped((1, hidden), wide),) + tuple(shapes),
+        (HELD,) + (RAW,) * len(shapes),
+        quarters.scratch(),
+    )
+
+
+def attend_back(meta, small, middle, tokens, cot, item_got, part, part_got, mixed, output, output_got, normed, projected, attention, expand_bias, joint, quarters):
     rows, width = middle.shape
     half = width // 2
     tokens_rows = rows // 2
     pairs = half // 128
     shapes = quarters.shapes()
 
-    def body(meta_ref, small_ref, middle_ref, cot_ref, item_ref, part_ref, part_got_ref, mixed_ref, output_ref, output_got_ref, normed_ref, projected_ref, attention_ref, back_middle_ref, back_projected_ref, sums_ref, *rest):
-        grads = rest[: len(shapes)]
-        *scratch, branch = rest[len(shapes) :]
+    def body(meta_ref, small_ref, middle_ref, tokens_ref, cot_ref, item_ref, part_ref, part_got_ref, mixed_ref, output_ref, output_got_ref, normed_ref, projected_ref, attention_ref, bias_ref, *rest):
+        pieces = rest[: len(joint.arrays)]
+        rest = rest[len(joint.arrays) :]
+        back_middle_ref, own_ref, other_ref = rest[:3]
+        grads = rest[3 : 3 + len(shapes)]
+        *scratch, branch, back_projected_ref, sums_ref = rest[3 + len(shapes) :]
         core = meta_ref[1]
-        storing = Storing(quarters, grads, meta_ref, scratch)
+        loading = Loading(joint, pieces, meta_ref, scratch[:3])
+        storing = Storing(quarters, grads, meta_ref, scratch[3:])
         mine = pl.ds(pl.multiple_of(core * half, 128), half)
         yours = pl.ds(pl.multiple_of((1 - core) * half, 128), half)
         gain = jnp.zeros((1, width), wide)
@@ -787,73 +776,66 @@
         for part_at in range(3):
             spot = slice(part_at * half, (part_at + 1) * half)
             storing.put(0, spot, outer_sum(normed_ref[...], back_projected_ref[:, spot]))
+        mat = loading.ready()
+        gain = jnp.zeros((1, width), wide)
+        shift = jnp.zeros((1, width), wide)
+        sides = (tokens_ref.ready()[...], item_ref.ready()[:tokens_rows])
+        for item, (side, ref) in enumerate(zip(sides, (own_ref, other_ref))):
+            take = slice(item * tokens_rows, (item + 1) * tokens_rows)
+            back = times_back(back_projected_ref[take], mat[:, : 3 * half])
+            ref[...] = back
+            unit, _ = norm_parts(side.astype(wide))
+            gain = gain + jnp.sum(back * unit, axis=0, keepdims=True)
+            shift = shift + jnp.sum(back, axis=0, keepdims=True)
+        sums_ref[0:1] = gain
+        sums_ref[2:3] = shift
+        count = bias_ref.shape[1] // width
+        for at in range(count):
+            sums_ref[pl.ds(8 + core * count + at, 1)] = bias_ref[:, at * width : (at + 1) * width]
+        storing.put(0, slice(4 * half, 4 * half + 128), sums_ref[...].T)
         storing.send()
         storing.wait()
 
     outs = (
         shaped((tokens_rows, width), wide),
-        shaped((rows, 3 * half), half_type),
-        shaped((16, width), wide),
+        shaped((tokens_rows, width), wide),
+        shaped((tokens_rows, width), wide),
     ) + tuple(shapes)
     return call(
         body,
         "attend_back",
-        (meta, small, middle, cot, item_got, part, part_got, mixed, output, output_got, normed, projected, attention),
-        (SCALAR, HELD, HELD, FETCH, FETCH, FETCH, FETCH, HELD, FETCH, FETCH, HELD, HELD, HELD),
+        (meta, small, middle, tokens, cot, item_got, part, part_got, mixed, output, output_got, normed, projected, attention, expand_bias, *joint.arrays),
+        (SCALAR, HELD, HELD, FETCH, FETCH, FETCH, FETCH, FETCH, HELD, FETCH, FETCH, HELD, HELD, HELD, HELD) + (RAW,) * len(joint.arrays),
         outs,
-        (HELD,) * 3 + (RAW,) * len(shapes),
-        (*quarters.scratch(), pltpu.VMEM((rows, width), half_type)),
-    )
-
-
-def joint_back(meta, back_projected, joint, width):
-    rows, depth = back_projected.shape
-    tokens_rows = rows // 2
-
-    def body(meta_ref, back_ref, *rest):
-        pieces = rest[: len(joint.arrays)]
-        own_ref, other_ref, *scratch = rest[len(joint.arrays) :]
-        mat = Loading(joint, pieces, meta_ref, scratch).ready()
-        other_ref[...] = times_back(back_ref[tokens_rows:], mat[:, :depth])
-        own_ref[...] = times_back(back_ref[:tokens_rows], mat[:, :depth])
-
-    return call(
-        body,
-        "joint_back",
-        (meta, back_projected, *joint.arrays),
-        (SCALAR, HELD) + (RAW,) * len(joint.arrays),
-        (shaped((tokens_rows, width), wide), shaped((tokens_rows, width), wide)),
-        (HELD, PUT),
-        joint.scratch(),
-    )
-
-
-def finish(meta, small, tokens, middle, second, second_got, back_middle, back_one, back_got, sums, expand_bias):
+        (HELD, HELD, PUT) + (RAW,) * len(shapes),
+        (
+            *joint.scratch(),
+            *quarters.scratch(),
+            pltpu.VMEM((rows, width), half_type),
+            pltpu.VMEM((rows, 3 * half), half_type),
+            pltpu.VMEM((128, width), wide),
+        ),
+    )
+
+
+def finish(meta, small, tokens, middle, second, second_got, back_middle, back_one, back_got):
     tokens_rows, width = tokens.shape
-    hidden = expand_bias.shape[1]
-
-    def body(meta_ref, small_ref, own_ref, middle_ref, second_ref, second_got_ref, back_middle_ref, back_ref, back_got_ref, sums_ref, bias_ref, result_ref, input_ref, total_ref):
-        core = meta_ref[1]
+
+    def body(meta_ref, small_ref, own_ref, middle_ref, second_ref, second_got_ref, back_middle_ref, back_ref, back_got_ref, result_ref, input_ref):
         result_ref[...] = middle_ref[:tokens_rows] + (
             second_ref[...] + second_got_ref.ready()[...] + small_ref[7:8]
         )
         unit, scale = norm_parts(own_ref.ready()[...].astype(wide))
         back = back_ref[...] + back_got_ref.ready()[...]
         input_ref[...] = back_middle_ref[...] + norm_back(unit, scale, small_ref[0:1], back)
-        total_ref[...] = sums_ref[...]
-        total_ref[0:1] = jnp.sum(back * unit, axis=0, keepdims=True)
-        total_ref[2:3] = jnp.sum(back, axis=0, keepdims=True)
-        count = hidden // width
-        for at in range(count):
-            total_ref[pl.ds(8 + core * count + at, 1)] = bias_ref[:, at * width : (at + 1) * width]
 
     return call(
         body,
         "finish",
-        (meta, small, tokens, middle, second, second_got, back_middle, back_one, back_got, sums, expand_bias),
-        (SCALAR, HELD, FETCH, HELD, HELD, FETCH, HELD, HELD, FETCH, HELD, HELD),
-        (shaped((tokens_rows, width), wide), shaped((tokens_rows, width), wide), shaped((16, width), wide)),
-        (PUT, PUT, PUT),
+        (meta, small, tokens, middle, second, second_got, back_middle, back_one, back_got),
+        (SCALAR, HELD, FETCH, HELD, HELD, FETCH, HELD, HELD, FETCH),
+        (shaped((tokens_rows, width), wide), shaped((tokens_rows, width), wide)),
+        (PUT, PUT),
         (),
     )
 
@@ -911,7 +893,7 @@
     three.high()
     one.low(True)
     one_near = one.first(0)
-    two.value = after(two.value, one_near[0][1][1], one_near[1][1])
+    two.value = after(two.value, one_near[0][1][1], one_near[1][1], one.start[1][1])
     two.low(False)
     three.low(False)
     one.start[1] = (one.start[1][0], after(one.start[1][1], one_near[0][1][1], one_near[1][1]))
@@ -928,50 +910,52 @@
     lasting = (*grid.low_bits[::-1], grid.top_bit)
     shrink_quarters = Parts(grid, shrink.layout, lasting[:-1])
     expand_quarters = Parts(grid, expand.layout, lasting)
-    joint_quarters = Parts(grid, Layout(size, joint.layout.rows, 4 * half), lasting)
+    joint_quarters = Parts(grid, Layout(size, joint.layout.rows, 4 * half + 128), lasting)
 
     normed, projected, attention, attended, output, small = attend(
         meta, lengths_own, tokens_own, item_got, joint
     )
-    attended_got = after(grid.swap_core(attended), three_all[0][1][1])
+    attended_got = after(
+        grid.swap_core(after(attended, expand.arrays[-1])), three_all[0][1][1], three_all[1][1]
+    )
     output_got = grid.swap_core(output)
     middle, normed_two, active, slope, mixed, *shrink_grads = grow(
         meta, small, tokens_own, cot, item_got, attended, attended_got,
         output, output_got, expand, shrink_quarters,
     )
     shrink_sum = third_sum(grid, *shrink_quarters.second(shrink_quarters.first(shrink_grads)), owned=True)
-    back_hidden, part = shrink_back(meta, cot, item_got, slope, shrink, expand)
+    back_hidden, part, second, second_other = shrink_back(
+        meta, cot, item_got, slope, active, shrink, expand
+    )
     part_got = grid.swap_core(part)
-    second, second_other, expand_bias, *expand_grad = expand_grads(
-        meta, active, normed_two, back_hidden, shrink, expand_quarters
-    )
+    expand_bias, *expand_grad = expand_grads(meta, normed_two, back_hidden, expand_quarters)
     expand_sum = third_sum(grid, *expand_quarters.second(expand_quarters.first(expand_grad)))
     second_got = grid.swap_core(second_other)
-    back_middle, back_projected, sums, *joint_grad = attend_back(
-        meta, small, middle, cot, item_got, part, part_got, mixed, output, output_got,
-        normed, projected, attention, joint_quarters,
+    back_middle, back_one, back_other, *joint_grad = attend_back(
+        meta, small, middle, tokens_own, cot, item_got, part, part_got, mixed, output, output_got,
+        normed, projected, attention, expand_bias, joint, joint_quarters,
     )
     joint_first = joint_quarters.first(joint_grad)
     joint_sum_all = third_sum(grid, *joint_quarters.second(joint_first))
-    back_one, back_other = joint_back(meta, after(back_projected, joint_first[0]), joint, width)
     back_got = grid.swap_core(back_other)
-    result, input_grad, small_grads = finish(
-        meta, small, tokens_own, middle, second, second_got, back_middle, back_one, back_got,
-        sums, expand_bias,
-    )
-    small_sum = sum_all(grid, small_grads)
-    own = norm_gains.shape[2]
-    small_own = lax.dynamic_slice_in_dim(small_sum, grid.index * own, own, axis=1)
+    result, input_grad = finish(
+        meta, small, tokens_own, middle, second, second_got, back_middle, back_one, back_got
+    )
     gains_count = norm_gains.shape[1]
 
     third = [joint_sum_all[:, part_at * half : (part_at + 1) * half] for part_at in range(3)]
-    joint_got = grid.swap_core(jnp.where(core == 0, third[2], third[0]))
+    small_part = joint_sum_all[:, 4 * half :]
+    got = grid.swap_core(
+        jnp.concatenate([jnp.where(core == 0, third[2], third[0]), small_part], axis=1)
+    )
+    joint_got = got[:, :half]
+    small_own = (small_part + got[:, half:])[:, :small_rows].T
     joint_sum = jnp.where(
         core == 0,
         jnp.concatenate([third[0], joint_got, third[1]], axis=1),
         jnp.concatenate([third[1], joint_got, third[2]], axis=1),
     )
-    output_sum = joint_sum_all[:, 3 * half :]
+    output_sum = joint_sum_all[:, 3 * half : 4 * half]
     owner = grid.top == core
     side = shrink_sum.shape[1] // 2
     shrink_send = lax.dynamic_slice_in_dim(shrink_sum, (1 - core) * side, side, axis=1)

time: 197 us -> 189 us (0.959)
  Pallas kernels: 41.1 us -> 35.7 us
  other arithmetic: 16.2 us -> 12.9 us
    ppermute x14 -> x10, waiting for transfers between devices: 44.7 us -> 38 us  [swap(): lax.ppermute(value, 'fsdp', [(i, i ^ 1 << bit) for i in range(self.size)])]
    pallas_call x8 -> x7, Pallas kernels: 41.1 us -> 35.7 us  [call(): pl.pallas_call(whole, name=name, out_shape=tuple(outs), in_specs=[pl.Bloc...]
    ppermute x18, waiting for transfers between devices: 37.8 us -> 43.2 us  [swap_step(): return lax.ppermute(value, ('dp', 'fsdp'), pairs)]
    ppermute x14 -> x10, starting transfers between devices: 20.1 us -> 15.5 us  [swap(): lax.ppermute(value, 'fsdp', [(i, i ^ 1 << bit) for i in range(self.size)])]
    ppermute x18, starting transfers between devices: 17 us -> 20.8 us  [swap_step(): return lax.ppermute(value, ('dp', 'fsdp'), pairs)]
    ppermute x2, waiting for transfers between devices: 0.01 us -> 2.62 us  [swap_owned(): return lax.ppermute(value, ('dp', 'fsdp'), pairs)]
    unnamed x111 -> x107, local copies, waits for them, and re-layouts: 10.9 us -> 10.5 us
  transfers between devices with their start and end apart: 43 -> 38, of which waited for: 26 -> 22; matrix products, arithmetic and copies ran while one was open for 9% -> 6% of each run, Pallas kernels for 19% -> 17%
where the time goes in v3:
time: 189 us
  waiting for transfers between devices  84.9 us (45%)
  starting transfers between devices  42.3 us (22%)
  Pallas kernels  35.7 us (19%)
  other arithmetic  12.9 us (7%)
  local copies, waits for them, and re-layouts  11.4 us (6%)
    ppermute x18, waiting for transfers between devices, swap_step(): return lax.ppermute(value, ('dp', 'fsdp'), pairs)  43.2 us
    ppermute x10, waiting for transfers between devices, swap(): lax.ppermute(value, 'fsdp', [(i, i ^ 1 << bit) for i in range(self.size)])  38 us
    pallas_call x7, Pallas kernels, call(): pl.pallas_call(whole, name=name, out_shape=tuple(outs), in_specs=[pl.Bloc...  35.7 us
    ppermute x18, starting transfers between devices, swap_step(): return lax.ppermute(value, ('dp', 'fsdp'), pairs)  20.8 us
    ppermute x10, starting transfers between devices, swap(): lax.ppermute(value, 'fsdp', [(i, i ^ 1 << bit) for i in range(self.size)])  15.5 us
    unnamed x107, local copies, waits for them, and re-layouts  10.5 us
    convert_element_type x9, other arithmetic, join(): return (keep.astype(wide) + got.astype(wide)).astype(half_type)  5.64 us
    ppermute x2, starting transfers between devices, swap_owned(): return lax.ppermute(value, ('dp', 'fsdp'), pairs)  4.8 us
  transfers between devices with their start and end apart: 38, of which 22 were waited for; matrix products, arithmetic and copies ran while one was open for 6% of the time, Pallas kernels for 17%

profile of v3, /device:TPU:0, one launch (start us, length us, event | category | flops | bytes accessed | tf_op | source)
XLA Modules:
  0.0 188.5 jit_solution(9568236885600683520)
XLA Ops:
  1.3 2.9 %pack_blocks.1 = (bf16[48,1664]{1,0:T(8,128)(2,1)}, bf16[48,1536]{1,0:T(8,128)(2,1)}, bf16[272,768]{1,0:T(8,128)(2,1)}) custom-call(s32[2]{0:T(128)} %pad_add_fusion.refs_0_, s32[2]{0:T(128)} %bitcast.84, bf16[128,768]{1,0:T(8,128)(2,1)} %bitcast.79, bf16[128,768]{1,0:T(8,128)(2,1)} %bitcast.75, bf16[48,2304]{1,0:T(8,128)(2,1)} %bitcast.93, ...), custom_call_target="tpu_custom_call" | custom-call | flops 1724999936 | bytes 1 | tf_op jit(solution)/shard_map/pack_blocks/pallas_call | solution.py:231
  4.2 4.1 %collective-permute-start.1 = (bf16[1,48,1664]{2,1,0:T(8,128)(2,1)}, bf16[1,48,1664]{2,1,0:T(8,128)(2,1)S(1)}, u32[]{:S(2)}, u32[]{:S(2)}) collective-permute-start(bf16[1,48,1664]{2,1,0:T(8,128)(2,1)} %bitcast.87), channel_id=1, source_target_pairs={{0,8},{1,9},{2,10},{3,11},{4,12},{5,13},{6,14},{7,15},{8,0},{9,1},... | collective-permute-start | bytes 479240 | tf_op jit(solution)/shard_map/ppermute | solution.py:71
  8.3 7.7 %collective-permute-done.1 = bf16[1,48,1664]{2,1,0:T(8,128)(2,1)S(1)} collective-permute-done((bf16[1,48,1664]{2,1,0:T(8,128)(2,1)}, bf16[1,48,1664]{2,1,0:T(8,128)(2,1)S(1)}, u32[]{:S(2)}, u32[]{:S(2)}) %collective-permute-start.1) | collective-permute-done | bytes 159776 | tf_op jit(solution)/shard_map/ppermute | solution.py:71
  17.0 1.6 collective-permute-start.2
  18.6 1.5 collective-permute-start.3
  20.9 3.3 %collective-permute-start.9 = (bf16[1,48,1536]{2,1,0:T(8,128)(2,1)}, bf16[1,48,1536]{2,1,0:T(8,128)(2,1)S(1)}, u32[]{:S(2)}, u32[]{:S(2)}) collective-permute-start(bf16[1,48,1536]{2,1,0:T(8,128)(2,1)} %bitcast.89), channel_id=1, source_target_pairs={{0,8},{1,9},{2,10},{3,11},{4,12},{5,13},{6,14},{7,15},{8,0},{9,1},... | collective-permute-start | bytes 442376 | tf_op jit(solution)/shard_map/ppermute | solution.py:71
  25.1 5.4 %collective-permute-done.9 = bf16[1,48,1536]{2,1,0:T(8,128)(2,1)S(1)} collective-permute-done((bf16[1,48,1536]{2,1,0:T(8,128)(2,1)}, bf16[1,48,1536]{2,1,0:T(8,128)(2,1)S(1)}, u32[]{:S(2)}, u32[]{:S(2)}) %collective-permute-start.9) | collective-permute-done | bytes 147488 | tf_op jit(solution)/shard_map/ppermute | solution.py:71
  31.2 3.4 %collective-permute-start.10 = (bf16[2,48,1536]{2,1,0:T(8,128)(2,1)S(1)}, bf16[2,48,1536]{2,1,0:T(8,128)(2,1)S(1)}, u32[]{:S(2)}, u32[]{:S(2)}) collective-permute-start(bf16[2,48,1536]{2,1,0:T(8,128)(2,1)S(1)} %constant_dynamic-update-slice_fusion), channel_id=1, source_target_pairs={{0,4},{1,5},{2,6},{3,7},{4,0},{5,1},{6,2},{7,3},{8,12},{9,13},{10,... | collective-permute-start | bytes 884744 | tf_op jit(solution)/shard_map/ppermute | solution.py:71
  35.7 1.5 collective-permute-start.4
  37.2 3.5 %collective-permute-start.14 = (bf16[1,192,768]{2,1,0:T(8,128)(2,1)S(1)}, bf16[1,192,768]{2,1,0:T(8,128)(2,1)S(1)}, u32[]{:S(2)}, u32[]{:S(2)}) collective-permute-start(bf16[1,192,768]{2,1,0:T(8,128)(2,1)S(1)} %copy-done.32), channel_id=1, source_target_pairs={{0,8},{1,9},{2,10},{3,11},{4,12},{5,13},{6,14},{7,15},{24,16},{25,... | collective-permute-start | bytes 884744 | tf_op jit(solution)/shard_map/ppermute | solution.py:90
  41.1 1.8 collective-permute-done.7.refs_10_.refs_21_
  42.9 2.7 %collective-permute-done.6.refs_9_.refs_20_ = bf16[2,48,1664]{2,1,0:T(8,128)(2,1)S(1)} collective-permute-done((bf16[2,48,1664]{2,1,0:T(8,128)(2,1)S(1)}, bf16[2,48,1664]{2,1,0:T(8,128)(2,1)S(1)}, u32[]{:S(2)}, u32[]{:S(2)}) %collective-permute-start.6) | collective-permute-done | bytes 319520 | tf_op jit(solution)/shard_map/ppermute | solution.py:79
  46.3 1.5 collective-permute-start.11
  48.8 1.5 collective-permute-start.19
  50.3 5.0 %collective-permute-done.15 = bf16[1,192,768]{2,1,0:T(8,128)(2,1)S(1)} collective-permute-done((bf16[1,192,768]{2,1,0:T(8,128)(2,1)S(1)}, bf16[1,192,768]{2,1,0:T(8,128)(2,1)S(1)}, u32[]{:S(2)}, u32[]{:S(2)}) %collective-permute-start.15) | collective-permute-done | bytes 294944 | tf_op jit(solution)/shard_map/ppermute | solution.py:71
  55.4 5.5 %collective-permute-done.11.refs_10_ = bf16[4,48,1536]{2,1,0:T(8,128)(2,1)S(1)} collective-permute-done((bf16[4,48,1536]{2,1,0:T(8,128)(2,1)S(1)}, bf16[4,48,1536]{2,1,0:T(8,128)(2,1)S(1)}, u32[]{:S(2)}, u32[]{:S(2)}) %collective-permute-start.11) | collective-permute-done | bytes 589856 | tf_op jit(solution)/shard_map/ppermute | solution.py:79
  61.0 1.5 collective-permute-start.16
  63.1 1.5 collective-permute-start.12
  64.6 4.3 %attend.1 = (bf16[256,768]{1,0:T(8,128)(2,1)S(1)}, bf16[256,1152]{1,0:T(8,128)(2,1)S(1)}, f32[6,256,128]{2,1,0:T(8,128)S(1)}, bf16[256,384]{1,0:T(8,128)(2,1)S(1...) custom-call(s32[2]{0:T(128)S(1)} %copy-done.15, s32[2]{0:T(128)S(1)} %bitcast.85, bf16[128,768]{1,0:T(8,128)(2,1)S(1)} %bitcast.80, ...), custom_call_target="tpu_custom_call" | custom-call | flops 4944999936 | bytes 1 | tf_op jit(solution)/shard_map/attend/pallas_call | solution.py:231
  69.0 14.8 %collective-permute-done.12.refs_12_ = bf16[4,48,1536]{2,1,0:T(8,128)(2,1)S(1)} collective-permute-done((bf16[4,48,1536]{2,1,0:T(8,128)(2,1)S(1)}, bf16[4,48,1536]{2,1,0:T(8,128)(2,1)S(1)}, u32[]{:S(2)}, u32[]{:S(2)}) %collective-permute-start.12) | collective-permute-done | bytes 589856 | tf_op jit(solution)/shard_map/ppermute | solution.py:79
  85.8 7.5 %grow.1 = (f32[256,768]{1,0:T(8,128)S(1)}, bf16[256,768]{1,0:T(8,128)(2,1)S(1)}, bf16[256,1536]{1,0:T(8,128)(2,1)S(1)}, f32[256,1536]{1,0:T(8,128)S(1)}, bf16[25...) custom-call(s32[2]{0:T(128)S(1)} %copy-done.15, ...), custom_call_target="tpu_custom_call" | custom-call | flops 10924999680 | bytes 1 | tf_op jit(solution)/shard_map/grow/pallas_call | solution.py:231
  93.3 1.6 collective-permute-start.33
  94.9 5.4 %shrink_back.1 = (bf16[256,1536]{1,0:T(8,128)(2,1)S(1)}, f32[256,768]{1,0:T(8,128)S(1)}, f32[128,768]{1,0:T(8,128)S(1)}, f32[128,768]{1,0:T(8,128)S(1)}) custom-call(s32[2]{0:T(128)S(1)} %copy-done.15, bf16[128,768]{1,0:T(8,128)(2,1)S(1)} %bitcast.77, bf16[272,768]{1,0:T(8,128)(2,1)S(1)} %collective-permute-done.refs_3_.refs_4_.refs_2_.refs_5_, ...), custom_call_target="tpu_custom_call" | custom-call | flops 7360000000 | bytes 1 | tf_op jit(solution)/shard_map/shrink_back/pallas_call | solution.py:231
  100.4 2.2 %expand_grads.1 = (f32[1,1536]{1,0:T(1,128)S(1)}, bf16[8,48,1536]{2,1,0:T(8,128)(2,1)S(1)}, bf16[4,48,1536]{2,1,0:T(8,128)(2,1)S(1)}, bf16[4,48,1536]{2,1,0:T(8,128)(2,1)S(1)}) custom-call(s32[2]{0:T(128)S(1)} %copy-done.15, bf16[256,768]{1,0:T(8,128)(2,1)S(1)} %get-tuple-element.101.refs_1_, bf16[256,1536]{1,0:T(8,128)(2,1)S(1)} %get-tuple-element.102.refs_2_), custom_call_target="tpu_custom_call" | custom-call | flops 4944999936 | bytes 1 | tf_op jit(solution)/shard_map/expand_grads/pallas_call | solution.py:231
  102.6 1.3 collective-permute-start.29
  103.9 5.7 %collective-permute-done.33 = bf16[4,192,768]{2,1,0:T(8,128)(2,1)S(1)} collective-permute-done((bf16[4,192,768]{2,1,0:T(8,128)(2,1)S(1)}, bf16[4,192,768]{2,1,0:T(8,128)(2,1)S(1)}, u32[]{:S(2)}, u32[]{:S(2)}) %collective-permute-start.33) | collective-permute-done | bytes 1179680 | tf_op jit(solution)/shard_map/ppermute | solution.py:79
  111.3 10.3 %attend_back.1 = (f32[128,768]{1,0:T(8,128)S(1)}, f32[128,768]{1,0:T(8,128)S(1)}, f32[128,768]{1,0:T(8,128)}, bf16[8,48,1664]{2,1,0:T(8,128)(2,1)S(1)}, bf16[4,4...) custom-call(s32[2]{0:T(128)S(1)} %copy-done.15, f32[16,768]{1,0:T(8,128)S(1)} %get-tuple-element.79.refs_1_, ...), custom_call_target="tpu_custom_call" | custom-call | flops 10350000128 | bytes 1 | tf_op jit(solution)/shard_map/attend_back/pallas_call | solution.py:231
  121.6 1.6 collective-permute-start.24
  123.1 5.4 %collective-permute-done.29 = bf16[8,48,1536]{2,1,0:T(8,128)(2,1)S(1)} collective-permute-done((bf16[8,48,1536]{2,1,0:T(8,128)(2,1)S(1)}, bf16[8,48,1536]{2,1,0:T(8,128)(2,1)S(1)}, u32[]{:S(2)}, u32[]{:S(2)}) %collective-permute-start.29) | collective-permute-done | bytes 1179680 | tf_op jit(solution)/shard_map/ppermute | solution.py:79
  128.5 1.3 add_convert_fusion.5
  132.4 1.4 copy.78
  133.7 1.1 copy-done.17
  137.9 3.1 %finish.1 = (f32[128,768]{1,0:T(8,128)}, f32[128,768]{1,0:T(8,128)}) custom-call(s32[2]{0:T(128)S(1)} %copy-done.15, f32[16,768]{1,0:T(8,128)S(1)} %get-tuple-element.79.refs_1_, bf16[128,768]{1,0:T(8,128)(2,1)S(1)} %bitcast.83, f32[256,768]{1,0:T(8,128)S(1)} %copy-done.17, f32[128,768]{1,0:T(8,128)S(1)} %copy-done.19, ...), custom_call_target="tpu_custom_call" | custom-call | flops 2990000128 | bytes 1 | tf_op jit(solution)/shard_map/finish/pallas_call | solution.py:231
  141.1 1.3 collective-permute-start.36
  142.4 4.1 %collective-permute-done.30 = bf16[4,48,1536]{2,1,0:T(8,128)(2,1)} collective-permute-done((bf16[4,48,1536]{2,1,0:T(8,128)(2,1)}, bf16[4,48,1536]{2,1,0:T(8,128)(2,1)}, u32[]{:S(2)}, u32[]{:S(2)}) %collective-permute-start.30) | collective-permute-done | bytes 589856 | tf_op jit(solution)/shard_map/ppermute | solution.py:79
  146.5 1.2 add_convert_fusion.11
  148.7 1.6 add_convert_fusion.1
  150.2 1.0 collective-permute-start.25
  151.3 2.6 %collective-permute-done.36 = bf16[1,192,768]{2,1,0:T(8,128)(2,1)S(1)} collective-permute-done((bf16[1,192,768]{2,1,0:T(8,128)(2,1)S(1)}, bf16[1,192,768]{2,1,0:T(8,128)(2,1)S(1)}, u32[]{:S(2)}, u32[]{:S(2)}) %collective-permute-start.36) | collective-permute-done | bytes 294944 | tf_op jit(solution)/shard_map/ppermute | solution.py:90
  154.2 3.1 %collective-permute-done.31 = bf16[2,48,1536]{2,1,0:T(8,128)(2,1)S(1)} collective-permute-done((bf16[2,48,1536]{2,1,0:T(8,128)(2,1)S(1)}, bf16[2,48,1536]{2,1,0:T(8,128)(2,1)S(1)}, u32[]{:S(2)}, u32[]{:S(2)}) %collective-permute-start.31) | collective-permute-done | bytes 294944 | tf_op jit(solution)/shard_map/ppermute | solution.py:71
  157.3 1.4 collective-permute-start.32
  158.8 1.9 %collective-permute-done.25 = bf16[4,48,1664]{2,1,0:T(8,128)(2,1)S(1)} collective-permute-done((bf16[4,48,1664]{2,1,0:T(8,128)(2,1)S(1)}, bf16[4,48,1664]{2,1,0:T(8,128)(2,1)S(1)}, u32[]{:S(2)}, u32[]{:S(2)}) %collective-permute-start.25) | collective-permute-done | bytes 639008 | tf_op jit(solution)/shard_map/ppermute | solution.py:79
  160.9 1.2 collective-permute-start.26
  162.1 3.5 %collective-permute-done.32 = bf16[1,48,1536]{2,1,0:T(8,128)(2,1)S(1)} collective-permute-done((bf16[1,48,1536]{2,1,0:T(8,128)(2,1)S(1)}, bf16[1,48,1536]{2,1,0:T(8,128)(2,1)S(1)}, u32[]{:S(2)}, u32[]{:S(2)}) %collective-permute-start.32) | collective-permute-done | bytes 147488 | tf_op jit(solution)/shard_map/ppermute | solution.py:71
  165.6 1.1 fusion.24
  166.8 4.9 %collective-permute-done.26 = bf16[2,48,1664]{2,1,0:T(8,128)(2,1)S(1)} collective-permute-done((bf16[2,48,1664]{2,1,0:T(8,128)(2,1)S(1)}, bf16[2,48,1664]{2,1,0:T(8,128)(2,1)S(1)}, u32[]{:S(2)}, u32[]{:S(2)}) %collective-permute-start.26) | collective-permute-done | bytes 319520 | tf_op jit(solution)/shard_map/ppermute | solution.py:71
  171.8 1.1 fusion.21
  173.0 7.4 %collective-permute-done.27 = bf16[1,48,1664]{2,1,0:T(8,128)(2,1)S(1)} collective-permute-done((bf16[1,48,1664]{2,1,0:T(8,128)(2,1)S(1)}, bf16[1,48,1664]{2,1,0:T(8,128)(2,1)S(1)}, u32[]{:S(2)}, u32[]{:S(2)}) %collective-permute-start.27) | collective-permute-done | bytes 159776 | tf_op jit(solution)/shard_map/ppermute | solution.py:71
  (177 shorter events, 26.6 us)
Async XLA Ops:
  4.2 33.0 %copy-start.32 = (bf16[1,192,768]{2,1,0:T(8,128)(2,1)S(1)}, bf16[1,192,768]{2,1,0:T(8,128)(2,1)}, u32[]{:S(2)}) copy-start(bf16[1,192,768]{2,1,0:T(8,128)(2,1)} %param.33) | copy-start | bytes 884740
  4.2 11.8 %collective-permute-start.1 = (bf16[1,48,1664]{2,1,0:T(8,128)(2,1)}, bf16[1,48,1664]{2,1,0:T(8,128)(2,1)S(1)}, u32[]{:S(2)}, u32[]{:S(2)}) collective-permute-start(bf16[1,48,1664]{2,1,0:T(8,128)(2,1)} %bitcast.87), channel_id=1, source_target_pairs={{0,8},{1,9},{2,10},{3,11},{4,12},{5,13},{6,14},{7,15},{8,0},{9,1},... | collective-permute-start | bytes 479240 | tf_op jit(solution)/shard_map/ppermute | solution.py:71
  17.0 13.6 %collective-permute-start.2 = (bf16[2,48,1664]{2,1,0:T(8,128)(2,1)S(1)}, bf16[2,48,1664]{2,1,0:T(8,128)(2,1)S(1)}, u32[]{:S(2)}, u32[]{:S(2)}) collective-permute-start(bf16[2,48,1664]{2,1,0:T(8,128)(2,1)S(1)} %pad_maximum_fusion.2.refs_4_.refs_15_), channel_id=1, source_target_pairs={{0,1},{1,0},{2,3},{3,2},{4,5},{5,4},{6,7},{7,6},{8,9},{9,8},{10,11... | collective-permute-start | bytes 958472 | tf_op jit(solution)/shard_map/ppermute | solution.py:79
  18.6 12.0 %collective-permute-start.3 = (bf16[2,48,1664]{2,1,0:T(8,128)(2,1)S(1)}, bf16[2,48,1664]{2,1,0:T(8,128)(2,1)S(1)}, u32[]{:S(2)}, u32[]{:S(2)}) collective-permute-start(bf16[2,48,1664]{2,1,0:T(8,128)(2,1)S(1)} %pad_maximum_fusion.2.refs_4_.refs_15_), channel_id=1, source_target_pairs={{0,2},{1,3},{2,0},{3,1},{4,6},{5,7},{6,4},{7,5},{8,10},{9,11},{10,... | collective-permute-start | bytes 958472 | tf_op jit(solution)/shard_map/ppermute | solution.py:79
  20.1 11.1 %collective-permute-start.5 = (bf16[2,48,1664]{2,1,0:T(8,128)(2,1)S(1)}, bf16[2,48,1664]{2,1,0:T(8,128)(2,1)S(1)}, u32[]{:S(2)}, u32[]{:S(2)}) collective-permute-start(bf16[2,48,1664]{2,1,0:T(8,128)(2,1)S(1)} %pad_maximum_fusion.2.refs_4_.refs_15_), channel_id=1, source_target_pairs={{0,4},{1,5},{2,6},{3,7},{4,0},{5,1},{6,2},{7,3},{8,12},{9,13},{10,... | collective-permute-start | bytes 958472 | tf_op jit(solution)/shard_map/ppermute | solution.py:71
  20.9 9.7 %collective-permute-start.9 = (bf16[1,48,1536]{2,1,0:T(8,128)(2,1)}, bf16[1,48,1536]{2,1,0:T(8,128)(2,1)S(1)}, u32[]{:S(2)}, u32[]{:S(2)}) collective-permute-start(bf16[1,48,1536]{2,1,0:T(8,128)(2,1)} %bitcast.89), channel_id=1, source_target_pairs={{0,8},{1,9},{2,10},{3,11},{4,12},{5,13},{6,14},{7,15},{8,0},{9,1},... | collective-permute-start | bytes 442376 | tf_op jit(solution)/shard_map/ppermute | solution.py:71
  30.6 33.9 %copy-start = (bf16[2,48,1664]{2,1,0:T(8,128)(2,1)}, bf16[2,48,1664]{2,1,0:T(8,128)(2,1)S(1)}, u32[]{:S(2)}) copy-start(bf16[2,48,1664]{2,1,0:T(8,128)(2,1)S(1)} %collective-permute-done.2.refs_5_.refs_16_) | copy-start | bytes 958468
  30.6 33.9 %copy-start.2 = (bf16[2,48,1664]{2,1,0:T(8,128)(2,1)}, bf16[2,48,1664]{2,1,0:T(8,128)(2,1)S(1)}, u32[]{:S(2)}) copy-start(bf16[2,48,1664]{2,1,0:T(8,128)(2,1)S(1)} %collective-permute-done.3.refs_6_.refs_17_) | copy-start | bytes 958468
  31.2 33.3 %copy-start.4 = (bf16[2,48,1664]{2,1,0:T(8,128)(2,1)}, bf16[2,48,1664]{2,1,0:T(8,128)(2,1)S(1)}, u32[]{:S(2)}) copy-start(bf16[2,48,1664]{2,1,0:T(8,128)(2,1)S(1)} %collective-permute-done.5.refs_8_.refs_19_) | copy-start | bytes 958468
  31.2 9.8 %collective-permute-start.10 = (bf16[2,48,1536]{2,1,0:T(8,128)(2,1)S(1)}, bf16[2,48,1536]{2,1,0:T(8,128)(2,1)S(1)}, u32[]{:S(2)}, u32[]{:S(2)}) collective-permute-start(bf16[2,48,1536]{2,1,0:T(8,128)(2,1)S(1)} %constant_dynamic-update-slice_fusion), channel_id=1, source_target_pairs={{0,4},{1,5},{2,6},{3,7},{4,0},{5,1},{6,2},{7,3},{8,12},{9,13},{10,... | collective-permute-start | bytes 884744 | tf_op jit(solution)/shard_map/ppermute | solution.py:71
  34.6 8.3 %collective-permute-start.7 = (bf16[2,48,1664]{2,1,0:T(8,128)(2,1)S(1)}, bf16[2,48,1664]{2,1,0:T(8,128)(2,1)S(1)}, u32[]{:S(2)}, u32[]{:S(2)}) collective-permute-start(bf16[2,48,1664]{2,1,0:T(8,128)(2,1)S(1)} %collective-permute-done.5.refs_8_.refs_19_), channel_id=1, source_target_pairs={{0,2},{1,3},{2,0},{3,1},{4,6},{5,7},{6,4},{7,5},{8,10},{9,11},{10,... | collective-permute-start | bytes 958472 | tf_op jit(solution)/shard_map/ppermute | solution.py:79
  35.1 10.5 %collective-permute-start.6 = (bf16[2,48,1664]{2,1,0:T(8,128)(2,1)S(1)}, bf16[2,48,1664]{2,1,0:T(8,128)(2,1)S(1)}, u32[]{:S(2)}, u32[]{:S(2)}) collective-permute-start(bf16[2,48,1664]{2,1,0:T(8,128)(2,1)S(1)} %collective-permute-done.5.refs_8_.refs_19_), channel_id=1, source_target_pairs={{0,1},{1,0},{2,3},{3,2},{4,5},{5,4},{6,7},{7,6},{8,9},{9,8},{10,11... | collective-permute-start | bytes 958472 | tf_op jit(solution)/shard_map/ppermute | solution.py:79
  35.7 10.6 %collective-permute-start.4 = (bf16[2,48,1664]{2,1,0:T(8,128)(2,1)S(1)}, bf16[2,48,1664]{2,1,0:T(8,128)(2,1)S(1)}, u32[]{:S(2)}, u32[]{:S(2)}) collective-permute-start(bf16[2,48,1664]{2,1,0:T(8,128)(2,1)S(1)} %collective-permute-done.2.refs_5_.refs_16_), channel_id=1, source_target_pairs={{0,2},{1,3},{2,0},{3,1},{4,6},{5,7},{6,4},{7,5},{8,10},{9,11},{10,... | collective-permute-start | bytes 958472 | tf_op jit(solution)/shard_map/ppermute | solution.py:79
  37.2 10.6 %collective-permute-start.14 = (bf16[1,192,768]{2,1,0:T(8,128)(2,1)S(1)}, bf16[1,192,768]{2,1,0:T(8,128)(2,1)S(1)}, u32[]{:S(2)}, u32[]{:S(2)}) collective-permute-start(bf16[1,192,768]{2,1,0:T(8,128)(2,1)S(1)} %copy-done.32), channel_id=1, source_target_pairs={{0,8},{1,9},{2,10},{3,11},{4,12},{5,13},{6,14},{7,15},{24,16},{25,... | collective-permute-start | bytes 884744 | tf_op jit(solution)/shard_map/ppermute | solution.py:90
  41.1 23.5 %copy-start.13 = (bf16[1,128,768]{2,1,0:T(8,128)(2,1)S(1)}, bf16[1,128,768]{2,1,0:T(8,128)(2,1)}, u32[]{:S(2)}) copy-start(bf16[1,128,768]{2,1,0:T(8,128)(2,1)} %param.27) | copy-start | bytes 589828
  41.1 23.5 %copy-start.14 = (s32[1,2]{1,0:T(1,128)S(1)}, s32[1,2]{1,0:T(1,128)}, u32[]{:S(2)}) copy-start(s32[1,2]{1,0:T(1,128)} %param.29) | copy-start | bytes 28
  41.1 23.5 %copy-start.15 = (s32[2]{0:T(128)S(1)}, s32[2]{0:T(128)}, u32[]{:S(2)}) copy-start(s32[2]{0:T(128)} %pad_add_fusion.refs_0_) | copy-start | bytes 28
  42.9 26.0 %copy-start.6 = (bf16[2,48,1664]{2,1,0:T(8,128)(2,1)}, bf16[2,48,1664]{2,1,0:T(8,128)(2,1)S(1)}, u32[]{:S(2)}) copy-start(bf16[2,48,1664]{2,1,0:T(8,128)(2,1)S(1)} %collective-permute-done.7.refs_10_.refs_21_) | copy-start | bytes 958468
  45.6 23.3 %copy-start.8 = (bf16[2,48,1664]{2,1,0:T(8,128)(2,1)}, bf16[2,48,1664]{2,1,0:T(8,128)(2,1)S(1)}, u32[]{:S(2)}) copy-start(bf16[2,48,1664]{2,1,0:T(8,128)(2,1)S(1)} %collective-permute-done.6.refs_9_.refs_20_) | copy-start | bytes 958468
  46.3 14.6 %collective-permute-start.11 = (bf16[4,48,1536]{2,1,0:T(8,128)(2,1)S(1)}, bf16[4,48,1536]{2,1,0:T(8,128)(2,1)S(1)}, u32[]{:S(2)}, u32[]{:S(2)}) collective-permute-start(bf16[4,48,1536]{2,1,0:T(8,128)(2,1)S(1)} %pad_maximum_fusion.refs_9_), channel_id=1, source_target_pairs={{0,1},{1,0},{2,3},{3,2},{4,5},{5,4},{6,7},{7,6},{8,9},{9,8},{10,11... | collective-permute-start | bytes 1769480 | tf_op jit(solution)/shard_map/ppermute | solution.py:79
  47.9 7.5 %collective-permute-start.15 = (bf16[1,192,768]{2,1,0:T(8,128)(2,1)S(1)}, bf16[1,192,768]{2,1,0:T(8,128)(2,1)S(1)}, u32[]{:S(2)}, u32[]{:S(2)}) collective-permute-start(bf16[1,192,768]{2,1,0:T(8,128)(2,1)S(1)} %broadcast_select_fusion), channel_id=1, source_target_pairs={{0,4},{1,5},{2,6},{3,7},{4,0},{5,1},{6,2},{7,3},{8,12},{9,13},{10,... | collective-permute-start | bytes 884744 | tf_op jit(solution)/shard_map/ppermute | solution.py:71
  48.3 14.8 %collective-permute-start = (bf16[272,768]{1,0:T(8,128)(2,1)S(1)}, bf16[272,768]{1,0:T(8,128)(2,1)S(1)}, u32[]{:S(2)}, u32[]{:S(2)}) collective-permute-start(bf16[272,768]{1,0:T(8,128)(2,1)S(1)} %copy-done.48), channel_id=1, source_target_pairs={{0,16},{16,0},{1,17},{17,1},{2,18},{18,2},{3,19},{19,3},{4,20},{20... | collective-permute-start | bytes 1253384 | tf_op jit(solution)/shard_map/ppermute | solution.py:82
  48.3 16.2 %collective-permute-start.8 = (bf16[2,48,1664]{2,1,0:T(8,128)(2,1)S(1)}, bf16[2,48,1664]{2,1,0:T(8,128)(2,1)S(1)}, u32[]{:S(2)}, u32[]{:S(2)}) collective-permute-start(bf16[2,48,1664]{2,1,0:T(8,128)(2,1)S(1)} %collective-permute-done.6.refs_9_.refs_20_), channel_id=1, source_target_pairs={{0,2},{1,3},{2,0},{3,1},{4,6},{5,7},{6,4},{7,5},{8,10},{9,11},{10,... | collective-permute-start | bytes 958472 | tf_op jit(solution)/shard_map/ppermute | solution.py:79
  48.8 37.0 %collective-permute-start.19 = (bf16[4,48,1536]{2,1,0:T(8,128)(2,1)S(1)}, bf16[4,48,1536]{2,1,0:T(8,128)(2,1)S(1)}, u32[]{:S(2)}, u32[]{:S(2)}) collective-permute-start(bf16[4,48,1536]{2,1,0:T(8,128)(2,1)S(1)} %pad_maximum_fusion.refs_9_), channel_id=1, source_target_pairs={{0,2},{1,3},{2,0},{3,1},{4,6},{5,7},{6,4},{7,5},{8,10},{9,11},{10,... | collective-permute-start | bytes 1769480 | tf_op jit(solution)/shard_map/ppermute | solution.py:79
  55.4 30.4 %copy-start.12 = (bf16[1,128,768]{2,1,0:T(8,128)(2,1)S(1)}, bf16[1,128,768]{2,1,0:T(8,128)(2,1)}, u32[]{:S(2)}) copy-start(bf16[1,128,768]{2,1,0:T(8,128)(2,1)} %param.28) | copy-start | bytes 589828
  61.0 23.8 %collective-permute-start.16 = (bf16[2,192,768]{2,1,0:T(8,128)(2,1)S(1)}, bf16[2,192,768]{2,1,0:T(8,128)(2,1)S(1)}, u32[]{:S(2)}, u32[]{:S(2)}) collective-permute-start(bf16[2,192,768]{2,1,0:T(8,128)(2,1)S(1)} %pad_maximum_fusion.1.refs_5_), channel_id=1, source_target_pairs={{0,1},{1,0},{2,3},{3,2},{4,5},{5,4},{6,7},{7,6},{8,9},{9,8},{10,11... | collective-permute-start | bytes 1769480 | tf_op jit(solution)/shard_map/ppermute | solution.py:79
  62.5 22.7 %collective-permute-start.17 = (bf16[2,192,768]{2,1,0:T(8,128)(2,1)S(1)}, bf16[2,192,768]{2,1,0:T(8,128)(2,1)S(1)}, u32[]{:S(2)}, u32[]{:S(2)}) collective-permute-start(bf16[2,192,768]{2,1,0:T(8,128)(2,1)S(1)} %pad_maximum_fusion.1.refs_5_), channel_id=1, source_target_pairs={{0,2},{1,3},{2,0},{3,1},{4,6},{5,7},{6,4},{7,5},{8,10},{9,11},{10,... | collective-permute-start | bytes 1769480 | tf_op jit(solution)/shard_map/ppermute | solution.py:79
  63.1 20.7 %collective-permute-start.12 = (bf16[4,48,1536]{2,1,0:T(8,128)(2,1)S(1)}, bf16[4,48,1536]{2,1,0:T(8,128)(2,1)S(1)}, u32[]{:S(2)}, u32[]{:S(2)}) collective-permute-start(bf16[4,48,1536]{2,1,0:T(8,128)(2,1)S(1)} %collective-permute-done.11.refs_10_), channel_id=1, source_target_pairs={{0,2},{1,3},{2,0},{3,1},{4,6},{5,7},{6,4},{7,5},{8,10},{9,11},{10,... | collective-permute-start | bytes 1769480 | tf_op jit(solution)/shard_map/ppermute | solution.py:79
  68.9 16.9 %collective-permute-start.18 = (bf16[768,384]{1,0:T(8,128)(2,1)S(1)}, bf16[768,384]{1,0:T(8,128)(2,1)S(1)}, u32[]{:S(2)}, u32[]{:S(2)}) collective-permute-start(bf16[768,384]{1,0:T(8,128)(2,1)S(1)} %get-tuple-element.90.refs_7_.refs_9_), channel_id=1, source_target_pairs={{0,16},{16,0},{1,17},{17,1},{2,18},{18,2},{3,19},{19,3},{4,20},{20... | collective-permute-start | bytes 1769480 | tf_op jit(solution)/shard_map/ppermute | solution.py:82
  83.8 2.0 %collective-permute-start.13 = (bf16[256,384]{1,0:T(8,128)(2,1)S(1)}, bf16[256,384]{1,0:T(8,128)(2,1)S(1)}, u32[]{:S(2)}, u32[]{:S(2)}) collective-permute-start(bf16[256,384]{1,0:T(8,128)(2,1)S(1)} %get-tuple-element.85.refs_5_), channel_id=1, source_target_pairs={{0,16},{16,0},{1,17},{17,1},{2,18},{18,2},{3,19},{19,3},{4,20},{20... | collective-permute-start | bytes 589832 | tf_op jit(solution)/shard_map/ppermute | solution.py:82
  84.7 10.1 %collective-permute-start.20 = (bf16[2,192,768]{2,1,0:T(8,128)(2,1)S(1)}, bf16[2,192,768]{2,1,0:T(8,128)(2,1)S(1)}, u32[]{:S(2)}, u32[]{:S(2)}) collective-permute-start(bf16[2,192,768]{2,1,0:T(8,128)(2,1)S(1)} %collective-permute-done.16.refs_6_), channel_id=1, source_target_pairs={{0,2},{1,3},{2,0},{3,1},{4,6},{5,7},{6,4},{7,5},{8,10},{9,11},{10,... | collective-permute-start | bytes 1769480 | tf_op jit(solution)/shard_map/ppermute | solution.py:79
  93.3 16.3 %collective-permute-start.33 = (bf16[4,192,768]{2,1,0:T(8,128)(2,1)S(1)}, bf16[4,192,768]{2,1,0:T(8,128)(2,1)S(1)}, u32[]{:S(2)}, u32[]{:S(2)}) collective-permute-start(bf16[4,192,768]{2,1,0:T(8,128)(2,1)S(1)} %get-tuple-element.116), channel_id=1, source_target_pairs={{0,1},{1,0},{2,3},{3,2},{4,5},{5,4},{6,7},{7,6},{8,9},{9,8},{10,11... | collective-permute-start | bytes 3538952 | tf_op jit(solution)/shard_map/ppermute | solution.py:79
  100.3 10.7 %collective-permute-start.22 = (f32[256,768]{1,0:T(8,128)S(1)}, f32[256,768]{1,0:T(8,128)S(1)}, u32[]{:S(2)}, u32[]{:S(2)}) collective-permute-start(f32[256,768]{1,0:T(8,128)S(1)} %get-tuple-element.96.refs_6_), channel_id=1, source_target_pairs={{0,16},{16,0},{1,17},{17,1},{2,18},{18,2},{3,19},{19,3},{4,20},{20... | collective-permute-start | bytes 2359304 | tf_op jit(solution)/shard_map/ppermute | solution.py:82
  102.6 25.9 %collective-permute-start.29 = (bf16[8,48,1536]{2,1,0:T(8,128)(2,1)S(1)}, bf16[8,48,1536]{2,1,0:T(8,128)(2,1)S(1)}, u32[]{:S(2)}, u32[]{:S(2)}) collective-permute-start(bf16[8,48,1536]{2,1,0:T(8,128)(2,1)S(1)} %get-tuple-element.113), channel_id=1, source_target_pairs={{0,1},{1,0},{2,3},{3,2},{4,5},{5,4},{6,7},{7,6},{8,9},{9,8},{10,11... | collective-permute-start | bytes 3538952 | tf_op jit(solution)/shard_map/ppermute | solution.py:79
  103.9 29.8 %collective-permute-start.21 = (f32[128,768]{1,0:T(8,128)S(1)}, f32[128,768]{1,0:T(8,128)}, u32[]{:S(2)}, u32[]{:S(2)}) collective-permute-start(f32[128,768]{1,0:T(8,128)S(1)} %get-tuple-element.95), channel_id=1, source_target_pairs={{0,16},{16,0},{1,17},{17,1},{2,18},{18,2},{3,19},{19,3},{4,20},{20... | collective-permute-start | bytes 1179656 | tf_op jit(solution)/shard_map/ppermute | solution.py:82
  109.9 20.9 %collective-permute-start.34 = (bf16[2,192,768]{2,1,0:T(8,128)(2,1)S(1)}, bf16[2,192,768]{2,1,0:T(8,128)(2,1)S(1)}, u32[]{:S(2)}, u32[]{:S(2)}) collective-permute-start(bf16[2,192,768]{2,1,0:T(8,128)(2,1)S(1)} %get-tuple-element.214), channel_id=1, source_target_pairs={{0,2},{1,3},{2,0},{3,1},{4,6},{5,7},{6,4},{7,5},{8,10},{9,11},{10,... | collective-permute-start | bytes 1769480 | tf_op jit(solution)/shard_map/ppermute | solution.py:79
  121.6 27.1 %collective-permute-start.24 = (bf16[8,48,1664]{2,1,0:T(8,128)(2,1)S(1)}, bf16[8,48,1664]{2,1,0:T(8,128)(2,1)}, u32[]{:S(2)}, u32[]{:S(2)}) collective-permute-start(bf16[8,48,1664]{2,1,0:T(8,128)(2,1)S(1)} %get-tuple-element.110), channel_id=1, source_target_pairs={{0,1},{1,0},{2,3},{3,2},{4,5},{5,4},{6,7},{7,6},{8,9},{9,8},{10,11... | collective-permute-start | bytes 3833864 | tf_op jit(solution)/shard_map/ppermute | solution.py:79
  123.1 10.6 %collective-permute-start.23 = (f32[128,768]{1,0:T(8,128)}, f32[128,768]{1,0:T(8,128)}, u32[]{:S(2)}, u32[]{:S(2)}) collective-permute-start(f32[128,768]{1,0:T(8,128)} %get-tuple-element.106), channel_id=1, source_target_pairs={{0,16},{16,0},{1,17},{17,1},{2,18},{18,2},{3,19},{19,3},{4,20},{20... | collective-permute-start | bytes 1179656 | tf_op jit(solution)/shard_map/ppermute | solution.py:82
  129.9 16.6 %collective-permute-start.30 = (bf16[4,48,1536]{2,1,0:T(8,128)(2,1)}, bf16[4,48,1536]{2,1,0:T(8,128)(2,1)}, u32[]{:S(2)}, u32[]{:S(2)}) collective-permute-start(bf16[4,48,1536]{2,1,0:T(8,128)(2,1)} %get-tuple-element.218), channel_id=1, source_target_pairs={{0,2},{1,3},{2,0},{3,1},{4,6},{5,7},{6,4},{7,5},{8,10},{9,11},{10,... | collective-permute-start | bytes 1769480 | tf_op jit(solution)/shard_map/ppermute | solution.py:79
  131.8 9.2 %collective-permute-start.35 = (bf16[1,192,768]{2,1,0:T(8,128)(2,1)}, bf16[1,192,768]{2,1,0:T(8,128)(2,1)S(1)}, u32[]{:S(2)}, u32[]{:S(2)}) collective-permute-start(bf16[1,192,768]{2,1,0:T(8,128)(2,1)} %add_convert_fusion.8), channel_id=1, source_target_pairs={{0,4},{1,5},{2,6},{3,7},{4,0},{5,1},{6,2},{7,3},{8,12},{9,13},{10,... | collective-permute-start | bytes 884744 | tf_op jit(solution)/shard_map/ppermute | solution.py:71
  141.1 12.8 %collective-permute-start.36 = (bf16[1,192,768]{2,1,0:T(8,128)(2,1)S(1)}, bf16[1,192,768]{2,1,0:T(8,128)(2,1)S(1)}, u32[]{:S(2)}, u32[]{:S(2)}) collective-permute-start(bf16[1,192,768]{2,1,0:T(8,128)(2,1)S(1)} %fusion), channel_id=1, source_target_pairs={{8,0},{9,1},{10,2},{11,3},{12,4},{13,5},{14,6},{15,7},{16,24},{17,... | collective-permute-start | bytes 884744 | tf_op jit(solution)/shard_map/ppermute | solution.py:90
  147.7 9.6 %collective-permute-start.31 = (bf16[2,48,1536]{2,1,0:T(8,128)(2,1)S(1)}, bf16[2,48,1536]{2,1,0:T(8,128)(2,1)S(1)}, u32[]{:S(2)}, u32[]{:S(2)}) collective-permute-start(bf16[2,48,1536]{2,1,0:T(8,128)(2,1)S(1)} %get-tuple-element.216), channel_id=1, source_target_pairs={{0,4},{1,5},{2,6},{3,7},{4,0},{5,1},{6,2},{7,3},{8,12},{9,13},{10,... | collective-permute-start | bytes 884744 | tf_op jit(solution)/shard_map/ppermute | solution.py:71
  150.2 10.5 %collective-permute-start.25 = (bf16[4,48,1664]{2,1,0:T(8,128)(2,1)S(1)}, bf16[4,48,1664]{2,1,0:T(8,128)(2,1)S(1)}, u32[]{:S(2)}, u32[]{:S(2)}) collective-permute-start(bf16[4,48,1664]{2,1,0:T(8,128)(2,1)S(1)} %get-tuple-element.212), channel_id=1, source_target_pairs={{0,2},{1,3},{2,0},{3,1},{4,6},{5,7},{6,4},{7,5},{8,10},{9,11},{10,... | collective-permute-start | bytes 1916936 | tf_op jit(solution)/shard_map/ppermute | solution.py:79
  154.1 17.7 %collective-permute-start.37 = (f32[192,384]{1,0:T(8,128)S(1)}, f32[192,384]{1,0:T(8,128)S(1)}, u32[]{:S(2)}, u32[]{:S(2)}) collective-permute-start(f32[192,384]{1,0:T(8,128)S(1)} %dynamic-slice_bitcast_fusion), channel_id=1, source_target_pairs={{0,16},{16,0},{1,17},{17,1},{2,18},{18,2},{3,19},{19,3},{4,20},{20... | collective-permute-start | bytes 884744 | tf_op jit(solution)/shard_map/ppermute | solution.py:82
  157.3 8.3 %collective-permute-start.32 = (bf16[1,48,1536]{2,1,0:T(8,128)(2,1)S(1)}, bf16[1,48,1536]{2,1,0:T(8,128)(2,1)S(1)}, u32[]{:S(2)}, u32[]{:S(2)}) collective-permute-start(bf16[1,48,1536]{2,1,0:T(8,128)(2,1)S(1)} %add_convert_fusion.13), channel_id=1, source_target_pairs={{0,8},{1,9},{2,10},{3,11},{4,12},{5,13},{6,14},{7,15},{8,0},{9,1},... | collective-permute-start | bytes 442376 | tf_op jit(solution)/shard_map/ppermute | solution.py:71
  160.9 10.7 %collective-permute-start.26 = (bf16[2,48,1664]{2,1,0:T(8,128)(2,1)S(1)}, bf16[2,48,1664]{2,1,0:T(8,128)(2,1)S(1)}, u32[]{:S(2)}, u32[]{:S(2)}) collective-permute-start(bf16[2,48,1664]{2,1,0:T(8,128)(2,1)S(1)} %get-tuple-element.210), channel_id=1, source_target_pairs={{0,4},{1,5},{2,6},{3,7},{4,0},{5,1},{6,2},{7,3},{8,12},{9,13},{10,... | collective-permute-start | bytes 958472 | tf_op jit(solution)/shard_map/ppermute | solution.py:71
  171.7 8.6 %collective-permute-start.27 = (bf16[1,48,1664]{2,1,0:T(8,128)(2,1)S(1)}, bf16[1,48,1664]{2,1,0:T(8,128)(2,1)S(1)}, u32[]{:S(2)}, u32[]{:S(2)}) collective-permute-start(bf16[1,48,1664]{2,1,0:T(8,128)(2,1)S(1)} %add_convert_fusion.12), channel_id=1, source_target_pairs={{0,8},{1,9},{2,10},{3,11},{4,12},{5,13},{6,14},{7,15},{8,0},{9,1},... | collective-permute-start | bytes 479240 | tf_op jit(solution)/shard_map/ppermute | solution.py:71
  181.2 1.4 collective-permute-start.28
  (39 other events, 253.7 us)

commit v4 on v3

--- a/solution.py
+++ b/solution.py
@@ -238,7 +238,7 @@
         + rooms
         + ([pltpu.SemaphoreType.DMA((len(moved),))] if moved else []),
         compiler_params=pltpu.CompilerParams(vmem_limit_bytes=(60 if name == "pack_blocks" else 28) << 20),
-        cost_estimate=pl.CostEstimate(flops=int({'pack_blocks': 1.5, 'attend': 4.3, 'grow': 9.5, 'shrink_back': 6.4, 'expand_grads': 4.3, 'attend_back': 9.0, 'finish': 2.6}[name] * 1150000000), bytes_accessed=1, transcendentals=0),
+        cost_estimate=pl.CostEstimate(flops=int({'pack_blocks': 1.5, 'attend': 4.3, 'grow': 9.5, 'shrink_back': 6.4, 'expand_grads': 4.3, 'attend_back': 9.0, 'finish': 2.6, 'update_small': 1.5}[name] * 1150000000), bytes_accessed=1, transcendentals=0),
     )(*operands)
 
 
@@ -840,6 +840,39 @@
     )
 
 
+def update_small(meta, part, got, states):
+    rows, width = part.shape
+    shapes = []
+    for value in states[::3]:
+        shape = (value.shape[0], 1, rows)
+        shapes += [shaped(shape, wide)] * 4 + [shaped(shape, half_type)]
+
+    def body(meta_ref, part_ref, got_ref, *rest):
+        held, outs, room = rest[:6], rest[6:16], rest[16]
+        room[...] = jnp.zeros_like(room)
+        room[:rows] = part_ref.ready()[...] + got_ref.ready()[...]
+        small = room[...].T
+        start = 0
+        for at in range(2):
+            values = [ref.ready()[...] for ref in held[3 * at : 3 * at + 3]]
+            count = values[0].shape[0]
+            gradient = small[start : start + count, :rows]
+            start += count
+            new = adamw(*values, gradient, small_rate)
+            for ref, value in zip(outs[5 * at : 5 * at + 5], (gradient, *new)):
+                ref[...] = value.reshape(ref.shape)
+
+    return call(
+        body,
+        "update_small",
+        (meta, part, got, *states),
+        (SCALAR,) + (FETCH,) * 8,
+        shapes,
+        (PUT,) * 10,
+        (pltpu.VMEM((width, width), wide),),
+    )
+
+
 def local(
     tokens,
     cotangent,
@@ -874,7 +907,6 @@
     size = grid.size
     width = tokens.shape[2]
     half = width // 2
-    small_rows = norm_gains.shape[1] + bias_rows.shape[1]
     meta = jnp.stack([grid.index, core])
     lengths_own = lengths[0]
     tokens_own, cot = tokens[0], cotangent[0]
@@ -941,7 +973,6 @@
     result, input_grad = finish(
         meta, small, tokens_own, middle, second, second_got, back_middle, back_one, back_got
     )
-    gains_count = norm_gains.shape[1]
 
     third = [joint_sum_all[:, part_at * half : (part_at + 1) * half] for part_at in range(3)]
     small_part = joint_sum_all[:, 4 * half :]
@@ -949,7 +980,18 @@
         jnp.concatenate([jnp.where(core == 0, third[2], third[0]), small_part], axis=1)
     )
     joint_got = got[:, :half]
-    small_own = (small_part + got[:, half:])[:, :small_rows].T
+    small_results = update_small(
+        meta,
+        small_part,
+        got[:, half:],
+        [
+            value[0]
+            for value in (
+                master_gains, first_gains, second_gains, master_biases, first_biases, second_biases,
+            )
+        ],
+    )
+    small_results = [jnp.transpose(value, (1, 0, 2)) for value in small_results]
     joint_sum = jnp.where(
         core == 0,
         jnp.concatenate([third[0], joint_got, third[1]], axis=1),
@@ -962,43 +1004,16 @@
     shrink_keep = lax.dynamic_slice_in_dim(shrink_sum, core * side, side, axis=1)
     shrink_own = jnp.where(owner, shrink_keep, grid.swap_core(shrink_send))
 
-    masters = (
-        master_joint,
-        master_output,
-        master_expand,
-        master_shrink,
-        master_gains,
-        master_biases,
-    )
-    firsts = (first_joint, first_output, first_expand, first_shrink, first_gains, first_biases)
-    seconds = (
-        second_joint,
-        second_output,
-        second_expand,
-        second_shrink,
-        second_gains,
-        second_biases,
-    )
-    totals_all = (
-        joint_sum[None],
-        output_sum[None],
-        expand_sum[None],
-        shrink_own[None],
-        small_own[None, :gains_count],
-        small_own[None, gains_count:small_rows],
-    )
     results = [result[None], input_grad[None]]
-    for group_index in range(6):
-        group_rate = learning_rate if group_index < 4 else small_rate
-        new_master, new_first, new_second, new_copy = adamw(
-            masters[group_index],
-            firsts[group_index],
-            seconds[group_index],
-            totals_all[group_index],
-            group_rate,
-        )
-        results.extend([totals_all[group_index], new_master, new_first, new_second, new_copy])
-    return tuple(results)
+    for total, master, first, second_moment in (
+        (joint_sum, master_joint, first_joint, second_joint),
+        (output_sum, master_output, first_output, second_output),
+        (expand_sum, master_expand, first_expand, second_expand),
+        (shrink_own, master_shrink, first_shrink, second_shrink),
+    ):
+        gradient = total[None]
+        results += [gradient, *adamw(master, first, second_moment, gradient, learning_rate)]
+    return tuple([*results, *small_results])
 
 
 def solution(mesh):

time: 189 us -> 186 us (0.984)
  local copies, waits for them, and re-layouts: 11.4 us -> 6.71 us
  waiting for transfers between devices: 84.9 us -> 87 us
    unnamed x107, local copies, waits for them, and re-layouts: 10.5 us -> 6.66 us
    pallas_call x7 -> x8, Pallas kernels: 35.7 us -> 37.2 us  [call(): pl.pallas_call(whole, name=name, out_shape=tuple(outs), in_specs=[pl.Bloc...]
    convert_element_type x6 -> x4, other arithmetic: 4.7 us -> 4.02 us  [adamw(): return (master_new, first_new, second_new, master_new.astype(jnp.bfloat16))]
  transfers between devices with their start and end apart: 38 -> 38, of which waited for: 22 -> 23; matrix products, arithmetic and copies ran while one was open for 6% -> 5% of each run, Pallas kernels for 17% -> 18%
where the time goes in v4:
time: 186 us
  waiting for transfers between devices  87 us (47%)
  starting transfers between devices  40.9 us (22%)
  Pallas kernels  37.2 us (20%)
  other arithmetic  12.3 us (7%)
  local copies, waits for them, and re-layouts  6.71 us (4%)
    ppermute x18, waiting for transfers between devices, swap_step(): return lax.ppermute(value, ('dp', 'fsdp'), pairs)  43.8 us
    ppermute x10, waiting for transfers between devices, swap(): lax.ppermute(value, 'fsdp', [(i, i ^ 1 << bit) for i in range(self.size)])  39.8 us
    pallas_call x8, Pallas kernels, call(): pl.pallas_call(whole, name=name, out_shape=tuple(outs), in_specs=[pl.Bloc...  37.2 us
    ppermute x18, starting transfers between devices, swap_step(): return lax.ppermute(value, ('dp', 'fsdp'), pairs)  20.7 us
    ppermute x10, starting transfers between devices, swap(): lax.ppermute(value, 'fsdp', [(i, i ^ 1 << bit) for i in range(self.size)])  14.1 us
    unnamed x107, local copies, waits for them, and re-layouts  6.66 us
    convert_element_type x9, other arithmetic, join(): return (keep.astype(wide) + got.astype(wide)).astype(half_type)  5.72 us
    ppermute x2, starting transfers between devices, swap_owned(): return lax.ppermute(value, ('dp', 'fsdp'), pairs)  4.8 us
  transfers between devices with their start and end apart: 38, of which 23 were waited for; matrix products, arithmetic and copies ran while one was open for 5% of the time, Pallas kernels for 18%

profile of v4, /device:TPU:0, one launch (start us, length us, event | category | flops | bytes accessed | tf_op | source)
XLA Modules:
  0.0 185.5 jit_solution(16325331045312415837)
XLA Ops:
  1.3 2.9 %pack_blocks.1 = (bf16[48,1664]{1,0:T(8,128)(2,1)}, bf16[48,1536]{1,0:T(8,128)(2,1)}, bf16[272,768]{1,0:T(8,128)(2,1)}) custom-call(s32[2]{0:T(128)} %pad_add_fusion.refs_0_, s32[2]{0:T(128)} %bitcast.91, bf16[128,768]{1,0:T(8,128)(2,1)} %bitcast.83, bf16[128,768]{1,0:T(8,128)(2,1)} %bitcast.79, bf16[48,2304]{1,0:T(8,128)(2,1)} %bitcast.100, ...), custom_call_target="tpu_custom_call" | custom-call | flops 1724999936 | bytes 1 | tf_op jit(solution)/shard_map/pack_blocks/pallas_call | solution.py:231
  4.2 4.1 %collective-permute-start.1 = (bf16[1,48,1664]{2,1,0:T(8,128)(2,1)}, bf16[1,48,1664]{2,1,0:T(8,128)(2,1)S(1)}, u32[]{:S(2)}, u32[]{:S(2)}) collective-permute-start(bf16[1,48,1664]{2,1,0:T(8,128)(2,1)} %bitcast.94), channel_id=1, source_target_pairs={{0,8},{1,9},{2,10},{3,11},{4,12},{5,13},{6,14},{7,15},{8,0},{9,1},... | collective-permute-start | bytes 479240 | tf_op jit(solution)/shard_map/ppermute | solution.py:71
  8.3 7.7 %collective-permute-done.1 = bf16[1,48,1664]{2,1,0:T(8,128)(2,1)S(1)} collective-permute-done((bf16[1,48,1664]{2,1,0:T(8,128)(2,1)}, bf16[1,48,1664]{2,1,0:T(8,128)(2,1)S(1)}, u32[]{:S(2)}, u32[]{:S(2)}) %collective-permute-start.1) | collective-permute-done | bytes 159776 | tf_op jit(solution)/shard_map/ppermute | solution.py:71
  17.0 1.6 collective-permute-start.2
  18.6 1.5 collective-permute-start.3
  20.9 3.3 %collective-permute-start.9 = (bf16[1,48,1536]{2,1,0:T(8,128)(2,1)}, bf16[1,48,1536]{2,1,0:T(8,128)(2,1)S(1)}, u32[]{:S(2)}, u32[]{:S(2)}) collective-permute-start(bf16[1,48,1536]{2,1,0:T(8,128)(2,1)} %bitcast.96), channel_id=1, source_target_pairs={{0,8},{1,9},{2,10},{3,11},{4,12},{5,13},{6,14},{7,15},{8,0},{9,1},... | collective-permute-start | bytes 442376 | tf_op jit(solution)/shard_map/ppermute | solution.py:71
  25.1 5.4 %collective-permute-done.9 = bf16[1,48,1536]{2,1,0:T(8,128)(2,1)S(1)} collective-permute-done((bf16[1,48,1536]{2,1,0:T(8,128)(2,1)}, bf16[1,48,1536]{2,1,0:T(8,128)(2,1)S(1)}, u32[]{:S(2)}, u32[]{:S(2)}) %collective-permute-start.9) | collective-permute-done | bytes 147488 | tf_op jit(solution)/shard_map/ppermute | solution.py:71
  31.2 3.4 %collective-permute-start.10 = (bf16[2,48,1536]{2,1,0:T(8,128)(2,1)S(1)}, bf16[2,48,1536]{2,1,0:T(8,128)(2,1)S(1)}, u32[]{:S(2)}, u32[]{:S(2)}) collective-permute-start(bf16[2,48,1536]{2,1,0:T(8,128)(2,1)S(1)} %constant_dynamic-update-slice_fusion), channel_id=1, source_target_pairs={{0,4},{1,5},{2,6},{3,7},{4,0},{5,1},{6,2},{7,3},{8,12},{9,13},{10,... | collective-permute-start | bytes 884744 | tf_op jit(solution)/shard_map/ppermute | solution.py:71
  35.7 1.5 collective-permute-start.4
  37.2 3.5 %collective-permute-start.14 = (bf16[1,192,768]{2,1,0:T(8,128)(2,1)S(1)}, bf16[1,192,768]{2,1,0:T(8,128)(2,1)S(1)}, u32[]{:S(2)}, u32[]{:S(2)}) collective-permute-start(bf16[1,192,768]{2,1,0:T(8,128)(2,1)S(1)} %copy-done.37), channel_id=1, source_target_pairs={{0,8},{1,9},{2,10},{3,11},{4,12},{5,13},{6,14},{7,15},{24,16},{25,... | collective-permute-start | bytes 884744 | tf_op jit(solution)/shard_map/ppermute | solution.py:90
  41.1 1.8 collective-permute-done.7.refs_10_.refs_21_
  42.9 2.7 %collective-permute-done.6.refs_9_.refs_20_ = bf16[2,48,1664]{2,1,0:T(8,128)(2,1)S(1)} collective-permute-done((bf16[2,48,1664]{2,1,0:T(8,128)(2,1)S(1)}, bf16[2,48,1664]{2,1,0:T(8,128)(2,1)S(1)}, u32[]{:S(2)}, u32[]{:S(2)}) %collective-permute-start.6) | collective-permute-done | bytes 319520 | tf_op jit(solution)/shard_map/ppermute | solution.py:79
  46.3 1.5 collective-permute-start.11
  48.8 1.5 collective-permute-start.19
  50.3 5.0 %collective-permute-done.15 = bf16[1,192,768]{2,1,0:T(8,128)(2,1)S(1)} collective-permute-done((bf16[1,192,768]{2,1,0:T(8,128)(2,1)S(1)}, bf16[1,192,768]{2,1,0:T(8,128)(2,1)S(1)}, u32[]{:S(2)}, u32[]{:S(2)}) %collective-permute-start.15) | collective-permute-done | bytes 294944 | tf_op jit(solution)/shard_map/ppermute | solution.py:71
  55.4 5.5 %collective-permute-done.11.refs_10_ = bf16[4,48,1536]{2,1,0:T(8,128)(2,1)S(1)} collective-permute-done((bf16[4,48,1536]{2,1,0:T(8,128)(2,1)S(1)}, bf16[4,48,1536]{2,1,0:T(8,128)(2,1)S(1)}, u32[]{:S(2)}, u32[]{:S(2)}) %collective-permute-start.11) | collective-permute-done | bytes 589856 | tf_op jit(solution)/shard_map/ppermute | solution.py:79
  61.0 1.5 collective-permute-start.16
  63.1 1.5 collective-permute-start.12
  64.6 4.3 %attend.1 = (bf16[256,768]{1,0:T(8,128)(2,1)S(1)}, bf16[256,1152]{1,0:T(8,128)(2,1)S(1)}, f32[6,256,128]{2,1,0:T(8,128)S(1)}, bf16[256,384]{1,0:T(8,128)(2,1)S(1...) custom-call(s32[2]{0:T(128)S(1)} %copy-done.18, s32[2]{0:T(128)S(1)} %bitcast.92, bf16[128,768]{1,0:T(8,128)(2,1)S(1)} %bitcast.84, ...), custom_call_target="tpu_custom_call" | custom-call | flops 4944999936 | bytes 1 | tf_op jit(solution)/shard_map/attend/pallas_call | solution.py:231
  69.0 14.8 %collective-permute-done.12.refs_12_ = bf16[4,48,1536]{2,1,0:T(8,128)(2,1)S(1)} collective-permute-done((bf16[4,48,1536]{2,1,0:T(8,128)(2,1)S(1)}, bf16[4,48,1536]{2,1,0:T(8,128)(2,1)S(1)}, u32[]{:S(2)}, u32[]{:S(2)}) %collective-permute-start.12) | collective-permute-done | bytes 589856 | tf_op jit(solution)/shard_map/ppermute | solution.py:79
  85.8 7.5 %grow.1 = (f32[256,768]{1,0:T(8,128)S(1)}, bf16[256,768]{1,0:T(8,128)(2,1)S(1)}, bf16[256,1536]{1,0:T(8,128)(2,1)S(1)}, f32[256,1536]{1,0:T(8,128)S(1)}, bf16[25...) custom-call(s32[2]{0:T(128)S(1)} %copy-done.18, ...), custom_call_target="tpu_custom_call" | custom-call | flops 10924999680 | bytes 1 | tf_op jit(solution)/shard_map/grow/pallas_call | solution.py:231
  93.3 1.6 collective-permute-start.33
  94.9 5.4 %shrink_back.1 = (bf16[256,1536]{1,0:T(8,128)(2,1)S(1)}, f32[256,768]{1,0:T(8,128)S(1)}, f32[128,768]{1,0:T(8,128)S(1)}, f32[128,768]{1,0:T(8,128)S(1)}) custom-call(s32[2]{0:T(128)S(1)} %copy-done.18, bf16[128,768]{1,0:T(8,128)(2,1)S(1)} %bitcast.81, bf16[272,768]{1,0:T(8,128)(2,1)S(1)} %collective-permute-done.refs_3_.refs_4_.refs_2_.refs_5_, ...), custom_call_target="tpu_custom_call" | custom-call | flops 7360000000 | bytes 1 | tf_op jit(solution)/shard_map/shrink_back/pallas_call | solution.py:231
  100.4 2.2 %expand_grads.1 = (f32[1,1536]{1,0:T(1,128)S(1)}, bf16[8,48,1536]{2,1,0:T(8,128)(2,1)S(1)}, bf16[4,48,1536]{2,1,0:T(8,128)(2,1)S(1)}, bf16[4,48,1536]{2,1,0:T(8,128)(2,1)S(1)}) custom-call(s32[2]{0:T(128)S(1)} %copy-done.18, bf16[256,768]{1,0:T(8,128)(2,1)S(1)} %get-tuple-element.111.refs_1_, bf16[256,1536]{1,0:T(8,128)(2,1)S(1)} %get-tuple-element.112.refs_2_), custom_call_target="tpu_custom_call" | custom-call | flops 4944999936 | bytes 1 | tf_op jit(solution)/shard_map/expand_grads/pallas_call | solution.py:231
  102.6 1.3 collective-permute-start.29
  103.9 5.7 %collective-permute-done.33 = bf16[4,192,768]{2,1,0:T(8,128)(2,1)S(1)} collective-permute-done((bf16[4,192,768]{2,1,0:T(8,128)(2,1)S(1)}, bf16[4,192,768]{2,1,0:T(8,128)(2,1)S(1)}, u32[]{:S(2)}, u32[]{:S(2)}) %collective-permute-start.33) | collective-permute-done | bytes 1179680 | tf_op jit(solution)/shard_map/ppermute | solution.py:79
  109.9 1.0 collective-permute-start.34
  111.3 10.3 %attend_back.1 = (f32[128,768]{1,0:T(8,128)S(1)}, f32[128,768]{1,0:T(8,128)S(1)}, f32[128,768]{1,0:T(8,128)}, bf16[8,48,1664]{2,1,0:T(8,128)(2,1)S(1)}, bf16[4,4...) custom-call(s32[2]{0:T(128)S(1)} %copy-done.18, f32[16,768]{1,0:T(8,128)S(1)} %get-tuple-element.89.refs_1_, ...), custom_call_target="tpu_custom_call" | custom-call | flops 10350000128 | bytes 1 | tf_op jit(solution)/shard_map/attend_back/pallas_call | solution.py:231
  121.6 1.6 collective-permute-start.24
  123.1 5.4 %collective-permute-done.29 = bf16[8,48,1536]{2,1,0:T(8,128)(2,1)S(1)} collective-permute-done((bf16[8,48,1536]{2,1,0:T(8,128)(2,1)S(1)}, bf16[8,48,1536]{2,1,0:T(8,128)(2,1)S(1)}, u32[]{:S(2)}, u32[]{:S(2)}) %collective-permute-start.29) | collective-permute-done | bytes 1179680 | tf_op jit(solution)/shard_map/ppermute | solution.py:79
  128.6 1.3 add_convert_fusion.5
  132.2 1.1 copy-done.20
  136.3 3.1 %finish.1 = (f32[128,768]{1,0:T(8,128)}, f32[128,768]{1,0:T(8,128)}) custom-call(s32[2]{0:T(128)S(1)} %copy-done.18, f32[16,768]{1,0:T(8,128)S(1)} %get-tuple-element.89.refs_1_, bf16[128,768]{1,0:T(8,128)(2,1)S(1)} %bitcast.87, f32[256,768]{1,0:T(8,128)S(1)} %copy-done.20, f32[128,768]{1,0:T(8,128)S(1)} %copy-done.22, ...), custom_call_target="tpu_custom_call" | custom-call | flops 2990000128 | bytes 1 | tf_op jit(solution)/shard_map/finish/pallas_call | solution.py:231
  139.4 1.2 collective-permute-done.35
  140.8 1.3 collective-permute-start.36
  142.1 4.4 %collective-permute-done.30 = bf16[4,48,1536]{2,1,0:T(8,128)(2,1)} collective-permute-done((bf16[4,48,1536]{2,1,0:T(8,128)(2,1)}, bf16[4,48,1536]{2,1,0:T(8,128)(2,1)}, u32[]{:S(2)}, u32[]{:S(2)}) %collective-permute-start.30) | collective-permute-done | bytes 589856 | tf_op jit(solution)/shard_map/ppermute | solution.py:79
  146.5 1.2 add_convert_fusion.11
  148.7 1.6 add_convert_fusion.1
  151.3 2.2 %collective-permute-done.36 = bf16[1,192,768]{2,1,0:T(8,128)(2,1)S(1)} collective-permute-done((bf16[1,192,768]{2,1,0:T(8,128)(2,1)S(1)}, bf16[1,192,768]{2,1,0:T(8,128)(2,1)S(1)}, u32[]{:S(2)}, u32[]{:S(2)}) %collective-permute-start.36) | collective-permute-done | bytes 294944 | tf_op jit(solution)/shard_map/ppermute | solution.py:90
  153.8 4.5 %collective-permute-done.31 = bf16[2,48,1536]{2,1,0:T(8,128)(2,1)S(1)} collective-permute-done((bf16[2,48,1536]{2,1,0:T(8,128)(2,1)S(1)}, bf16[2,48,1536]{2,1,0:T(8,128)(2,1)S(1)}, u32[]{:S(2)}, u32[]{:S(2)}) %collective-permute-start.31) | collective-permute-done | bytes 294944 | tf_op jit(solution)/shard_map/ppermute | solution.py:71
  158.5 2.3 %collective-permute-done.25 = bf16[4,48,1664]{2,1,0:T(8,128)(2,1)S(1)} collective-permute-done((bf16[4,48,1664]{2,1,0:T(8,128)(2,1)S(1)}, bf16[4,48,1664]{2,1,0:T(8,128)(2,1)S(1)}, u32[]{:S(2)}, u32[]{:S(2)}) %collective-permute-start.25) | collective-permute-done | bytes 639008 | tf_op jit(solution)/shard_map/ppermute | solution.py:79
  161.0 1.2 collective-permute-start.26
  162.2 3.9 %collective-permute-done.32 = bf16[1,48,1536]{2,1,0:T(8,128)(2,1)S(1)} collective-permute-done((bf16[1,48,1536]{2,1,0:T(8,128)(2,1)S(1)}, bf16[1,48,1536]{2,1,0:T(8,128)(2,1)S(1)}, u32[]{:S(2)}, u32[]{:S(2)}) %collective-permute-start.32) | collective-permute-done | bytes 147488 | tf_op jit(solution)/shard_map/ppermute | solution.py:71
  166.1 1.2 fusion.15
  167.3 4.3 %collective-permute-done.26 = bf16[2,48,1664]{2,1,0:T(8,128)(2,1)S(1)} collective-permute-done((bf16[2,48,1664]{2,1,0:T(8,128)(2,1)S(1)}, bf16[2,48,1664]{2,1,0:T(8,128)(2,1)S(1)}, u32[]{:S(2)}, u32[]{:S(2)}) %collective-permute-start.26) | collective-permute-done | bytes 319520 | tf_op jit(solution)/shard_map/ppermute | solution.py:71
  171.7 1.1 fusion.12
  172.9 6.7 %collective-permute-done.27 = bf16[1,48,1664]{2,1,0:T(8,128)(2,1)S(1)} collective-permute-done((bf16[1,48,1664]{2,1,0:T(8,128)(2,1)S(1)}, bf16[1,48,1664]{2,1,0:T(8,128)(2,1)S(1)}, u32[]{:S(2)}, u32[]{:S(2)}) %collective-permute-start.27) | collective-permute-done | bytes 159776 | tf_op jit(solution)/shard_map/ppermute | solution.py:71
  181.8 1.6 update_small.1
  (170 shorter events, 22.6 us)
Async XLA Ops:
  4.2 33.0 %copy-start.37 = (bf16[1,192,768]{2,1,0:T(8,128)(2,1)S(1)}, bf16[1,192,768]{2,1,0:T(8,128)(2,1)}, u32[]{:S(2)}) copy-start(bf16[1,192,768]{2,1,0:T(8,128)(2,1)} %param.33) | copy-start | bytes 884740
  4.2 11.8 %collective-permute-start.1 = (bf16[1,48,1664]{2,1,0:T(8,128)(2,1)}, bf16[1,48,1664]{2,1,0:T(8,128)(2,1)S(1)}, u32[]{:S(2)}, u32[]{:S(2)}) collective-permute-start(bf16[1,48,1664]{2,1,0:T(8,128)(2,1)} %bitcast.94), channel_id=1, source_target_pairs={{0,8},{1,9},{2,10},{3,11},{4,12},{5,13},{6,14},{7,15},{8,0},{9,1},... | collective-permute-start | bytes 479240 | tf_op jit(solution)/shard_map/ppermute | solution.py:71
  17.0 13.6 %collective-permute-start.2 = (bf16[2,48,1664]{2,1,0:T(8,128)(2,1)S(1)}, bf16[2,48,1664]{2,1,0:T(8,128)(2,1)S(1)}, u32[]{:S(2)}, u32[]{:S(2)}) collective-permute-start(bf16[2,48,1664]{2,1,0:T(8,128)(2,1)S(1)} %pad_maximum_fusion.2.refs_4_.refs_15_), channel_id=1, source_target_pairs={{0,1},{1,0},{2,3},{3,2},{4,5},{5,4},{6,7},{7,6},{8,9},{9,8},{10,11... | collective-permute-start | bytes 958472 | tf_op jit(solution)/shard_map/ppermute | solution.py:79
  18.6 12.0 %collective-permute-start.3 = (bf16[2,48,1664]{2,1,0:T(8,128)(2,1)S(1)}, bf16[2,48,1664]{2,1,0:T(8,128)(2,1)S(1)}, u32[]{:S(2)}, u32[]{:S(2)}) collective-permute-start(bf16[2,48,1664]{2,1,0:T(8,128)(2,1)S(1)} %pad_maximum_fusion.2.refs_4_.refs_15_), channel_id=1, source_target_pairs={{0,2},{1,3},{2,0},{3,1},{4,6},{5,7},{6,4},{7,5},{8,10},{9,11},{10,... | collective-permute-start | bytes 958472 | tf_op jit(solution)/shard_map/ppermute | solution.py:79
  20.1 11.1 %collective-permute-start.5 = (bf16[2,48,1664]{2,1,0:T(8,128)(2,1)S(1)}, bf16[2,48,1664]{2,1,0:T(8,128)(2,1)S(1)}, u32[]{:S(2)}, u32[]{:S(2)}) collective-permute-start(bf16[2,48,1664]{2,1,0:T(8,128)(2,1)S(1)} %pad_maximum_fusion.2.refs_4_.refs_15_), channel_id=1, source_target_pairs={{0,4},{1,5},{2,6},{3,7},{4,0},{5,1},{6,2},{7,3},{8,12},{9,13},{10,... | collective-permute-start | bytes 958472 | tf_op jit(solution)/shard_map/ppermute | solution.py:71
  20.9 9.7 %collective-permute-start.9 = (bf16[1,48,1536]{2,1,0:T(8,128)(2,1)}, bf16[1,48,1536]{2,1,0:T(8,128)(2,1)S(1)}, u32[]{:S(2)}, u32[]{:S(2)}) collective-permute-start(bf16[1,48,1536]{2,1,0:T(8,128)(2,1)} %bitcast.96), channel_id=1, source_target_pairs={{0,8},{1,9},{2,10},{3,11},{4,12},{5,13},{6,14},{7,15},{8,0},{9,1},... | collective-permute-start | bytes 442376 | tf_op jit(solution)/shard_map/ppermute | solution.py:71
  30.6 33.9 %copy-start = (bf16[2,48,1664]{2,1,0:T(8,128)(2,1)}, bf16[2,48,1664]{2,1,0:T(8,128)(2,1)S(1)}, u32[]{:S(2)}) copy-start(bf16[2,48,1664]{2,1,0:T(8,128)(2,1)S(1)} %collective-permute-done.2.refs_5_.refs_16_) | copy-start | bytes 958468
  30.6 33.9 %copy-start.2 = (bf16[2,48,1664]{2,1,0:T(8,128)(2,1)}, bf16[2,48,1664]{2,1,0:T(8,128)(2,1)S(1)}, u32[]{:S(2)}) copy-start(bf16[2,48,1664]{2,1,0:T(8,128)(2,1)S(1)} %collective-permute-done.3.refs_6_.refs_17_) | copy-start | bytes 958468
  31.2 33.3 %copy-start.4 = (bf16[2,48,1664]{2,1,0:T(8,128)(2,1)}, bf16[2,48,1664]{2,1,0:T(8,128)(2,1)S(1)}, u32[]{:S(2)}) copy-start(bf16[2,48,1664]{2,1,0:T(8,128)(2,1)S(1)} %collective-permute-done.5.refs_8_.refs_19_) | copy-start | bytes 958468
  31.2 9.8 %collective-permute-start.10 = (bf16[2,48,1536]{2,1,0:T(8,128)(2,1)S(1)}, bf16[2,48,1536]{2,1,0:T(8,128)(2,1)S(1)}, u32[]{:S(2)}, u32[]{:S(2)}) collective-permute-start(bf16[2,48,1536]{2,1,0:T(8,128)(2,1)S(1)} %constant_dynamic-update-slice_fusion), channel_id=1, source_target_pairs={{0,4},{1,5},{2,6},{3,7},{4,0},{5,1},{6,2},{7,3},{8,12},{9,13},{10,... | collective-permute-start | bytes 884744 | tf_op jit(solution)/shard_map/ppermute | solution.py:71
  34.6 8.3 %collective-permute-start.7 = (bf16[2,48,1664]{2,1,0:T(8,128)(2,1)S(1)}, bf16[2,48,1664]{2,1,0:T(8,128)(2,1)S(1)}, u32[]{:S(2)}, u32[]{:S(2)}) collective-permute-start(bf16[2,48,1664]{2,1,0:T(8,128)(2,1)S(1)} %collective-permute-done.5.refs_8_.refs_19_), channel_id=1, source_target_pairs={{0,2},{1,3},{2,0},{3,1},{4,6},{5,7},{6,4},{7,5},{8,10},{9,11},{10,... | collective-permute-start | bytes 958472 | tf_op jit(solution)/shard_map/ppermute | solution.py:79
  35.1 10.5 %collective-permute-start.6 = (bf16[2,48,1664]{2,1,0:T(8,128)(2,1)S(1)}, bf16[2,48,1664]{2,1,0:T(8,128)(2,1)S(1)}, u32[]{:S(2)}, u32[]{:S(2)}) collective-permute-start(bf16[2,48,1664]{2,1,0:T(8,128)(2,1)S(1)} %collective-permute-done.5.refs_8_.refs_19_), channel_id=1, source_target_pairs={{0,1},{1,0},{2,3},{3,2},{4,5},{5,4},{6,7},{7,6},{8,9},{9,8},{10,11... | collective-permute-start | bytes 958472 | tf_op jit(solution)/shard_map/ppermute | solution.py:79
  35.7 10.6 %collective-permute-start.4 = (bf16[2,48,1664]{2,1,0:T(8,128)(2,1)S(1)}, bf16[2,48,1664]{2,1,0:T(8,128)(2,1)S(1)}, u32[]{:S(2)}, u32[]{:S(2)}) collective-permute-start(bf16[2,48,1664]{2,1,0:T(8,128)(2,1)S(1)} %collective-permute-done.2.refs_5_.refs_16_), channel_id=1, source_target_pairs={{0,2},{1,3},{2,0},{3,1},{4,6},{5,7},{6,4},{7,5},{8,10},{9,11},{10,... | collective-permute-start | bytes 958472 | tf_op jit(solution)/shard_map/ppermute | solution.py:79
  37.2 10.6 %collective-permute-start.14 = (bf16[1,192,768]{2,1,0:T(8,128)(2,1)S(1)}, bf16[1,192,768]{2,1,0:T(8,128)(2,1)S(1)}, u32[]{:S(2)}, u32[]{:S(2)}) collective-permute-start(bf16[1,192,768]{2,1,0:T(8,128)(2,1)S(1)} %copy-done.37), channel_id=1, source_target_pairs={{0,8},{1,9},{2,10},{3,11},{4,12},{5,13},{6,14},{7,15},{24,16},{25,... | collective-permute-start | bytes 884744 | tf_op jit(solution)/shard_map/ppermute | solution.py:90
  41.1 23.5 %copy-start.13 = (bf16[1,128,768]{2,1,0:T(8,128)(2,1)S(1)}, bf16[1,128,768]{2,1,0:T(8,128)(2,1)}, u32[]{:S(2)}) copy-start(bf16[1,128,768]{2,1,0:T(8,128)(2,1)} %param.27) | copy-start | bytes 589828
  41.1 23.5 %copy-start.17 = (s32[1,2]{1,0:T(1,128)S(1)}, s32[1,2]{1,0:T(1,128)}, u32[]{:S(2)}) copy-start(s32[1,2]{1,0:T(1,128)} %param.29) | copy-start | bytes 28
  41.1 23.5 %copy-start.18 = (s32[2]{0:T(128)S(1)}, s32[2]{0:T(128)}, u32[]{:S(2)}) copy-start(s32[2]{0:T(128)} %pad_add_fusion.refs_0_) | copy-start | bytes 28
  42.9 26.0 %copy-start.6 = (bf16[2,48,1664]{2,1,0:T(8,128)(2,1)}, bf16[2,48,1664]{2,1,0:T(8,128)(2,1)S(1)}, u32[]{:S(2)}) copy-start(bf16[2,48,1664]{2,1,0:T(8,128)(2,1)S(1)} %collective-permute-done.7.refs_10_.refs_21_) | copy-start | bytes 958468
  45.6 23.3 %copy-start.8 = (bf16[2,48,1664]{2,1,0:T(8,128)(2,1)}, bf16[2,48,1664]{2,1,0:T(8,128)(2,1)S(1)}, u32[]{:S(2)}) copy-start(bf16[2,48,1664]{2,1,0:T(8,128)(2,1)S(1)} %collective-permute-done.6.refs_9_.refs_20_) | copy-start | bytes 958468
  46.3 14.6 %collective-permute-start.11 = (bf16[4,48,1536]{2,1,0:T(8,128)(2,1)S(1)}, bf16[4,48,1536]{2,1,0:T(8,128)(2,1)S(1)}, u32[]{:S(2)}, u32[]{:S(2)}) collective-permute-start(bf16[4,48,1536]{2,1,0:T(8,128)(2,1)S(1)} %pad_maximum_fusion.refs_9_), channel_id=1, source_target_pairs={{0,1},{1,0},{2,3},{3,2},{4,5},{5,4},{6,7},{7,6},{8,9},{9,8},{10,11... | collective-permute-start | bytes 1769480 | tf_op jit(solution)/shard_map/ppermute | solution.py:79
  47.9 7.5 %collective-permute-start.15 = (bf16[1,192,768]{2,1,0:T(8,128)(2,1)S(1)}, bf16[1,192,768]{2,1,0:T(8,128)(2,1)S(1)}, u32[]{:S(2)}, u32[]{:S(2)}) collective-permute-start(bf16[1,192,768]{2,1,0:T(8,128)(2,1)S(1)} %broadcast_select_fusion), channel_id=1, source_target_pairs={{0,4},{1,5},{2,6},{3,7},{4,0},{5,1},{6,2},{7,3},{8,12},{9,13},{10,... | collective-permute-start | bytes 884744 | tf_op jit(solution)/shard_map/ppermute | solution.py:71
  48.3 14.8 %collective-permute-start = (bf16[272,768]{1,0:T(8,128)(2,1)S(1)}, bf16[272,768]{1,0:T(8,128)(2,1)S(1)}, u32[]{:S(2)}, u32[]{:S(2)}) collective-permute-start(bf16[272,768]{1,0:T(8,128)(2,1)S(1)} %copy-done.50), channel_id=1, source_target_pairs={{0,16},{16,0},{1,17},{17,1},{2,18},{18,2},{3,19},{19,3},{4,20},{20... | collective-permute-start | bytes 1253384 | tf_op jit(solution)/shard_map/ppermute | solution.py:82
  48.3 16.2 %collective-permute-start.8 = (bf16[2,48,1664]{2,1,0:T(8,128)(2,1)S(1)}, bf16[2,48,1664]{2,1,0:T(8,128)(2,1)S(1)}, u32[]{:S(2)}, u32[]{:S(2)}) collective-permute-start(bf16[2,48,1664]{2,1,0:T(8,128)(2,1)S(1)} %collective-permute-done.6.refs_9_.refs_20_), channel_id=1, source_target_pairs={{0,2},{1,3},{2,0},{3,1},{4,6},{5,7},{6,4},{7,5},{8,10},{9,11},{10,... | collective-permute-start | bytes 958472 | tf_op jit(solution)/shard_map/ppermute | solution.py:79
  48.8 37.0 %collective-permute-start.19 = (bf16[4,48,1536]{2,1,0:T(8,128)(2,1)S(1)}, bf16[4,48,1536]{2,1,0:T(8,128)(2,1)S(1)}, u32[]{:S(2)}, u32[]{:S(2)}) collective-permute-start(bf16[4,48,1536]{2,1,0:T(8,128)(2,1)S(1)} %pad_maximum_fusion.refs_9_), channel_id=1, source_target_pairs={{0,2},{1,3},{2,0},{3,1},{4,6},{5,7},{6,4},{7,5},{8,10},{9,11},{10,... | collective-permute-start | bytes 1769480 | tf_op jit(solution)/shard_map/ppermute | solution.py:79
  55.4 30.4 %copy-start.12 = (bf16[1,128,768]{2,1,0:T(8,128)(2,1)S(1)}, bf16[1,128,768]{2,1,0:T(8,128)(2,1)}, u32[]{:S(2)}) copy-start(bf16[1,128,768]{2,1,0:T(8,128)(2,1)} %param.28) | copy-start | bytes 589828
  61.0 23.8 %collective-permute-start.16 = (bf16[2,192,768]{2,1,0:T(8,128)(2,1)S(1)}, bf16[2,192,768]{2,1,0:T(8,128)(2,1)S(1)}, u32[]{:S(2)}, u32[]{:S(2)}) collective-permute-start(bf16[2,192,768]{2,1,0:T(8,128)(2,1)S(1)} %pad_maximum_fusion.1.refs_5_), channel_id=1, source_target_pairs={{0,1},{1,0},{2,3},{3,2},{4,5},{5,4},{6,7},{7,6},{8,9},{9,8},{10,11... | collective-permute-start | bytes 1769480 | tf_op jit(solution)/shard_map/ppermute | solution.py:79
  62.5 22.7 %collective-permute-start.17 = (bf16[2,192,768]{2,1,0:T(8,128)(2,1)S(1)}, bf16[2,192,768]{2,1,0:T(8,128)(2,1)S(1)}, u32[]{:S(2)}, u32[]{:S(2)}) collective-permute-start(bf16[2,192,768]{2,1,0:T(8,128)(2,1)S(1)} %pad_maximum_fusion.1.refs_5_), channel_id=1, source_target_pairs={{0,2},{1,3},{2,0},{3,1},{4,6},{5,7},{6,4},{7,5},{8,10},{9,11},{10,... | collective-permute-start | bytes 1769480 | tf_op jit(solution)/shard_map/ppermute | solution.py:79
  63.1 20.7 %collective-permute-start.12 = (bf16[4,48,1536]{2,1,0:T(8,128)(2,1)S(1)}, bf16[4,48,1536]{2,1,0:T(8,128)(2,1)S(1)}, u32[]{:S(2)}, u32[]{:S(2)}) collective-permute-start(bf16[4,48,1536]{2,1,0:T(8,128)(2,1)S(1)} %collective-permute-done.11.refs_10_), channel_id=1, source_target_pairs={{0,2},{1,3},{2,0},{3,1},{4,6},{5,7},{6,4},{7,5},{8,10},{9,11},{10,... | collective-permute-start | bytes 1769480 | tf_op jit(solution)/shard_map/ppermute | solution.py:79
  68.9 16.9 %collective-permute-start.18 = (bf16[768,384]{1,0:T(8,128)(2,1)S(1)}, bf16[768,384]{1,0:T(8,128)(2,1)S(1)}, u32[]{:S(2)}, u32[]{:S(2)}) collective-permute-start(bf16[768,384]{1,0:T(8,128)(2,1)S(1)} %get-tuple-element.100.refs_7_.refs_9_), channel_id=1, source_target_pairs={{0,16},{16,0},{1,17},{17,1},{2,18},{18,2},{3,19},{19,3},{4,20},{20... | collective-permute-start | bytes 1769480 | tf_op jit(solution)/shard_map/ppermute | solution.py:82
  83.8 2.0 %collective-permute-start.13 = (bf16[256,384]{1,0:T(8,128)(2,1)S(1)}, bf16[256,384]{1,0:T(8,128)(2,1)S(1)}, u32[]{:S(2)}, u32[]{:S(2)}) collective-permute-start(bf16[256,384]{1,0:T(8,128)(2,1)S(1)} %get-tuple-element.95.refs_5_), channel_id=1, source_target_pairs={{0,16},{16,0},{1,17},{17,1},{2,18},{18,2},{3,19},{19,3},{4,20},{20... | collective-permute-start | bytes 589832 | tf_op jit(solution)/shard_map/ppermute | solution.py:82
  84.7 10.1 %collective-permute-start.20 = (bf16[2,192,768]{2,1,0:T(8,128)(2,1)S(1)}, bf16[2,192,768]{2,1,0:T(8,128)(2,1)S(1)}, u32[]{:S(2)}, u32[]{:S(2)}) collective-permute-start(bf16[2,192,768]{2,1,0:T(8,128)(2,1)S(1)} %collective-permute-done.16.refs_6_), channel_id=1, source_target_pairs={{0,2},{1,3},{2,0},{3,1},{4,6},{5,7},{6,4},{7,5},{8,10},{9,11},{10,... | collective-permute-start | bytes 1769480 | tf_op jit(solution)/shard_map/ppermute | solution.py:79
  93.3 16.3 %collective-permute-start.33 = (bf16[4,192,768]{2,1,0:T(8,128)(2,1)S(1)}, bf16[4,192,768]{2,1,0:T(8,128)(2,1)S(1)}, u32[]{:S(2)}, u32[]{:S(2)}) collective-permute-start(bf16[4,192,768]{2,1,0:T(8,128)(2,1)S(1)} %get-tuple-element.126), channel_id=1, source_target_pairs={{0,1},{1,0},{2,3},{3,2},{4,5},{5,4},{6,7},{7,6},{8,9},{9,8},{10,11... | collective-permute-start | bytes 3538952 | tf_op jit(solution)/shard_map/ppermute | solution.py:79
  100.3 10.7 %collective-permute-start.22 = (f32[256,768]{1,0:T(8,128)S(1)}, f32[256,768]{1,0:T(8,128)S(1)}, u32[]{:S(2)}, u32[]{:S(2)}) collective-permute-start(f32[256,768]{1,0:T(8,128)S(1)} %get-tuple-element.106.refs_6_), channel_id=1, source_target_pairs={{0,16},{16,0},{1,17},{17,1},{2,18},{18,2},{3,19},{19,3},{4,20},{20... | collective-permute-start | bytes 2359304 | tf_op jit(solution)/shard_map/ppermute | solution.py:82
  102.6 25.9 %collective-permute-start.29 = (bf16[8,48,1536]{2,1,0:T(8,128)(2,1)S(1)}, bf16[8,48,1536]{2,1,0:T(8,128)(2,1)S(1)}, u32[]{:S(2)}, u32[]{:S(2)}) collective-permute-start(bf16[8,48,1536]{2,1,0:T(8,128)(2,1)S(1)} %get-tuple-element.123), channel_id=1, source_target_pairs={{0,1},{1,0},{2,3},{3,2},{4,5},{5,4},{6,7},{7,6},{8,9},{9,8},{10,11... | collective-permute-start | bytes 3538952 | tf_op jit(solution)/shard_map/ppermute | solution.py:79
  103.9 28.3 %collective-permute-start.21 = (f32[128,768]{1,0:T(8,128)S(1)}, f32[128,768]{1,0:T(8,128)}, u32[]{:S(2)}, u32[]{:S(2)}) collective-permute-start(f32[128,768]{1,0:T(8,128)S(1)} %get-tuple-element.105), channel_id=1, source_target_pairs={{0,16},{16,0},{1,17},{17,1},{2,18},{18,2},{3,19},{19,3},{4,20},{20... | collective-permute-start | bytes 1179656 | tf_op jit(solution)/shard_map/ppermute | solution.py:82
  109.9 20.9 %collective-permute-start.34 = (bf16[2,192,768]{2,1,0:T(8,128)(2,1)S(1)}, bf16[2,192,768]{2,1,0:T(8,128)(2,1)S(1)}, u32[]{:S(2)}, u32[]{:S(2)}) collective-permute-start(bf16[2,192,768]{2,1,0:T(8,128)(2,1)S(1)} %get-tuple-element.162), channel_id=1, source_target_pairs={{0,2},{1,3},{2,0},{3,1},{4,6},{5,7},{6,4},{7,5},{8,10},{9,11},{10,... | collective-permute-start | bytes 1769480 | tf_op jit(solution)/shard_map/ppermute | solution.py:79
  121.6 27.1 %collective-permute-start.24 = (bf16[8,48,1664]{2,1,0:T(8,128)(2,1)S(1)}, bf16[8,48,1664]{2,1,0:T(8,128)(2,1)}, u32[]{:S(2)}, u32[]{:S(2)}) collective-permute-start(bf16[8,48,1664]{2,1,0:T(8,128)(2,1)S(1)} %get-tuple-element.120), channel_id=1, source_target_pairs={{0,1},{1,0},{2,3},{3,2},{4,5},{5,4},{6,7},{7,6},{8,9},{9,8},{10,11... | collective-permute-start | bytes 3833864 | tf_op jit(solution)/shard_map/ppermute | solution.py:79
  123.1 9.1 %collective-permute-start.23 = (f32[128,768]{1,0:T(8,128)}, f32[128,768]{1,0:T(8,128)}, u32[]{:S(2)}, u32[]{:S(2)}) collective-permute-start(f32[128,768]{1,0:T(8,128)} %get-tuple-element.116), channel_id=1, source_target_pairs={{0,16},{16,0},{1,17},{17,1},{2,18},{18,2},{3,19},{19,3},{4,20},{20... | collective-permute-start | bytes 1179656 | tf_op jit(solution)/shard_map/ppermute | solution.py:82
  129.9 16.6 %collective-permute-start.30 = (bf16[4,48,1536]{2,1,0:T(8,128)(2,1)}, bf16[4,48,1536]{2,1,0:T(8,128)(2,1)}, u32[]{:S(2)}, u32[]{:S(2)}) collective-permute-start(bf16[4,48,1536]{2,1,0:T(8,128)(2,1)} %get-tuple-element.166), channel_id=1, source_target_pairs={{0,2},{1,3},{2,0},{3,1},{4,6},{5,7},{6,4},{7,5},{8,10},{9,11},{10,... | collective-permute-start | bytes 1769480 | tf_op jit(solution)/shard_map/ppermute | solution.py:79
  131.8 8.9 %collective-permute-start.35 = (bf16[1,192,768]{2,1,0:T(8,128)(2,1)}, bf16[1,192,768]{2,1,0:T(8,128)(2,1)S(1)}, u32[]{:S(2)}, u32[]{:S(2)}) collective-permute-start(bf16[1,192,768]{2,1,0:T(8,128)(2,1)} %add_convert_fusion.8), channel_id=1, source_target_pairs={{0,4},{1,5},{2,6},{3,7},{4,0},{5,1},{6,2},{7,3},{8,12},{9,13},{10,... | collective-permute-start | bytes 884744 | tf_op jit(solution)/shard_map/ppermute | solution.py:71
  140.8 12.8 %collective-permute-start.36 = (bf16[1,192,768]{2,1,0:T(8,128)(2,1)S(1)}, bf16[1,192,768]{2,1,0:T(8,128)(2,1)S(1)}, u32[]{:S(2)}, u32[]{:S(2)}) collective-permute-start(bf16[1,192,768]{2,1,0:T(8,128)(2,1)S(1)} %fusion), channel_id=1, source_target_pairs={{8,0},{9,1},{10,2},{11,3},{12,4},{13,5},{14,6},{15,7},{16,24},{17,... | collective-permute-start | bytes 884744 | tf_op jit(solution)/shard_map/ppermute | solution.py:90
  147.7 10.7 %collective-permute-start.31 = (bf16[2,48,1536]{2,1,0:T(8,128)(2,1)S(1)}, bf16[2,48,1536]{2,1,0:T(8,128)(2,1)S(1)}, u32[]{:S(2)}, u32[]{:S(2)}) collective-permute-start(bf16[2,48,1536]{2,1,0:T(8,128)(2,1)S(1)} %get-tuple-element.164), channel_id=1, source_target_pairs={{0,4},{1,5},{2,6},{3,7},{4,0},{5,1},{6,2},{7,3},{8,12},{9,13},{10,... | collective-permute-start | bytes 884744 | tf_op jit(solution)/shard_map/ppermute | solution.py:71
  150.3 10.5 %collective-permute-start.25 = (bf16[4,48,1664]{2,1,0:T(8,128)(2,1)S(1)}, bf16[4,48,1664]{2,1,0:T(8,128)(2,1)S(1)}, u32[]{:S(2)}, u32[]{:S(2)}) collective-permute-start(bf16[4,48,1664]{2,1,0:T(8,128)(2,1)S(1)} %get-tuple-element.160), channel_id=1, source_target_pairs={{0,2},{1,3},{2,0},{3,1},{4,6},{5,7},{6,4},{7,5},{8,10},{9,11},{10,... | collective-permute-start | bytes 1916936 | tf_op jit(solution)/shard_map/ppermute | solution.py:79
  153.8 17.9 %collective-permute-start.37 = (f32[192,384]{1,0:T(8,128)S(1)}, f32[192,384]{1,0:T(8,128)S(1)}, u32[]{:S(2)}, u32[]{:S(2)}) collective-permute-start(f32[192,384]{1,0:T(8,128)S(1)} %dynamic-slice_bitcast_fusion), channel_id=1, source_target_pairs={{0,16},{16,0},{1,17},{17,1},{2,18},{18,2},{3,19},{19,3},{4,20},{20... | collective-permute-start | bytes 884744 | tf_op jit(solution)/shard_map/ppermute | solution.py:82
  158.4 7.7 %collective-permute-start.32 = (bf16[1,48,1536]{2,1,0:T(8,128)(2,1)S(1)}, bf16[1,48,1536]{2,1,0:T(8,128)(2,1)S(1)}, u32[]{:S(2)}, u32[]{:S(2)}) collective-permute-start(bf16[1,48,1536]{2,1,0:T(8,128)(2,1)S(1)} %add_convert_fusion.13), channel_id=1, source_target_pairs={{0,8},{1,9},{2,10},{3,11},{4,12},{5,13},{6,14},{7,15},{8,0},{9,1},... | collective-permute-start | bytes 442376 | tf_op jit(solution)/shard_map/ppermute | solution.py:71
  161.0 10.6 %collective-permute-start.26 = (bf16[2,48,1664]{2,1,0:T(8,128)(2,1)S(1)}, bf16[2,48,1664]{2,1,0:T(8,128)(2,1)S(1)}, u32[]{:S(2)}, u32[]{:S(2)}) collective-permute-start(bf16[2,48,1664]{2,1,0:T(8,128)(2,1)S(1)} %get-tuple-element.158), channel_id=1, source_target_pairs={{0,4},{1,5},{2,6},{3,7},{4,0},{5,1},{6,2},{7,3},{8,12},{9,13},{10,... | collective-permute-start | bytes 958472 | tf_op jit(solution)/shard_map/ppermute | solution.py:71
  171.6 8.0 %collective-permute-start.27 = (bf16[1,48,1664]{2,1,0:T(8,128)(2,1)S(1)}, bf16[1,48,1664]{2,1,0:T(8,128)(2,1)S(1)}, u32[]{:S(2)}, u32[]{:S(2)}) collective-permute-start(bf16[1,48,1664]{2,1,0:T(8,128)(2,1)S(1)} %add_convert_fusion.12), channel_id=1, source_target_pairs={{0,8},{1,9},{2,10},{3,11},{4,12},{5,13},{6,14},{7,15},{8,0},{9,1},... | collective-permute-start | bytes 479240 | tf_op jit(solution)/shard_map/ppermute | solution.py:71
  180.4 1.4 collective-permute-start.28
  (41 other events, 253.3 us)
